TPU v7x, 32 devices: a whole 2x2x4 slice. The times are simulated.
32 devices in a mesh: narrow: 4 (over y, x), wide: 8 (over z, core).
Axes of the slice: x: 2, y: 2, z: 4, core: 2. Of those that a mesh axis runs over, the one named last changes fastest.
Arguments:
- byte_ids: int32 [8192], P(('narrow', 'wide')), may hold values from 0 to 255
- doc_patches: int32 [9], replicated, may hold values from 1 to 341, 1024 in all
- pad_bytes: int32 [9], replicated, may hold values from 0 to 7
- byte_table: bfloat16 [256, 128], P(('narrow', 'wide')), may hold values from -6 to 6
- patch_weight: bfloat16 [1024, 1024], P(('narrow', 'wide')), may hold values from -0.1875 to 0.1875
- gain_mix: float32 [1024], replicated, may hold values from 0.5 to 1.5
- in_weight: bfloat16 [1024, 4384], P(('narrow', 'wide')), may hold values from -0.1875 to 0.1875
- conv_weight: float32 [4, 2304], replicated, may hold values from -3 to 3
- conv_bias: float32 [2304], replicated, may hold values from -2 to 2
- step_bias: float32 [32], replicated, may hold values from -6.9 to -2.25
- log_rate: float32 [32], replicated, may hold values from 0 to 2.77
- skip_gain: float32 [32], replicated, may hold values from 0.5 to 1.5
- gated_gain: float32 [2048], replicated, may hold values from 0.5 to 1.5
- out_weight: bfloat16 [2048, 1024], P(('narrow', 'wide')), may hold values from -0.125 to 0.125
- local_weight: bfloat16 [128, 1024], P(None, ('narrow', 'wide')), may hold values from -0.5 to 0.5
- gain_attn: float32 [1024], replicated, may hold values from 0.5 to 1.5
- query_weight: bfloat16 [1024, 1024], P(('narrow', 'wide')), may hold values from -0.1875 to 0.1875
- key_weight: bfloat16 [1024, 1024], P(('narrow', 'wide')), may hold values from -0.1875 to 0.1875
- value_weight: bfloat16 [1024, 1024], P(('narrow', 'wide')), may hold values from -0.1875 to 0.1875
- attn_weight: bfloat16 [1024, 1024], P(('narrow', 'wide')), may hold values from -0.5 to 0.5
- feed_gain: float32 [1024], replicated, may hold values from 0.5 to 1.5
- gate_weight: bfloat16 [1024, 4096], P('narrow', 'wide'), may hold values from -0.1875 to 0.1875
- up_weight: bfloat16 [1024, 4096], P('narrow', 'wide'), may hold values from -0.1875 to 0.1875
- down_weight: bfloat16 [4096, 1024], P('wide', 'narrow'), may hold values from -0.09375 to 0.09375
- cotangent: bfloat16 [8192, 1024], P(('narrow', 'wide')), may hold values from -6 to 6
Outputs:
- out_rows: bfloat16 [8192, 1024], P(('narrow', 'wide'))
- grad_table: float32 [256, 128], P(('narrow', 'wide'))
- grad_patch: float32 [1024, 1024], P(('narrow', 'wide'))
- grad_gain_mix: float32 [1024], replicated
- grad_in: float32 [1024, 4384], P(('narrow', 'wide'))
- grad_conv_weight: float32 [4, 2304], replicated
- grad_conv_bias: float32 [2304], replicated
- grad_step_bias: float32 [32], replicated
- grad_log_rate: float32 [32], replicated
- grad_skip_gain: float32 [32], replicated
- grad_gated_gain: float32 [2048], replicated
- grad_out: float32 [2048, 1024], P(('narrow', 'wide'))
- grad_local: float32 [128, 1024], P(None, ('narrow', 'wide'))
- grad_gain_attn: float32 [1024], replicated
- grad_query: float32 [1024, 1024], P(('narrow', 'wide'))
- grad_key: float32 [1024, 1024], P(('narrow', 'wide'))
- grad_value: float32 [1024, 1024], P(('narrow', 'wide'))
- grad_attn: float32 [1024, 1024], P(('narrow', 'wide'))
- grad_feed_gain: float32 [1024], replicated
- grad_gate: float32 [1024, 4096], P('narrow', 'wide')
- grad_up: float32 [1024, 4096], P('narrow', 'wide')
- grad_down: float32 [4096, 1024], P('wide', 'narrow')
Inputs may be any that keep to these rules, and one draw needn't show every extreme that they name: `doc_patches`: documents lie end to end over all patches; the longest has exactly 341 patches.
All inputs are finite; a program needn't handle non-finite values.
Results may differ from a plain program's by a relative error of at most 0.04.
Values may be sent and summed in bfloat16 or wider, within the bound.
A program may use at most 448 MiB of HBM per device.

v0:
```python
from functools import partial

import jax
import jax.numpy as jnp
from jax import lax
from jax.sharding import PartitionSpec as P

D = 1024
PATCH = 8
EMB = 128
VOCAB = 256
HEADS_M = 32
HEAD_M = 64
DI = 2048
STATE = 128
CONV = 4
HEADS_A = 16
HEAD_A = 64


epsilon = 1e-05
highest = lax.Precision.HIGHEST
masked_score = -1e30


def passed_along(x, axis, by):
    peers = lax.axis_size(axis)
    pairs = [(i, i + by) for i in range(peers) if 0 <= i + by < peers]
    return lax.ppermute(x, axis, pairs)


def prefix_2(x, axis, join, neutral):
    place = lax.axis_index(axis)
    gathered = jax.tree.map(
        lambda a, kind: lax.all_gather(a.astype(kind), axis), x, (jnp.bfloat16, jnp.bfloat16)
    )
    state = jax.tree.map(lambda a, e: jnp.zeros_like(a) + jnp.asarray(e, a.dtype), x, neutral)

    def prefix_one(hop, state):
        return join(
            state,
            jax.tree.map(
                lambda a, own: lax.dynamic_index_in_dim(a, hop, 0, False).astype(own.dtype),
                gathered,
                x,
            ),
        )

    return lax.fori_loop(0, place, prefix_one, state)


def carried_in_2(x, axis, join, neutral):
    count = lax.axis_size(axis)
    place = lax.axis_index(axis)
    ahead = count - 1 - place
    gathered = jax.tree.map(
        lambda a, kind: lax.all_gather(a.astype(kind), axis),
        x,
        jax.tree.map(lambda a: jnp.bfloat16 if a.dtype == jnp.float32 else a.dtype, x),
    )
    state = jax.tree.map(lambda a, e: jnp.zeros_like(a) + jnp.asarray(e, a.dtype), x, neutral)

    def carried_one(hop, state):
        source = count - 1 - hop
        return join(
            state,
            jax.tree.map(
                lambda a, own: lax.dynamic_index_in_dim(a, source, 0, False).astype(own.dtype),
                gathered,
                x,
            ),
        )

    return lax.fori_loop(0, ahead, carried_one, state)


def root_norm(values, gain):
    return values * lax.rsqrt(jnp.mean(values * values, axis=-1, keepdims=True) + epsilon) * gain


def patch_layout(doc_patches, pad_bytes, first_index, patch_count):
    patch_index = first_index + jnp.arange(patch_count, dtype=jnp.int32)
    doc_ends = jnp.cumsum(doc_patches)
    doc_index = jnp.arange(doc_patches.shape[0], dtype=jnp.int32)
    segment = jnp.sum((patch_index[:, None] >= doc_ends[None, :]).astype(jnp.int32), axis=1)
    owner_mask = segment[:, None] == doc_index[None, :]
    last_end = jnp.sum(jnp.where(owner_mask, doc_ends[None, :] - 1, 0), axis=1)
    doc_starts = jnp.sum(jnp.where(owner_mask, (doc_ends - doc_patches)[None, :], 0), axis=1)
    pad_count = jnp.sum(jnp.where(owner_mask, pad_bytes[None, :], 0), axis=1)
    offset = jnp.arange(PATCH, dtype=jnp.int32)
    padded = (patch_index == last_end)[:, None] & (offset[None, :] >= PATCH - pad_count[:, None])
    keep_mask = 1.0 - padded.astype(jnp.float32).reshape(-1)
    return (segment, (patch_index == doc_starts).astype(jnp.int32), keep_mask)


def ssd_terms(layout, projected, rim_rows, small_params):
    conv_weight, conv_bias, step_bias, log_rate, skip_gain = small_params
    segment, rim_segment, first_patch = layout
    conv_in = projected[:, DI : 2 * DI + 2 * STATE]
    patch_count = conv_in.shape[0]
    padded = jnp.concatenate([rim_rows, conv_in], 0)
    padded_seg = jnp.concatenate([rim_segment, segment], 0)
    conv_sum = conv_bias
    for conv_tap in range(CONV):
        same_doc = (padded_seg[conv_tap : conv_tap + patch_count] == segment).astype(jnp.float32)[
            :, None
        ]
        conv_sum = (
            conv_sum + conv_weight[conv_tap] * padded[conv_tap : conv_tap + patch_count] * same_doc
        )
    activated = jax.nn.silu(conv_sum)
    values = activated[:, :DI].reshape(patch_count, HEADS_M, HEAD_M)
    input_map = activated[:, DI : DI + STATE]
    output_map = activated[:, DI + STATE :]
    time_steps = jax.nn.softplus(projected[:, 2 * DI + 2 * STATE :] + step_bias)
    cumulative = jnp.cumsum(-time_steps * jnp.exp(log_rate), axis=0)
    no_reset = (jnp.cumsum(first_patch) == 0).astype(jnp.float32)
    return (values, input_map, output_map, time_steps, cumulative, no_reset)


def local_state(layout, projected, rim_rows, small_params):
    values, input_map, output_map, time_steps, cumulative, no_reset = ssd_terms(
        layout, projected, rim_rows, small_params
    )
    segment = layout[0]
    decay_tail = (
        jnp.exp(cumulative[-1][None, :] - cumulative)
        * (segment == segment[-1]).astype(jnp.float32)[:, None]
        * time_steps
    )
    state_local = jnp.einsum("sh,shp,sn->hpn", decay_tail, values, input_map, precision=highest)
    decay_total = jnp.exp(cumulative[-1]) * no_reset[-1]
    return (decay_total, state_local)


def mixer_output(layout, projected, rim_rows, small_params, incoming, gated_gain):
    values, input_map, output_map, time_steps, cumulative, no_reset = ssd_terms(
        layout, projected, rim_rows, small_params
    )
    segment = layout[0]
    patch_count = values.shape[0]
    position = jnp.arange(patch_count)
    visible = (segment[:, None] == segment[None, :]) & (position[:, None] >= position[None, :])
    log_gap = jnp.where(visible[:, :, None], cumulative[:, None, :] - cumulative[None, :, :], 0.0)
    inner = jnp.dot(output_map, input_map.T, precision=highest)
    weight = (
        jnp.exp(log_gap)
        * visible[:, :, None].astype(jnp.float32)
        * time_steps[None, :, :]
        * inner[:, :, None]
    )
    within = jnp.einsum("tsh,shp->thp", weight, values, precision=highest)
    carried_in = (
        jnp.einsum("tn,hpn->thp", output_map, incoming, precision=highest)
        * (jnp.exp(cumulative) * no_reset[:, None])[:, :, None]
    )
    result = (within + carried_in + small_params[4][None, :, None] * values).reshape(
        patch_count, DI
    )
    gated_rows = result * jax.nn.silu(projected[:, :DI])
    return root_norm(gated_rows, gated_gain)


def combine_states(earlier, following):
    return (earlier[0] * following[0], following[0][:, None, None] * earlier[1] + following[1])


def attend(stream, gain_attn, query_all, key_all, value_all):
    head_shape = (-1, PATCH, HEADS_A, HEAD_A)
    normed_attn = root_norm(stream, gain_attn).astype(jnp.bfloat16)
    queries = jnp.dot(normed_attn, query_all, preferred_element_type=jnp.float32).astype(
        jnp.bfloat16
    )
    key_rows = jnp.dot(normed_attn, key_all, preferred_element_type=jnp.float32).astype(
        jnp.bfloat16
    )
    value_rows = jnp.dot(normed_attn, value_all, preferred_element_type=jnp.float32).astype(
        jnp.bfloat16
    )
    scores = jnp.einsum(
        "pqhe,pkhe->phqk",
        queries.reshape(head_shape),
        key_rows.reshape(head_shape),
        preferred_element_type=jnp.float32,
    ) * HEAD_A ** (-0.5)
    position = jnp.arange(PATCH)
    causal = position[:, None] >= position[None, :]
    attn_probs = jax.nn.softmax(jnp.where(causal, scores, masked_score), axis=-1)
    mixed_heads = jnp.einsum(
        "phqk,pkhe->pqhe",
        attn_probs.astype(jnp.bfloat16),
        value_rows.reshape(head_shape),
        preferred_element_type=jnp.float32,
    )
    mixed_heads = mixed_heads.reshape(stream.shape[0], -1).astype(jnp.bfloat16)
    return (normed_attn, queries, key_rows, value_rows, attn_probs, mixed_heads)


def spread(values):
    by_rows = lax.all_to_all(values, "narrow", split_axis=1, concat_axis=0, tiled=True)
    return lax.all_gather(by_rows, "wide", axis=0, tiled=True)


def collect(term_fn, row_count):
    summed = lax.psum_scatter(
        term_fn(jnp.int32(0), row_count * lax.axis_size("wide")).astype(jnp.bfloat16),
        "wide",
        scatter_dimension=0,
        tiled=True,
    )
    return lax.all_to_all(summed, "narrow", split_axis=0, concat_axis=1, tiled=True)


def narrow_total(partial_rows):
    return lax.psum(partial_rows, "narrow").astype(jnp.float32)


def silu_back(gate_up, hidden_grad, hidden_width):
    gate_rows = gate_up[:, :hidden_width]
    up_rows = gate_up[:, hidden_width:]
    sigmoid = jax.nn.sigmoid(gate_rows)
    gate_grad = hidden_grad * up_rows * sigmoid * (1.0 + gate_rows * (1.0 - sigmoid))
    up_grad = hidden_grad * gate_rows * sigmoid
    return jnp.concatenate([gate_grad, up_grad], axis=1)


def per_device(
    byte_ids,
    doc_patches,
    pad_bytes,
    byte_table,
    patch_weight,
    gain_mix,
    in_weight,
    conv_weight,
    conv_bias,
    step_bias,
    log_rate,
    skip_gain,
    gated_gain,
    out_weight,
    local_weight,
    gain_attn,
    query_weight,
    key_weight,
    value_weight,
    attn_weight,
    feed_gain,
    gate_weight,
    up_weight,
    down_weight,
    cotangent,
):
    byte_rows = byte_ids.shape[0]
    patches = byte_rows // PATCH
    device = lax.axis_index(("narrow", "wide"))
    wide_count = lax.axis_size("wide")
    segment, first_patch, keep_mask = patch_layout(
        doc_patches, pad_bytes, device * patches, patches
    )
    rim_segment = patch_layout(doc_patches, pad_bytes, device * patches - (CONV - 1), CONV - 1)[0]
    layout = (segment, rim_segment, first_patch)
    gathered = (
        lax.all_gather(byte_table, ("narrow", "wide"), axis=0, tiled=True),
        lax.all_gather(patch_weight, ("narrow", "wide"), axis=0, tiled=True),
        lax.all_gather(in_weight, ("narrow", "wide"), axis=0, tiled=True),
        lax.all_gather(out_weight, ("narrow", "wide"), axis=0, tiled=True),
        lax.all_gather(local_weight, ("narrow", "wide"), axis=1, tiled=True),
        lax.all_gather(query_weight, ("narrow", "wide"), axis=0, tiled=True),
        lax.all_gather(key_weight, ("narrow", "wide"), axis=0, tiled=True),
        lax.all_gather(value_weight, ("narrow", "wide"), axis=0, tiled=True),
        lax.all_gather(attn_weight, ("narrow", "wide"), axis=0, tiled=True),
    )
    table_all, patch_all, in_all, out_all, local_all, query_all, key_all, value_all, attn_all = (
        gathered
    )
    onehot = (byte_ids[:, None] == jnp.arange(VOCAB, dtype=jnp.int32)[None, :]).astype(jnp.bfloat16)
    embedded = (
        (jnp.dot(onehot, table_all, preferred_element_type=jnp.float32) * keep_mask[:, None])
        .astype(jnp.bfloat16)
        .reshape(patches, D)
    )
    mixed_in = jnp.dot(embedded, patch_all, preferred_element_type=jnp.float32)
    normed_mix = root_norm(mixed_in, gain_mix).astype(jnp.bfloat16)
    projected = jnp.dot(normed_mix, in_all, preferred_element_type=jnp.float32).astype(jnp.bfloat16)
    rim_rows = passed_along(
        projected[patches - (CONV - 1) :, DI : 2 * DI + 2 * STATE], ("narrow", "wide"), 1
    ).astype(jnp.float32)
    projected_f = projected.astype(jnp.float32)
    small_params = (conv_weight, conv_bias, step_bias, log_rate, skip_gain)
    (decay_total, state_local), state_back = jax.vjp(
        partial(local_state, layout), projected_f, rim_rows, small_params
    )
    prefix = prefix_2(
        (decay_total, state_local),
        ("narrow", "wide"),
        combine_states,
        (jnp.ones_like(decay_total), jnp.zeros_like(state_local)),
    )
    incoming = prefix[1]
    gated_norm, mixer_back = jax.vjp(
        partial(mixer_output, layout), projected_f, rim_rows, small_params, incoming, gated_gain
    )
    gated_low = gated_norm.astype(jnp.bfloat16)
    global_out = mixed_in + jnp.dot(gated_low, out_all, preferred_element_type=jnp.float32)
    local_rows = global_out.astype(jnp.bfloat16).reshape(byte_rows, EMB)
    stream = jnp.dot(local_rows, local_all, preferred_element_type=jnp.float32)
    normed_attn, queries, key_rows, value_rows, attn_probs, mixed_heads = attend(
        stream, gain_attn, query_all, key_all, value_all
    )
    after_attn = stream + jnp.dot(mixed_heads, attn_all, preferred_element_type=jnp.float32)
    normed_feed = root_norm(after_attn, feed_gain).astype(jnp.bfloat16)
    out_grad = cotangent.astype(jnp.float32) * keep_mask[:, None]
    feed_grad = out_grad.astype(jnp.bfloat16)
    grid_in = spread(normed_feed)
    both_weights = jnp.concatenate([gate_weight, up_weight], axis=1)
    hidden_width = gate_weight.shape[1]
    grid_share = grid_in.shape[0] // wide_count
    gate_up_part = jnp.dot(grid_in, both_weights, preferred_element_type=jnp.float32).astype(
        jnp.bfloat16
    )
    gate_up = narrow_total(gate_up_part)
    hidden = (jax.nn.silu(gate_up[:, :hidden_width]) * gate_up[:, hidden_width:]).astype(
        jnp.bfloat16
    )

    def down_term(first_row, row_count):
        return jnp.dot(hidden, down_weight, preferred_element_type=jnp.float32)

    feed_out = collect(down_term, grid_share)
    grid_grad = spread(feed_grad)
    grad_down = jnp.einsum("gf,gd->fd", hidden, grid_grad, preferred_element_type=jnp.float32)
    hidden_part = jnp.einsum(
        "gd,fd->gf", grid_grad, down_weight, preferred_element_type=jnp.float32
    ).astype(jnp.bfloat16)
    hidden_grad = narrow_total(hidden_part)
    gate_up_grad = silu_back(gate_up, hidden_grad, hidden_width).astype(jnp.bfloat16)
    grad_both = jnp.einsum("gd,gf->df", grid_in, gate_up_grad, preferred_element_type=jnp.float32)

    def back_term(first_row, row_count):
        return jnp.einsum(
            "gf,df->gd", gate_up_grad, both_weights, preferred_element_type=jnp.float32
        )

    feed_in_grad = collect(back_term, grid_share)
    grad_gate = grad_both[:, :hidden_width]
    grad_up = grad_both[:, hidden_width:]
    after_feed = after_attn + feed_out.astype(jnp.float32)
    out_rows = (after_feed * keep_mask[:, None]).astype(jnp.bfloat16)
    feed_normed, feed_norm_back = jax.vjp(root_norm, after_attn, feed_gain)
    after_norm_grad, grad_feed_gain = feed_norm_back(feed_in_grad.astype(jnp.float32))
    after_grad = out_grad + after_norm_grad
    head_shape = (-1, PATCH, HEADS_A, HEAD_A)
    score_scale = HEAD_A ** (-0.5)
    attn_grad = after_grad.astype(jnp.bfloat16)
    grad_attn = jnp.einsum("rd,re->de", mixed_heads, attn_grad, preferred_element_type=jnp.float32)
    heads_grad = (
        jnp.einsum("re,de->rd", attn_grad, attn_all, preferred_element_type=jnp.float32)
        .astype(jnp.bfloat16)
        .reshape(head_shape)
    )
    probs_grad = jnp.einsum(
        "pqhe,pkhe->phqk",
        heads_grad,
        value_rows.reshape(head_shape),
        preferred_element_type=jnp.float32,
    )
    value_grad = (
        jnp.einsum(
            "phqk,pqhe->pkhe",
            attn_probs.astype(jnp.bfloat16),
            heads_grad,
            preferred_element_type=jnp.float32,
        )
        .reshape(byte_rows, D)
        .astype(jnp.bfloat16)
    )
    score_grad = (
        attn_probs * (probs_grad - jnp.sum(attn_probs * probs_grad, axis=-1, keepdims=True))
    ).astype(jnp.bfloat16)
    query_grad = (
        (
            jnp.einsum(
                "phqk,pkhe->pqhe",
                score_grad,
                key_rows.reshape(head_shape),
                preferred_element_type=jnp.float32,
            )
            * score_scale
        )
        .reshape(byte_rows, D)
        .astype(jnp.bfloat16)
    )
    key_grad = (
        (
            jnp.einsum(
                "phqk,pqhe->pkhe",
                score_grad,
                queries.reshape(head_shape),
                preferred_element_type=jnp.float32,
            )
            * score_scale
        )
        .reshape(byte_rows, D)
        .astype(jnp.bfloat16)
    )
    grad_query = jnp.einsum(
        "rd,re->de", normed_attn, query_grad, preferred_element_type=jnp.float32
    )
    grad_key = jnp.einsum("rd,re->de", normed_attn, key_grad, preferred_element_type=jnp.float32)
    grad_value = jnp.einsum(
        "rd,re->de", normed_attn, value_grad, preferred_element_type=jnp.float32
    )
    normed_grad = jnp.einsum("re,de->rd", query_grad, query_all, preferred_element_type=jnp.float32)
    normed_grad = normed_grad + jnp.einsum(
        "re,de->rd", key_grad, key_all, preferred_element_type=jnp.float32
    )
    normed_grad = normed_grad + jnp.einsum(
        "re,de->rd", value_grad, value_all, preferred_element_type=jnp.float32
    )
    attn_normed, attn_norm_back = jax.vjp(root_norm, stream, gain_attn)
    stream_norm_grad, grad_gain_attn = attn_norm_back(normed_grad)
    stream_grad = (after_grad + stream_norm_grad).astype(jnp.bfloat16)
    grad_local = jnp.einsum(
        "re,rd->ed", local_rows, stream_grad, preferred_element_type=jnp.float32
    )
    global_grad = jnp.einsum(
        "rd,ed->re", stream_grad, local_all, preferred_element_type=jnp.float32
    ).reshape(patches, D)
    mix_grad = global_grad.astype(jnp.bfloat16)
    grad_out = jnp.einsum("pi,pd->id", gated_low, mix_grad, preferred_element_type=jnp.float32)
    gated_grad = jnp.einsum("pd,id->pi", mix_grad, out_all, preferred_element_type=jnp.float32)
    proj_grad_mix, rim_grad_mix, small_grad_mix, incoming_grad, grad_gated_gain = mixer_back(
        gated_grad
    )
    suffix = carried_in_2(
        (decay_total, incoming_grad),
        ("narrow", "wide"),
        combine_states,
        (jnp.ones_like(decay_total), jnp.zeros_like(incoming_grad)),
    )
    later_grad = suffix[1]
    decay_grad = jnp.sum(later_grad * incoming, axis=(1, 2))
    proj_grad_state, rim_grad_state, small_grad_state = state_back((decay_grad, later_grad))
    rim_from_next = passed_along(rim_grad_mix + rim_grad_state, ("narrow", "wide"), -1)
    proj_grad = proj_grad_mix + proj_grad_state
    proj_grad = proj_grad.at[patches - (CONV - 1) :, DI : 2 * DI + 2 * STATE].add(rim_from_next)
    proj_low = proj_grad.astype(jnp.bfloat16)
    grad_in = jnp.einsum("pd,pk->dk", normed_mix, proj_low, preferred_element_type=jnp.float32)
    normed_mix_grad = jnp.einsum("pk,dk->pd", proj_low, in_all, preferred_element_type=jnp.float32)
    mix_normed, mix_norm_back = jax.vjp(root_norm, mixed_in, gain_mix)
    mixed_norm_grad, grad_gain_mix = mix_norm_back(normed_mix_grad)
    embed_grad = (global_grad + mixed_norm_grad).astype(jnp.bfloat16)
    grad_patch = jnp.einsum("pi,pd->id", embedded, embed_grad, preferred_element_type=jnp.float32)
    byte_grad = (
        jnp.einsum("pd,id->pi", embed_grad, patch_all, preferred_element_type=jnp.float32).reshape(
            byte_rows, EMB
        )
        * keep_mask[:, None]
    )
    grad_table = jnp.dot(onehot.astype(jnp.float32).T, byte_grad, precision=highest)
    shared = (
        lax.psum_scatter(grad_table, ("narrow", "wide"), scatter_dimension=0, tiled=True),
        lax.psum_scatter(grad_patch, ("narrow", "wide"), scatter_dimension=0, tiled=True),
        lax.psum_scatter(grad_in, ("narrow", "wide"), scatter_dimension=0, tiled=True),
        lax.psum_scatter(grad_out, ("narrow", "wide"), scatter_dimension=0, tiled=True),
        lax.psum_scatter(grad_local, ("narrow", "wide"), scatter_dimension=1, tiled=True),
        lax.psum_scatter(grad_query, ("narrow", "wide"), scatter_dimension=0, tiled=True),
        lax.psum_scatter(grad_key, ("narrow", "wide"), scatter_dimension=0, tiled=True),
        lax.psum_scatter(grad_value, ("narrow", "wide"), scatter_dimension=0, tiled=True),
        lax.psum_scatter(grad_attn, ("narrow", "wide"), scatter_dimension=0, tiled=True),
    )
    small_sum = lax.psum(
        (
            small_grad_mix[0] + small_grad_state[0],
            small_grad_mix[1] + small_grad_state[1],
            small_grad_mix[2] + small_grad_state[2],
            small_grad_mix[3] + small_grad_state[3],
            small_grad_mix[4] + small_grad_state[4],
            grad_gain_mix,
            grad_gated_gain,
            grad_gain_attn,
            grad_feed_gain,
        ),
        ("narrow", "wide"),
    )
    return (
        out_rows,
        shared[0],
        shared[1],
        small_sum[5],
        shared[2],
        small_sum[0],
        small_sum[1],
        small_sum[2],
        small_sum[3],
        small_sum[4],
        small_sum[6],
        shared[3],
        shared[4],
        small_sum[7],
        shared[5],
        shared[6],
        shared[7],
        shared[8],
        small_sum[8],
        grad_gate,
        grad_up,
        grad_down,
    )


def solution(mesh):
    placed = (
        P(("narrow", "wide")),
        P(),
        P(),
        P(("narrow", "wide"), None),
        P(("narrow", "wide"), None),
        P(),
        P(("narrow", "wide"), None),
        P(),
        P(),
        P(),
        P(),
        P(),
        P(),
        P(("narrow", "wide"), None),
        P(None, ("narrow", "wide")),
        P(),
        P(("narrow", "wide"), None),
        P(("narrow", "wide"), None),
        P(("narrow", "wide"), None),
        P(("narrow", "wide"), None),
        P(),
        P("narrow", "wide"),
        P("narrow", "wide"),
        P("wide", "narrow"),
        P(("narrow", "wide"), None),
    )
    return jax.shard_map(
        per_device,
        mesh=mesh,
        in_specs=placed,
        out_specs=(
            P(("narrow", "wide"), None),
            P(("narrow", "wide"), None),
            P(("narrow", "wide"), None),
            P(),
            P(("narrow", "wide"), None),
            P(),
            P(),
            P(),
            P(),
            P(),
            P(),
            P(("narrow", "wide"), None),
            P(None, ("narrow", "wide")),
            P(),
            P(("narrow", "wide"), None),
            P(("narrow", "wide"), None),
            P(("narrow", "wide"), None),
            P(("narrow", "wide"), None),
            P(),
            P("narrow", "wide"),
            P("narrow", "wide"),
            P("wide", "narrow"),
        ),
        check_vma=False,
    )
```

profile of v0, /device:TPU:9, one launch (start us, length us, event | category | flops | bytes accessed | tf_op | source)
XLA Modules:
  0.0 3026.1 jit_solution(4190395277640049958)
XLA Ops:
  11.9 38.1 %all_gather.51 = bf16[256,128]{1,0:T(8,128)(2,1)S(1)} all-gather(bf16[8,128]{1,0:T(8,128)(2,1)} %param.35), channel_id=1, replica_groups=mesh['narrow'=4,'wide'=8] {'narrow','wide'}, dimensions={0}, use_global_device_ids=true | all-gather | bytes 67584 | tf_op jit(solution)/shard_map/all_gather | solution.py:264
  54.5 13.8 all-gather.15.cloned.1.call-done
  70.5 81.2 %all-gather.17.cloned.1.call-done = bf16[1024,4384]{1,0:T(8,128)(2,1)} async-done(((bf16[32,4384]{1,0:T(8,128)(2,1)}), bf16[1024,4384]{1,0:T(8,128)(2,1)}) %all-gather.17.cloned.1.call-update) | async-done | bytes 8978448 | tf_op jit(solution)/shard_map/all_gather | solution.py:266
  151.8 5.4 fusion.146
  169.3 10.3 all_to_all.64
  180.3 48.4 %all_gather.58 = bf16[128,1024]{0,1:T(8,128)(2,1)} all-gather(bf16[128,32]{0,1:T(8,128)(2,1)S(1)} %copy-done.108), channel_id=1, replica_groups=mesh['narrow'=4,'wide'=8] {'narrow','wide'}, dimensions={1}, use_global_device_ids=true | all-gather | bytes 270336 | tf_op jit(solution)/shard_map/all_gather | solution.py:268
  228.9 37.5 %all-gather.2 = bf16[32,1,32]{2,1,0:T(2,128)(2,1)S(1)} all-gather(bf16[1,1,32]{2,1,0:T(2,128)(2,1)S(1)} %get-tuple-element.275), channel_id=1, replica_groups=mesh['narrow'=4,'wide'=8] {'narrow','wide'}, dimensions={0}, use_global_device_ids=true | all-gather | bytes 2112 | tf_op jit(solution)/shard_map/all_gather | solution.py:35
  266.6 17.3 all-gather.33.cloned.1.call-done
  284.0 4.3 while.27
  295.3 52.9 %all-gather.19.cloned.1.call-done = bf16[2048,1024]{1,0:T(8,128)(2,1)} async-done(((bf16[64,1024]{1,0:T(8,128)(2,1)}), bf16[2048,1024]{1,0:T(8,128)(2,1)}) %all-gather.19.cloned.1.call-update) | async-done | bytes 4194320 | tf_op jit(solution)/shard_map/all_gather | solution.py:267
  353.7 51.5 %all-gather.23.cloned.1.call-done = bf16[1024,1024]{1,0:T(8,128)(2,1)} async-done(((bf16[32,1024]{1,0:T(8,128)(2,1)}), bf16[1024,1024]{1,0:T(8,128)(2,1)}) %all-gather.23.cloned.1.call-update) | async-done | bytes 2097168 | tf_op jit(solution)/shard_map/all_gather | solution.py:269
  411.0 52.4 %all-gather.25.cloned.1.call-done = bf16[1024,1024]{1,0:T(8,128)(2,1)} async-done(((bf16[32,1024]{1,0:T(8,128)(2,1)}), bf16[1024,1024]{1,0:T(8,128)(2,1)}) %all-gather.25.cloned.1.call-update) | async-done | bytes 2097168 | tf_op jit(solution)/shard_map/all_gather | solution.py:270
  469.0 52.8 %all-gather.21.cloned.1.call-done = bf16[1024,1024]{1,0:T(8,128)(2,1)} async-done(((bf16[32,1024]{1,0:T(8,128)(2,1)}), bf16[1024,1024]{1,0:T(8,128)(2,1)}) %all-gather.21.cloned.1.call-update) | async-done | bytes 2097168 | tf_op jit(solution)/shard_map/all_gather | solution.py:271
  527.4 5.3 fusion.147
  539.2 40.9 %all-gather.27.cloned.1.call-done = bf16[1024,1024]{1,0:T(8,128)(2,1)} async-done(((bf16[32,1024]{1,0:T(8,128)(2,1)}), bf16[1024,1024]{1,0:T(8,128)(2,1)}) %all-gather.27.cloned.1.call-update) | async-done | bytes 2097168 | tf_op jit(solution)/shard_map/all_gather | solution.py:272
  583.9 11.1 all_to_all.65
  598.9 28.2 all-gather.31.cloned.1.call-done
  627.1 7.8 convolution_convert_fusion.1
  634.9 39.5 %all-gather.29.cloned.1.call-done = bf16[8192,256]{1,0:T(8,128)(2,1)} async-done(((bf16[1024,256]{1,0:T(8,128)(2,1)}), bf16[8192,256]{1,0:T(8,128)(2,1)}) %all-gather.29.cloned.1.call-update) | async-done | bytes 4194320 | tf_op jit(solution)/shard_map/all_gather | solution.py:201
  674.4 12.6 convolution_convert_fusion
  687.3 444.1 %all-reduce.39.cloned.1.call-done = (bf16[8192,1024]{1,0:T(8,128)(2,1)}, bf16[8192,512]{1,0:T(8,128)(2,1)}) async-done(((bf16[8192,1024]{1,0:T(8,128)(2,1)}, bf16[8192,512]{1,0:T(8,128)(2,1)}), (bf16[8192,1024]{1,0:T(8,128)(2,1)}, bf16[8192,512]{1,0:T(8,128)(2,1)})) %all-reduce.39.cloned.1.call-update) | async-done | bytes 25165840 | tf_op jit(solution)/shard_map/psum | solution.py:215
  1131.4 18.6 convert_element_type.294
  1150.0 21.1 fusion.3
  1174.4 8.4 fusion.8
  1182.9 7.8 convolution_convert_fusion.2
  1190.8 41.4 %reduce-scatter.13.cloned.1.call-done = bf16[1024,256]{1,0:T(8,128)(2,1)} async-done(((bf16[8192,256]{1,0:T(8,128)(2,1)}), bf16[1024,256]{1,0:T(8,128)(2,1)}) %reduce-scatter.13.cloned.1.call-update) | async-done | bytes 524304 | tf_op jit(solution)/shard_map/reduce_scatter | solution.py:205
  1236.3 46.3 %reduce-scatter.11.cloned.1.call-done = bf16[1024,256]{1,0:T(8,128)(2,1)} async-done(((bf16[8192,256]{1,0:T(8,128)(2,1)}), bf16[1024,256]{1,0:T(8,128)(2,1)}) %reduce-scatter.11.cloned.1.call-update) | async-done | bytes 524304 | tf_op jit(solution)/shard_map/reduce_scatter | solution.py:205
  1282.7 4.1 all-to-all-start.1
  1334.2 4.2 multiply_reduce_fusion.20
  1360.6 99.8 %all-gather.35.cloned.1.call-done = bf16[1024,64,128]{2,1,0:T(8,128)(2,1)} async-done(((bf16[32,64,128]{2,1,0:T(8,128)(2,1)}), bf16[1024,64,128]{2,1,0:T(8,128)(2,1)}) %all-gather.35.cloned.1.call-update) | async-done | bytes 16777232 | tf_op jit(solution)/shard_map/all_gather | solution.py:57
  1460.5 56.7 %while.28 = (s32[]{:T(128)}, f32[32,64,128]{2,1,0:T(8,128)S(1)}, s32[]{:T(128)}, bf16[32,32]{1,0:T(8,128)(2,1)}, bf16[32,32,64,128]{3,2,1,0:T(8,128)(2,1)}, /*index=5*/s32[]{:T(128)}, s32[]{:T(128)}, s32[]{:T(128)}, s32[]{:T(128)}) while((s32[]{:T(128)}, f32[32,64,128]{2,1,0:T(8,128)S(1)}, s32[]{:T(128)}, bf16[32,32]{1,0:T(8,128)(2,1)}, ...), condition=%wide.region_31.33_spmd, body=%wide.region_30.32_spmd.sunk | while | flops 786470 | bytes 2621907 | solution.py:74
  1519.5 4.4 broadcast_multiply_fusion
  1533.5 4.2 collective-permute-start.1
  1541.6 7.1 multiply_reduce_fusion.24
  1567.4 4.6 fusion.99
  1578.8 7.8 fusion.88
  1586.6 11.8 fusion.6
  1599.4 6.6 fusion.164
  1606.0 66.2 %all-reduce.35.cloned.1.call-done = f32[256,128]{1,0:T(8,128)} async-done(((f32[256,128]{1,0:T(8,128)}), f32[256,128]{1,0:T(8,128)}) %all-reduce.35.cloned.1.call-update) | async-done | bytes 131088
  1673.5 125.6 %reduce-scatter.21.cloned.1.call-done = f32[128,32]{0,1:T(8,128)} async-done(((f32[128,1024]{0,1:T(8,128)}), f32[128,32]{0,1:T(8,128)}) %reduce-scatter.21.cloned.1.call-update) | async-done | bytes 16400 | tf_op jit(solution)/shard_map/reduce_scatter | solution.py:467
  1799.0 141.9 %reduce-scatter.27.cloned.1.call-done = f32[32,1024]{1,0:T(8,128)} async-done(((f32[1024,1024]{1,0:T(8,128)}), f32[32,1024]{1,0:T(8,128)}) %reduce-scatter.27.cloned.1.call-update) | async-done | bytes 131088 | tf_op jit(solution)/shard_map/reduce_scatter | solution.py:470
  1940.9 142.7 %reduce-scatter.25.cloned.1.call-done = f32[32,1024]{1,0:T(8,128)} async-done(((f32[1024,1024]{1,0:T(8,128)}), f32[32,1024]{1,0:T(8,128)}) %reduce-scatter.25.cloned.1.call-update) | async-done | bytes 131088 | tf_op jit(solution)/shard_map/reduce_scatter | solution.py:469
  2083.6 142.6 %reduce-scatter.29.cloned.1.call-done = f32[32,1024]{1,0:T(8,128)} async-done(((f32[1024,1024]{1,0:T(8,128)}), f32[32,1024]{1,0:T(8,128)}) %reduce-scatter.29.cloned.1.call-update) | async-done | bytes 131088 | tf_op jit(solution)/shard_map/reduce_scatter | solution.py:471
  2226.2 142.3 %reduce-scatter.23.cloned.1.call-done = f32[32,1024]{1,0:T(8,128)} async-done(((f32[1024,1024]{1,0:T(8,128)}), f32[32,1024]{1,0:T(8,128)}) %reduce-scatter.23.cloned.1.call-update) | async-done | bytes 131088 | tf_op jit(solution)/shard_map/reduce_scatter | solution.py:468
  2368.6 152.3 %reduce-scatter.19.cloned.1.call-done = f32[64,1024]{1,0:T(8,128)} async-done(((f32[2048,1024]{1,0:T(8,128)}), f32[64,1024]{1,0:T(8,128)}) %reduce-scatter.19.cloned.1.call-update) | async-done | bytes 262160 | tf_op jit(solution)/shard_map/reduce_scatter | solution.py:466
  2520.9 138.9 %all-reduce.37.cloned.1.call-done = (f32[1024]{0:T(1024)}, f32[4,2304]{1,0:T(4,128)}, f32[2304]{0:T(1024)}, f32[32]{0:T(128)}, f32[32]{0:T(128)}, /*index=5*/f32...) async-done(((f32[1024]{0:T(1024)}, f32[4,2304]{1,0:T(4,128)}, f32[2304]{0:T(1024)}, f32[32]{0:T(128)}, f32[32]{0:T(128)}, /*index=5*/f32[32]{0:T(128)}, ...) | async-done | bytes 66960 | tf_op jit(solution)/shard_map/psum | solution.py:473
  2659.8 138.3 %reduce-scatter.15.cloned.1.call-done = f32[32,1024]{1,0:T(8,128)} async-done(((f32[1024,1024]{1,0:T(8,128)}), f32[32,1024]{1,0:T(8,128)}) %reduce-scatter.15.cloned.1.call-update) | async-done | bytes 131088 | tf_op jit(solution)/shard_map/reduce_scatter | solution.py:464
  2798.1 209.7 %reduce-scatter.17.cloned.1.call-done = f32[32,4384]{1,0:T(8,128)} async-done(((f32[1024,4384]{1,0:T(8,128)}), f32[32,4384]{1,0:T(8,128)}) %reduce-scatter.17.cloned.1.call-update) | async-done | bytes 561168 | tf_op jit(solution)/shard_map/reduce_scatter | solution.py:465
  (553 shorter events, 258.2 us)
Async XLA Ops:
  7.2 619.9 %copy-start = (bf16[512,256]{1,0:T(8,128)(2,1)S(1)}, bf16[512,256]{1,0:T(8,128)(2,1)}, u32[]{:S(2)}) copy-start(bf16[512,256]{1,0:T(8,128)(2,1)} %param.55) | copy-start | bytes 786436
  7.2 61.1 %all-gather.15.cloned.1.call-start = ((), (), s32[]{:S(2)}) async-start(), calls=%async_computation.14 | async-start | bytes 2162688 | tf_op jit(solution)/shard_map/all_gather | solution.py:265
  7.9 143.8 %all-gather.17.cloned.1.call-start = ((), (), s32[]{:S(2)}) async-start(), calls=%async_computation.15 | async-start | bytes 9461760 | tf_op jit(solution)/shard_map/all_gather | solution.py:266
  8.7 275.2 %all-gather.33.cloned.1.call-start = ((), (), s32[]{:S(2)}) async-start(), calls=%async_computation.33 | async-start | bytes 17301504 | tf_op jit(solution)/shard_map/all_gather | solution.py:35
  11.9 157.2 %copy-start.84 = (f32[256]{0:T(256)}, f32[256]{0:T(256)S(1)}, u32[]{:S(2)}) copy-start(f32[256]{0:T(256)S(1)} %sub.102) | copy-start | bytes 3076
  50.9 100.8 %copy-start.43 = (bf16[32,1024]{1,0:T(8,128)(2,1)}, bf16[32,1024]{1,0:T(8,128)(2,1)S(1)}, u32[]{:S(2)}) copy-start(bf16[32,1024]{1,0:T(8,128)(2,1)S(1)} %reshape.550) | copy-start | bytes 196612
  51.6 108.5 %copy-start.119 = (f32[32]{0:T(128)}, f32[32]{0:T(128)S(1)}, u32[]{:S(2)}) copy-start(f32[32]{0:T(128)S(1)} %exp.46) | copy-start | bytes 388
  52.7 108.2 %copy-start.110 = (f32[32]{0:T(128)}, f32[32]{0:T(128)S(1)}, u32[]{:S(2)}) copy-start(f32[32]{0:T(128)S(1)} %fusion.137) | copy-start | bytes 388
  53.7 107.9 %copy-start.58 = (f32[2304]{0:T(1024)}, f32[2304]{0:T(1024)S(1)}, u32[]{:S(2)}) copy-start(f32[2304]{0:T(1024)S(1)} %get-tuple-element.193) | copy-start | bytes 27652
  53.7 107.9 %copy-start.59 = (f32[2304]{0:T(1024)}, f32[2304]{0:T(1024)S(1)}, u32[]{:S(2)}) copy-start(f32[2304]{0:T(1024)S(1)} %get-tuple-element.194) | copy-start | bytes 27652
  53.7 107.9 %copy-start.60 = (f32[2304]{0:T(1024)}, f32[2304]{0:T(1024)S(1)}, u32[]{:S(2)}) copy-start(f32[2304]{0:T(1024)S(1)} %get-tuple-element.196) | copy-start | bytes 27652
  53.7 107.9 %copy-start.61 = (f32[2304]{0:T(1024)}, f32[2304]{0:T(1024)S(1)}, u32[]{:S(2)}) copy-start(f32[2304]{0:T(1024)S(1)} %get-tuple-element.195) | copy-start | bytes 27652
  54.5 106.4 %copy-start.104 = (f32[32]{0:T(128)}, f32[32]{0:T(128)S(1)}, u32[]{:S(2)}) copy-start(f32[32]{0:T(128)S(1)} %get-tuple-element.283) | copy-start | bytes 388
  54.5 107.1 %copy-start.112 = (f32[32]{0:T(128)}, f32[32]{0:T(128)S(1)}, u32[]{:S(2)}) copy-start(f32[32]{0:T(128)S(1)} %get-tuple-element.278) | copy-start | bytes 388
  54.5 107.1 %copy-start.113 = (f32[32]{0:T(128)}, f32[32]{0:T(128)S(1)}, u32[]{:S(2)}) copy-start(f32[32]{0:T(128)S(1)} %get-tuple-element.279) | copy-start | bytes 388
  54.5 107.1 %copy-start.114 = (f32[32]{0:T(128)}, f32[32]{0:T(128)S(1)}, u32[]{:S(2)}) copy-start(f32[32]{0:T(128)S(1)} %get-tuple-element.280) | copy-start | bytes 388
  157.2 137.9 %copy-start.24 = (f32[32,4384]{1,0:T(8,128)}, f32[32,4384]{1,0:T(8,128)S(1)}, u32[]{:S(2)}) copy-start(f32[32,4384]{1,0:T(8,128)S(1)} %get-tuple-element.288) | copy-start | bytes 1683460
  157.2 4.3 collective-permute-start
  161.6 104.8 %copy-start.50 = (f32[3,2304]{1,0:T(4,128)}, f32[3,2304]{1,0:T(4,128)S(1)}, u32[]{:S(2)}) copy-start(f32[3,2304]{1,0:T(4,128)S(1)} %convert_element_type.269) | copy-start | bytes 82948
  162.6 125.7 %copy-start.25 = (f32[32,2304]{1,0:T(8,128)}, f32[32,2304]{1,0:T(8,128)S(1)}, u32[]{:S(2)}) copy-start(f32[32,2304]{1,0:T(8,128)S(1)} %get-tuple-element.247) | copy-start | bytes 884740
  165.8 182.3 %all-gather.19.cloned.1.call-start = ((), (), s32[]{:S(2)}) async-start(), calls=%async_computation.16 | async-start | bytes 4325376 | tf_op jit(solution)/shard_map/all_gather | solution.py:267
  166.4 238.8 %all-gather.23.cloned.1.call-start = ((), (), s32[]{:S(2)}) async-start(), calls=%async_computation.18 | async-start | bytes 2162688 | tf_op jit(solution)/shard_map/all_gather | solution.py:269
  167.0 296.4 %all-gather.25.cloned.1.call-start = ((), (), s32[]{:S(2)}) async-start(), calls=%async_computation.19 | async-start | bytes 2162688 | tf_op jit(solution)/shard_map/all_gather | solution.py:270
  167.6 354.2 %all-gather.21.cloned.1.call-start = ((), (), s32[]{:S(2)}) async-start(), calls=%async_computation.17 | async-start | bytes 2162688 | tf_op jit(solution)/shard_map/all_gather | solution.py:271
  168.3 411.8 %all-gather.27.cloned.1.call-start = ((), (), s32[]{:S(2)}) async-start(), calls=%async_computation.20 | async-start | bytes 2162688 | tf_op jit(solution)/shard_map/all_gather | solution.py:272
  169.1 458.0 %all-gather.31.cloned.1.call-start = ((), (), s32[]{:S(2)}) async-start(), calls=%async_computation.23 | async-start | bytes 4718592 | tf_op jit(solution)/shard_map/all_gather | solution.py:201
  179.7 494.8 %all-gather.29.cloned.1.call-start = ((), (), s32[]{:S(2)}) async-start(), calls=%async_computation.21 | async-start | bytes 4718592 | tf_op jit(solution)/shard_map/all_gather | solution.py:201
  595.1 536.4 %all-reduce.39.cloned.1.call-start = ((), (), s32[]{:S(2)}) async-start(), calls=%async_computation.37 | async-start | bytes 50331648 | tf_op jit(solution)/shard_map/psum | solution.py:215
  687.0 545.1 %reduce-scatter.13.cloned.1.call-start = ((), (), s32[]{:S(2)}) async-start(), calls=%async_computation.24 | async-start | bytes 4718592 | tf_op jit(solution)/shard_map/reduce_scatter | solution.py:205
  1182.9 99.8 %reduce-scatter.11.cloned.1.call-start = ((), (), s32[]{:S(2)}) async-start(), calls=%async_computation.22 | async-start | bytes 4718592 | tf_op jit(solution)/shard_map/reduce_scatter | solution.py:205
  1190.7 97.8 %copy-start.77 = (f32[1024]{0:T(1024)S(1)}, f32[1024]{0:T(1024)}, u32[]{:S(2)}) copy-start(f32[1024]{0:T(1024)} %param.52) | copy-start | bytes 12292
  1190.7 97.8 %copy-start.83 = (f32[256]{0:T(256)S(1)}, f32[256]{0:T(256)}, u32[]{:S(2)}) copy-start(f32[256]{0:T(256)} %copy-done.82) | copy-start | bytes 3076
  1190.7 98.7 %copy-start.103 = (f32[256]{0:T(256)S(1)}, f32[256]{0:T(256)}, u32[]{:S(2)}) copy-start(f32[256]{0:T(256)} %copy-done.102) | copy-start | bytes 3076
  1232.2 50.5 %all-to-all-start.3 = ((bf16[4,256,256]{2,1,0:T(8,128)(2,1)}), bf16[4,256,256]{2,1,0:T(8,128)(2,1)}, u32[]{:S(2)}, u32[]{:S(2)}) async-start(bf16[4,256,256]{2,1,0:T(8,128)(2,1)} %bitcast.184), calls=%async_computation.5 | async-start | bytes 1048576 | tf_op jit(solution)/shard_map/all_to_all | solution.py:211
  1282.7 11.3 all-to-all-start.1
  1286.8 173.6 %all-gather.35.cloned.1.call-start = ((), (), s32[]{:S(2)}) async-start(), calls=%async_computation.34 | async-start | bytes 17301504 | tf_op jit(solution)/shard_map/all_gather | solution.py:57
  1345.8 326.4 %all-reduce.35.cloned.1.call-start = ((), (), s32[]{:S(2)}) async-start(), calls=%async_computation.35 | async-start | bytes 262144
  1533.5 7.1 collective-permute-start.1
  1550.8 248.3 %reduce-scatter.21.cloned.1.call-start = ((), (), s32[]{:S(2)}) async-start(), calls=%async_computation.28 | async-start | bytes 540672 | tf_op jit(solution)/shard_map/reduce_scatter | solution.py:467
  1552.0 388.9 %reduce-scatter.27.cloned.1.call-start = ((), (), s32[]{:S(2)}) async-start(), calls=%async_computation.31 | async-start | bytes 4325376 | tf_op jit(solution)/shard_map/reduce_scatter | solution.py:470
  1554.9 528.7 %reduce-scatter.25.cloned.1.call-start = ((), (), s32[]{:S(2)}) async-start(), calls=%async_computation.30 | async-start | bytes 4325376 | tf_op jit(solution)/shard_map/reduce_scatter | solution.py:469
  1558.7 667.5 %reduce-scatter.29.cloned.1.call-start = ((), (), s32[]{:S(2)}) async-start(), calls=%async_computation.32 | async-start | bytes 4325376 | tf_op jit(solution)/shard_map/reduce_scatter | solution.py:471
  1563.9 804.7 %reduce-scatter.23.cloned.1.call-start = ((), (), s32[]{:S(2)}) async-start(), calls=%async_computation.29 | async-start | bytes 4325376 | tf_op jit(solution)/shard_map/reduce_scatter | solution.py:468
  1566.7 954.2 %reduce-scatter.19.cloned.1.call-start = ((), (), s32[]{:S(2)}) async-start(), calls=%async_computation.27 | async-start | bytes 8650752 | tf_op jit(solution)/shard_map/reduce_scatter | solution.py:466
  1572.2 1087.6 %all-reduce.37.cloned.1.call-start = ((), (), s32[]{:S(2)}) async-start(), calls=%async_computation.36 | async-start | bytes 142336 | tf_op jit(solution)/shard_map/psum | solution.py:473
  1575.9 1222.2 %reduce-scatter.15.cloned.1.call-start = ((), (), s32[]{:S(2)}) async-start(), calls=%async_computation.25 | async-start | bytes 4325376 | tf_op jit(solution)/shard_map/reduce_scatter | solution.py:464
  1578.7 1429.1 %reduce-scatter.17.cloned.1.call-start = ((), (), s32[]{:S(2)}) async-start(), calls=%async_computation.26 | async-start | bytes 18923520 | tf_op jit(solution)/shard_map/reduce_scatter | solution.py:465
  1599.4 1419.7 %copy-start.1 = (bf16[512,256]{1,0:T(8,128)(2,1)S(1)}, bf16[512,256]{1,0:T(8,128)(2,1)}, u32[]{:S(2)}) copy-start(bf16[512,256]{1,0:T(8,128)(2,1)} %param.55) | copy-start | bytes 786436
  (111 other events, 1535.8 us)
Sparse Core Ops, SparseCore 0:
  11.0 57.2 all-gather.14
  71.2 80.5 all-gather.16
  165.9 117.9 all-gather.32
  286.8 61.3 all-gather.18
  351.0 54.1 all-gather.22
  408.0 55.3 all-gather.24
  466.4 55.3 all-gather.20
  524.7 55.3 all-gather.26
  581.7 45.3 all-gather.30
  628.5 45.8 all-gather.28
  687.2 444.1 all-reduce.38
  1183.0 49.1 reduce-scatter.12
  1234.5 48.1 reduce-scatter.10
  1345.9 114.4 all-gather.34
  1550.9 121.2 all-reduce.34
  1674.9 124.1 reduce-scatter.20
  1801.8 139.0 reduce-scatter.26
  1943.7 139.8 reduce-scatter.24
  2086.6 139.6 reduce-scatter.28
  2229.0 139.4 reduce-scatter.22
  2371.5 149.2 reduce-scatter.18
  2530.1 129.5 all-reduce.36
  2662.6 135.4 reduce-scatter.14
  2800.9 206.8 reduce-scatter.16
where the time goes:
time: 3040 us; the launch traced here: 3030 us
  waiting for transfers between devices  2470 us (81%)
  matrix products  168 us (6%)
  blocking collectives  145 us (5%)
  other arithmetic  131 us (4%)
  local copies, waits for them, and re-layouts  75.3 us (2%)
    psum x1, waiting for transfers between devices, narrow_total(): return lax.psum(partial_rows, 'narrow').astype(jnp.float32)  444 us
    reduce_scatter x1, waiting for transfers between devices, per_device(): lax.psum_scatter(grad_in, ('narrow', 'wide'), scatter_dimension=0, tiled=...  210 us
    reduce_scatter x1, waiting for transfers between devices, per_device(): lax.psum_scatter(grad_out, ('narrow', 'wide'), scatter_dimension=0, tiled...  152 us
    reduce_scatter x1, waiting for transfers between devices, per_device(): lax.psum_scatter(grad_key, ('narrow', 'wide'), scatter_dimension=0, tiled...  143 us
    reduce_scatter x1, waiting for transfers between devices, per_device(): lax.psum_scatter(grad_attn, ('narrow', 'wide'), scatter_dimension=0, tile...  143 us
    reduce_scatter x1, waiting for transfers between devices, per_device(): lax.psum_scatter(grad_query, ('narrow', 'wide'), scatter_dimension=0, til...  142 us
    reduce_scatter x1, waiting for transfers between devices, per_device(): lax.psum_scatter(grad_value, ('narrow', 'wide'), scatter_dimension=0, til...  142 us
    psum x1, waiting for transfers between devices, per_device(): lax.psum((small_grad_mix[0] + small_grad_state[0], small_grad_mix[1] + sm...  139 us
  transfers between devices with their start and end apart: 28, of which 25 were waited for; matrix products, arithmetic and copies ran while one was open for 5% of the time, Pallas kernels for 0%

commit v1 on v0

--- a/solution.py
+++ b/solution.py
@@ -3,6 +3,8 @@
 import jax
 import jax.numpy as jnp
 from jax import lax
+from jax.experimental import pallas as pl
+from jax.experimental.pallas import tpu as pltpu
 from jax.sharding import PartitionSpec as P
 
 D = 1024
@@ -23,6 +25,14 @@
 masked_score = -1e30
 
 
+def running_sum(x):
+    place = jnp.arange(x.shape[0])
+    seen = place[:, None] >= place[None, :]
+    if x.ndim == 1:
+        return jnp.sum(jnp.where(seen, x[None, :], 0), axis=1).astype(x.dtype)
+    return jnp.dot(seen.astype(x.dtype), x, precision=highest)
+
+
 def passed_along(x, axis, by):
     peers = lax.axis_size(axis)
     pairs = [(i, i + by) for i in range(peers) if 0 <= i + by < peers]
@@ -80,7 +90,7 @@
 
 def patch_layout(doc_patches, pad_bytes, first_index, patch_count):
     patch_index = first_index + jnp.arange(patch_count, dtype=jnp.int32)
-    doc_ends = jnp.cumsum(doc_patches)
+    doc_ends = running_sum(doc_patches)
     doc_index = jnp.arange(doc_patches.shape[0], dtype=jnp.int32)
     segment = jnp.sum((patch_index[:, None] >= doc_ends[None, :]).astype(jnp.int32), axis=1)
     owner_mask = segment[:, None] == doc_index[None, :]
@@ -113,8 +123,8 @@
     input_map = activated[:, DI : DI + STATE]
     output_map = activated[:, DI + STATE :]
     time_steps = jax.nn.softplus(projected[:, 2 * DI + 2 * STATE :] + step_bias)
-    cumulative = jnp.cumsum(-time_steps * jnp.exp(log_rate), axis=0)
-    no_reset = (jnp.cumsum(first_patch) == 0).astype(jnp.float32)
+    cumulative = running_sum(-time_steps * jnp.exp(log_rate))
+    no_reset = (running_sum(first_patch) == 0).astype(jnp.float32)
     return (values, input_map, output_map, time_steps, cumulative, no_reset)
 
 
@@ -224,7 +234,7 @@
     return jnp.concatenate([gate_grad, up_grad], axis=1)
 
 
-def per_device(
+def per_device_rows(
     byte_ids,
     doc_patches,
     pad_bytes,
@@ -510,6 +520,758 @@
     )
 
 
+QUERY = 128
+BYTE_BLOCK = 128
+MESH = pl.DeviceIdType.MESH
+LOW = jnp.bfloat16
+FULL = jnp.float32
+BOTH = ("narrow", "wide")
+
+
+def nn(a, b, precision=None):
+    return lax.dot_general(
+        a, b, (((1,), (0,)), ((), ())), precision=precision, preferred_element_type=FULL
+    )
+
+
+def nt(a, b, precision=None):
+    return lax.dot_general(
+        a, b, (((1,), (1,)), ((), ())), precision=precision, preferred_element_type=FULL
+    )
+
+
+def tn(a, b, precision=None):
+    return lax.dot_general(
+        a, b, (((0,), (0,)), ((), ())), precision=precision, preferred_element_type=FULL
+    )
+
+
+def gather_kernel(count, narrow, depth, *refs):
+    ins, outs = refs[:count], refs[count : 2 * count]
+    local, z_send, z_recv, n_send, n_recv, c_send, c_recv = refs[2 * count :]
+    n, w = lax.axis_index("narrow"), lax.axis_index("wide")
+    z, c = lax.div(w, 2), lax.rem(w, 2)
+    z_peers = [(n, lax.rem(z + k, depth) * 2 + c) for k in range(1, depth)]
+    n_peers = [lax.rem(n + k, narrow) for k in range(1, narrow)]
+    twin = (n, z * 2 + 1 - c)
+    barrier = pltpu.get_barrier_semaphore()
+    for peer in z_peers:
+        pl.semaphore_signal(barrier, inc=1, device_id=peer, device_id_type=MESH)
+    for m in n_peers:
+        pl.semaphore_signal(barrier, inc=1, device_id=(m, w), device_id_type=MESH)
+    pl.semaphore_signal(barrier, inc=1, device_id=twin, device_id_type=MESH)
+    pl.semaphore_wait(barrier, len(z_peers) + len(n_peers) + 1)
+
+    def remote(src, dst, send, recv, peer):
+        return pltpu.make_async_remote_copy(
+            src_ref=src, dst_ref=dst, send_sem=send, recv_sem=recv, device_id=peer, device_id_type=MESH
+        )
+
+    own = [pltpu.make_async_copy(ins[i], outs[i].at[n, z, c], local.at[i]) for i in range(count)]
+    for i in range(count):
+        own[i].start()
+        for peer in z_peers:
+            remote(ins[i], outs[i].at[n, z, c], z_send.at[i], z_recv.at[i], peer).start()
+    for i in range(count):
+        own[i].wait()
+        part = outs[i].at[n, pl.ds(0, depth - 1), c]
+        remote(part, part, z_send.at[i], z_recv.at[i], twin).wait_recv()
+        mine = outs[i].at[n, :, c]
+        for m in n_peers:
+            remote(mine, mine, n_send.at[i], n_recv.at[i], (m, w)).start()
+        remote(mine, mine, c_send.at[i], c_recv.at[i], twin).start()
+    for i in range(count):
+        part = outs[i].at[pl.ds(0, narrow - 1), :, c]
+        remote(part, part, n_send.at[i], n_recv.at[i], twin).wait_recv()
+        for m in n_peers:
+            theirs = outs[i].at[m, :, c]
+            remote(theirs, theirs, c_send.at[i], c_recv.at[i], twin).start()
+    for i in range(count):
+        half = outs[i].at[:, :, 1 - c]
+        remote(half, half, c_send.at[i], c_recv.at[i], twin).wait()
+        part = outs[i].at[n, pl.ds(0, depth - 1), c]
+        remote(part, part, z_send.at[i], z_recv.at[i], twin).wait_send()
+        part = outs[i].at[pl.ds(0, narrow - 1), :, c]
+        remote(part, part, n_send.at[i], n_recv.at[i], twin).wait_send()
+
+
+def gather_all(arrays, collective_id):
+    narrow, wide = lax.axis_size("narrow"), lax.axis_size("wide")
+    count = len(arrays)
+    dma = pltpu.SemaphoreType.DMA((count,))
+    outs = pl.pallas_call(
+        partial(gather_kernel, count, narrow, wide // 2),
+        out_shape=[
+            jax.ShapeDtypeStruct((narrow, wide // 2, 2) + a.shape, a.dtype) for a in arrays
+        ],
+        in_specs=[pl.BlockSpec(memory_space=pl.ANY)] * count,
+        out_specs=[pl.BlockSpec(memory_space=pl.ANY)] * count,
+        scratch_shapes=[dma] * 7,
+        compiler_params=pltpu.CompilerParams(collective_id=collective_id, has_side_effects=True),
+        name="gather_all",
+    )(*arrays)
+    return [o.reshape((-1,) + a.shape[1:]) for o, a in zip(outs, arrays)]
+
+
+def exchange(blocks, axis):
+    return lax.all_to_all(blocks, axis, split_axis=0, concat_axis=0, tiled=True)
+
+
+def softplus(v):
+    return jnp.maximum(v, 0.0) + jnp.log1p(jnp.exp(-jnp.abs(v)))
+
+
+def convolved(window, marks, weight, bias):
+    pre = bias + weight[CONV - 1 :] * window[8:]
+    for lag in range(1, CONV):
+        pre = pre + weight[CONV - 1 - lag : CONV - lag] * (
+            window[8 - lag : 8 - lag + QUERY] * marks[:, lag : lag + 1]
+        )
+    return pre
+
+
+def decays(marks, dt, step_bias, rate_scale):
+    shape = (QUERY, QUERY)
+    row = lax.broadcasted_iota(jnp.int32, shape, 0)
+    column = lax.broadcasted_iota(jnp.int32, shape, 1)
+    lower = (row >= column).astype(FULL)
+    segment = jnp.broadcast_to(marks[:, :1], shape)
+    visible = (segment == segment.T) & (row >= column)
+    delta = jnp.broadcast_to(softplus(dt + step_bias), shape)
+    total = nn(lower, -delta * rate_scale, highest)
+    gap = jnp.where(visible, total - total.T, 0.0)
+    decay = jnp.where(visible, jnp.exp(gap), 0.0)
+    last = total[QUERY - 1 :, :]
+    begun = jnp.exp(total) * marks[:, 4:5]
+    tail = jnp.exp(last - total) * marks[:, 5:6]
+    kept = jnp.exp(last) * marks[:1, 6:7]
+    return lower, delta, decay, begun, tail, kept
+
+
+def mixer_forward_kernel(
+    numbers, xz, bc, dt, marks, wx, bx, wbc, bbc, u_out, y_out, states, xz_pad, bc_pad, state
+):
+    count = xz.shape[0]
+    xz_pad[pl.ds(0, 8), :] = jnp.zeros((8, xz_pad.shape[1]), FULL)
+    bc_pad[pl.ds(0, 8), :] = jnp.zeros((8, bc_pad.shape[1]), FULL)
+    state[...] = jnp.zeros_like(state)
+    step_bias, rate_scale, skip = numbers[0], numbers[1], numbers[2]
+
+    xz_pad[pl.ds(8, count), :] = xz[...].astype(FULL)
+    bc_pad[pl.ds(8, count), :] = bc[...].astype(FULL)
+
+    def block(i, carry):
+        start = pl.multiple_of(i * QUERY, QUERY)
+        rows = pl.ds(start, QUERY)
+        mark = marks[rows, :]
+        act_x = jax.nn.silu(convolved(xz_pad[pl.ds(start, QUERY + 8), :], mark, wx[...], bx[...]))
+        act = jax.nn.silu(convolved(bc_pad[pl.ds(start, QUERY + 8), :], mark, wbc[...], bbc[...]))
+        x, b, c = act_x[:, :HEAD_M], act[:, :STATE], act[:, STATE:]
+        lower, delta, decay, begun, tail, kept = decays(mark, dt[rows, :], step_bias, rate_scale)
+        weight = nt(c, b, highest) * decay * delta.T
+        held = state[...]
+        states[i] = held
+        y = (
+            nn(weight, x, highest)
+            + nt(c, held, highest) * begun[:, :HEAD_M]
+            + skip * x
+        )
+        state[...] = held * kept + tn(x * (tail * delta)[:, :HEAD_M], b, highest)
+        z = xz[rows, :].astype(FULL)[:, HEAD_M:]
+        y_out[rows, :] = y
+        u_out[rows, :] = y * jax.nn.silu(z)
+        return carry
+
+    lax.fori_loop(0, count // QUERY, block, 0)
+
+
+def mixer_backward_kernel(
+    numbers,
+    xz,
+    bc,
+    dt,
+    marks,
+    wx,
+    bx,
+    wbc,
+    bbc,
+    y_in,
+    states,
+    du_in,
+    dxz,
+    dbc,
+    ddt,
+    dwx,
+    dwbc,
+    dnumbers,
+    xz_pad,
+    bc_pad,
+    dx_pad,
+    dbc_pad,
+    dstate,
+):
+    count = xz.shape[0]
+    blocks = count // QUERY
+    xz_pad[pl.ds(0, 8), :] = jnp.zeros((8, xz_pad.shape[1]), FULL)
+    bc_pad[pl.ds(0, 8), :] = jnp.zeros((8, bc_pad.shape[1]), FULL)
+    dx_pad[pl.ds(count, 8), :] = jnp.zeros((8, dx_pad.shape[1]), FULL)
+    dbc_pad[pl.ds(count, 8), :] = jnp.zeros((8, dbc_pad.shape[1]), FULL)
+    dstate[...] = jnp.zeros_like(dstate)
+    dwx[...] = jnp.zeros_like(dwx)
+    dwbc[...] = jnp.zeros_like(dwbc)
+    dnumbers[...] = jnp.zeros_like(dnumbers)
+    step_bias, rate_scale, skip = numbers[0], numbers[1], numbers[2]
+
+    def fill(i, carry):
+        start = pl.multiple_of(i * QUERY, QUERY)
+        rows = pl.ds(start, QUERY)
+        xz_pad[pl.ds(start + 8, QUERY), :] = xz[rows, :].astype(FULL)
+        bc_pad[pl.ds(start + 8, QUERY), :] = bc[rows, :].astype(FULL)
+        return carry
+
+    lax.fori_loop(0, blocks, fill, 0)
+
+    def slope(pre):
+        s = jax.nn.sigmoid(pre)
+        return s * (1.0 + pre * (1.0 - s))
+
+    def total(v):
+        return jnp.sum(jnp.sum(v, axis=1, keepdims=True), axis=0, keepdims=True)
+
+    def conv_back(pad, start, dpre_pad, dpre, weight, dw):
+        mark = marks[pl.ds(start, QUERY), :]
+        window = pad[pl.ds(start, QUERY + 8), :]
+        later = dpre_pad[pl.ds(start, QUERY + 8), :]
+        later_marks = marks[pl.ds(start, QUERY + 8), :]
+        out = weight[CONV - 1 :] * dpre
+        dw[CONV - 1 : CONV, :] += jnp.sum(dpre * window[8:], axis=0, keepdims=True)
+        dw[CONV : CONV + 1, :] += jnp.sum(dpre, axis=0, keepdims=True)
+        for lag in range(1, CONV):
+            tap = CONV - 1 - lag
+            out = out + weight[tap : tap + 1] * (
+                (later * later_marks[:, lag : lag + 1])[lag : lag + QUERY]
+            )
+            dw[tap : tap + 1, :] += jnp.sum(
+                dpre * (window[8 - lag : 8 - lag + QUERY] * mark[:, lag : lag + 1]),
+                axis=0,
+                keepdims=True,
+            )
+        return out
+
+    def block(k, carry):
+        i = blocks - 1 - k
+        start = pl.multiple_of(i * QUERY, QUERY)
+        rows = pl.ds(start, QUERY)
+        mark = marks[rows, :]
+        pre_x = convolved(xz_pad[pl.ds(start, QUERY + 8), :], mark, wx[...], bx[...])
+        pre = convolved(bc_pad[pl.ds(start, QUERY + 8), :], mark, wbc[...], bbc[...])
+        act = jax.nn.silu(pre)
+        x, b, c = jax.nn.silu(pre_x)[:, :HEAD_M], act[:, :STATE], act[:, STATE:]
+        step = dt[rows, :]
+        lower, delta, decay, begun, tail, kept = decays(mark, step, step_bias, rate_scale)
+        held, dheld = states[i], dstate[...]
+        z = xz[rows, :].astype(FULL)[:, HEAD_M:]
+        du, y = du_in[rows, :].astype(FULL), y_in[rows, :]
+        dy = du * jax.nn.silu(z)
+        dz = du * y * slope(z)
+        scores = nt(c, b, highest)
+        reach = decay * delta.T
+        dweight = nt(dy, x, highest)
+        dscores = dweight * reach
+        fed = x * (tail * delta)[:, :HEAD_M]
+        begun_dy = dy * begun[:, :HEAD_M]
+        dc = nn(dscores, b, highest) + nn(begun_dy, held, highest)
+        db = tn(dscores, c, highest) + nn(fed, dheld, highest)
+        dfed = nt(b, dheld, highest)
+        dx = skip * dy + tn(scores * reach, dy, highest) + (tail * delta)[:, :HEAD_M] * dfed
+        moved = dweight * scores * decay
+        turned = moved.T
+        ddelta = jnp.sum(turned, axis=1, keepdims=True)
+        dtotal = jnp.sum(moved * delta.T, axis=1, keepdims=True) - ddelta * delta[:, :1]
+        dtotal += jnp.sum(begun_dy * nt(c, held, highest), axis=1, keepdims=True)
+        dtail = jnp.sum(dfed * x, axis=1, keepdims=True)
+        ddelta += dtail * tail[:, :1]
+        dtail = dtail * (tail * delta)[:, :1]
+        dtotal -= dtail
+        dlast = jnp.sum(dtail, axis=0, keepdims=True) + total(dheld * held * kept)
+        dlog = tn(lower, jnp.broadcast_to(dtotal, (QUERY, QUERY)), highest)[:, :1] + dlast
+        ddelta -= dlog * rate_scale
+        dstep = ddelta * jax.nn.sigmoid(step + step_bias)
+        ddt[rows, :] = dstep
+        dnumbers[0:1, :] += jnp.broadcast_to(jnp.sum(dstep, axis=0, keepdims=True), (1, 128))
+        dnumbers[1:2, :] -= jnp.broadcast_to(
+            jnp.sum(dlog * delta[:, :1] * rate_scale, axis=0, keepdims=True), (1, 128)
+        )
+        dnumbers[2:3, :] += jnp.broadcast_to(total(dy * x), (1, 128))
+        dstate[...] = dheld * kept + tn(begun_dy, c, highest)
+        dpre_x = jnp.concatenate([dx, jnp.zeros_like(dx)], axis=1) * slope(pre_x)
+        dpre = jnp.concatenate([db, dc], axis=1) * slope(pre)
+        dx_pad[rows, :] = dpre_x
+        dbc_pad[rows, :] = dpre
+        dxr = conv_back(xz_pad, start, dx_pad, dpre_x, wx[...], dwx)
+        dxz[rows, :] = jnp.concatenate([dxr[:, :HEAD_M], dz], axis=1).astype(dxz.dtype)
+        dbc[rows, :] = conv_back(bc_pad, start, dbc_pad, dpre, wbc[...], dwbc).astype(dbc.dtype)
+        return carry
+
+    lax.fori_loop(0, blocks, block, 0)
+
+
+def in_smem():
+    return pl.BlockSpec(memory_space=pltpu.SMEM)
+
+
+def in_vmem():
+    return pl.BlockSpec(memory_space=pltpu.VMEM)
+
+
+def mixer_forward(numbers, xz, bc, dt, marks, wx, bx, wbc, bbc):
+    count = xz.shape[0]
+    return pl.pallas_call(
+        mixer_forward_kernel,
+        out_shape=[
+            jax.ShapeDtypeStruct((count, HEAD_M), FULL),
+            jax.ShapeDtypeStruct((count, HEAD_M), FULL),
+            jax.ShapeDtypeStruct((count // QUERY, HEAD_M, STATE), FULL),
+        ],
+        in_specs=[in_smem()] + [in_vmem()] * 8,
+        out_specs=[in_vmem()] * 3,
+        scratch_shapes=[
+            pltpu.VMEM((count + 8, 2 * HEAD_M), FULL),
+            pltpu.VMEM((count + 8, 2 * STATE), FULL),
+            pltpu.VMEM((HEAD_M, STATE), FULL),
+        ],
+        compiler_params=pltpu.CompilerParams(vmem_limit_bytes=32 << 20),
+        name="mixer_forward",
+    )(numbers, xz, bc, dt, marks, wx, bx, wbc, bbc)
+
+
+def mixer_backward(numbers, xz, bc, dt, marks, wx, bx, wbc, bbc, y, states, du):
+    count = xz.shape[0]
+    return pl.pallas_call(
+        mixer_backward_kernel,
+        out_shape=[
+            jax.ShapeDtypeStruct((count, 2 * HEAD_M), LOW),
+            jax.ShapeDtypeStruct((count, 2 * STATE), LOW),
+            jax.ShapeDtypeStruct((count, 1), FULL),
+            jax.ShapeDtypeStruct((8, 2 * HEAD_M), FULL),
+            jax.ShapeDtypeStruct((8, 2 * STATE), FULL),
+            jax.ShapeDtypeStruct((8, 128), FULL),
+        ],
+        in_specs=[in_smem()] + [in_vmem()] * 11,
+        out_specs=[in_vmem()] * 6,
+        scratch_shapes=[
+            pltpu.VMEM((count + 8, 2 * HEAD_M), FULL),
+            pltpu.VMEM((count + 8, 2 * STATE), FULL),
+            pltpu.VMEM((count + 8, 2 * HEAD_M), FULL),
+            pltpu.VMEM((count + 8, 2 * STATE), FULL),
+            pltpu.VMEM((HEAD_M, STATE), FULL),
+        ],
+        compiler_params=pltpu.CompilerParams(vmem_limit_bytes=32 << 20),
+        name="mixer_backward",
+    )(numbers, xz, bc, dt, marks, wx, bx, wbc, bbc, y, states, du)
+
+
+def patch_causal():
+    row = lax.broadcasted_iota(jnp.int32, (BYTE_BLOCK, BYTE_BLOCK), 0)
+    column = lax.broadcasted_iota(jnp.int32, (BYTE_BLOCK, BYTE_BLOCK), 1)
+    return (lax.div(row, PATCH) == lax.div(column, PATCH)) & (row >= column)
+
+
+def head_probs(q, k, causal):
+    scores = jnp.where(causal, nt(q, k) * HEAD_A ** (-0.5), masked_score)
+    grown = jnp.exp(scores - jnp.max(scores, axis=1, keepdims=True))
+    return grown / jnp.sum(grown, axis=1, keepdims=True)
+
+
+def of_head(block, half):
+    lane = lax.broadcasted_iota(jnp.int32, block.shape, 1)
+    return jnp.where(lax.div(lane, HEAD_A) == half, block, jnp.zeros_like(block))
+
+
+def attend_kernel(q_ref, k_ref, v_ref, out):
+    causal = patch_causal()
+    for first in range(0, q_ref.shape[0], BYTE_BLOCK):
+        rows = pl.ds(first, BYTE_BLOCK)
+        q, k, v = q_ref[rows, :], k_ref[rows, :], v_ref[rows, :]
+        mixed = jnp.zeros(q.shape, FULL)
+        for half in range(2):
+            probs = head_probs(of_head(q, half), k, causal)
+            mixed += nn(probs.astype(LOW), of_head(v, half))
+        out[rows, :] = mixed.astype(LOW)
+
+
+def attend_back_kernel(q_ref, k_ref, v_ref, g_ref, dq_out, dk_out, dv_out):
+    causal = patch_causal()
+    scale = HEAD_A ** (-0.5)
+    for first in range(0, q_ref.shape[0], BYTE_BLOCK):
+        rows = pl.ds(first, BYTE_BLOCK)
+        q, k, v, g = q_ref[rows, :], k_ref[rows, :], v_ref[rows, :], g_ref[rows, :]
+        dq = jnp.zeros(q.shape, FULL)
+        dk = jnp.zeros(q.shape, FULL)
+        dv = jnp.zeros(q.shape, FULL)
+        for half in range(2):
+            own_q, own_k, own_g = of_head(q, half), of_head(k, half), of_head(g, half)
+            probs = head_probs(own_q, k, causal)
+            dprobs = nt(own_g, v)
+            dv += tn(probs.astype(LOW), own_g)
+            dscores = probs * (dprobs - jnp.sum(probs * dprobs, axis=1, keepdims=True))
+            dscores = dscores.astype(LOW)
+            dq += nn(dscores, own_k)
+            dk += tn(dscores, own_q)
+        dq_out[rows, :] = (dq * scale).astype(LOW)
+        dk_out[rows, :] = (dk * scale).astype(LOW)
+        dv_out[rows, :] = dv.astype(LOW)
+
+
+def attend_heads(qkv):
+    rows = qkv.shape[0]
+    pairs = HEADS_A // 2
+
+    def spec(offset):
+        return pl.BlockSpec((rows, 2 * HEAD_A), lambda i: (0, i + offset))
+
+    return pl.pallas_call(
+        attend_kernel,
+        grid=(pairs,),
+        out_shape=jax.ShapeDtypeStruct((rows, D), LOW),
+        in_specs=[spec(0), spec(pairs), spec(2 * pairs)],
+        out_specs=spec(0),
+        name="attend",
+    )(qkv, qkv, qkv)
+
+
+def attend_heads_back(qkv, heads_grad):
+    rows = qkv.shape[0]
+    pairs = HEADS_A // 2
+
+    def spec(offset):
+        return pl.BlockSpec((rows, 2 * HEAD_A), lambda i: (0, i + offset))
+
+    return pl.pallas_call(
+        attend_back_kernel,
+        grid=(pairs,),
+        out_shape=[jax.ShapeDtypeStruct((rows, D), LOW)] * 3,
+        in_specs=[spec(0), spec(pairs), spec(2 * pairs), spec(0)],
+        out_specs=[spec(0)] * 3,
+        name="attend_back",
+    )(qkv, qkv, qkv, heads_grad)
+
+
+def per_device_heads(
+    byte_ids,
+    doc_patches,
+    pad_bytes,
+    byte_table,
+    patch_weight,
+    gain_mix,
+    in_weight,
+    conv_weight,
+    conv_bias,
+    step_bias,
+    log_rate,
+    skip_gain,
+    gated_gain,
+    out_weight,
+    local_weight,
+    gain_attn,
+    query_weight,
+    key_weight,
+    value_weight,
+    attn_weight,
+    feed_gain,
+    gate_weight,
+    up_weight,
+    down_weight,
+    cotangent,
+):
+    narrow, wide = lax.axis_size("narrow"), lax.axis_size("wide")
+    devices = narrow * wide
+    device = lax.axis_index(BOTH)
+    rows = byte_ids.shape[0]
+    patches = rows // PATCH
+    everything = devices * patches
+    own_rows = patch_weight.shape[0]
+    hidden_width = gate_weight.shape[1]
+    share = hidden_width // narrow
+
+    segment, _, keep_all = patch_layout(doc_patches, pad_bytes, 0, everything)
+    keep_all = keep_all.reshape(everything, PATCH)
+    place = jnp.arange(everything)
+    mark_columns = [segment.astype(FULL)]
+    for lag in range(1, CONV):
+        earlier = jnp.concatenate([jnp.full((lag,), -1, jnp.int32), segment[:-lag]])
+        mark_columns.append((earlier == segment).astype(FULL))
+    by_block = segment.reshape(-1, QUERY)
+    before = jnp.concatenate([jnp.full((1,), -1, jnp.int32), by_block[:-1, -1]])
+    mark_columns.append((by_block == before[:, None]).astype(FULL).reshape(-1))
+    mark_columns.append((by_block == by_block[:, -1:]).astype(FULL).reshape(-1))
+    mark_columns.append(
+        jnp.broadcast_to((by_block[:, -1:] == before[:, None]).astype(FULL), by_block.shape).reshape(-1)
+    )
+    mark_columns.append(jnp.zeros((everything,), FULL))
+    marks = jnp.pad(jnp.stack(mark_columns, axis=1), ((0, 8), (0, 0)))
+    keep_rows = lax.dynamic_slice_in_dim(keep_all, device * patches, patches).reshape(-1)
+
+    ids_low = byte_ids.astype(LOW).reshape(patches, PATCH)
+    bcdt_width = 2 * STATE + HEADS_M
+    start_pack = jnp.concatenate(
+        [
+            patch_weight,
+            jnp.pad(in_weight[:, 2 * DI :], ((0, 0), (0, 96))),
+            jnp.pad(ids_low, ((0, 0), (0, 120))),
+        ],
+        axis=1,
+    )
+    xz_blocks = jnp.concatenate(
+        [
+            in_weight[:, DI : 2 * DI].reshape(own_rows, HEADS_M, HEAD_M),
+            in_weight[:, :DI].reshape(own_rows, HEADS_M, HEAD_M),
+        ],
+        axis=2,
+    ).transpose(1, 0, 2)
+    xz_weight = exchange(xz_blocks, BOTH).reshape(D, 2 * HEAD_M)
+    start_all, table_all = gather_all([start_pack, byte_table], 0)
+    middle_pack = jnp.concatenate(
+        [
+            query_weight,
+            key_weight,
+            value_weight,
+            attn_weight,
+            out_weight[:own_rows],
+            out_weight[own_rows:],
+            local_weight.T,
+        ],
+        axis=1,
+    )
+    middle_all = lax.all_gather(middle_pack, BOTH, axis=0, tiled=True)
+    feed_blocks = jnp.stack(
+        [
+            gate_weight.T.reshape(narrow, share, -1),
+            up_weight.T.reshape(narrow, share, -1),
+            down_weight.reshape(narrow, share, -1),
+        ],
+        axis=1,
+    )
+    feed_turned = exchange(feed_blocks, "narrow").transpose(1, 2, 0, 3).reshape(3, share, D)
+    feed_all = lax.all_gather(feed_turned, "wide")
+    in_all = lax.all_gather(in_weight, BOTH, axis=0, tiled=True)
+
+    patch_all = start_all[:, :D]
+    bcdt_weight = start_all[:, D : D + bcdt_width]
+    ids_all = start_all[:, D + 384 : D + 384 + PATCH].astype(jnp.int32)
+
+    vocabulary = jnp.arange(VOCAB, dtype=jnp.int32)
+    onehot = (ids_all[:, :, None] == vocabulary).astype(LOW) * keep_all[:, :, None].astype(LOW)
+    embedded = (
+        jnp.dot(onehot.reshape(everything * PATCH, VOCAB), table_all, preferred_element_type=FULL)
+        .astype(LOW)
+        .reshape(everything, D)
+    )
+    mixed_all = jnp.dot(embedded, patch_all, preferred_element_type=FULL)
+    normed_all = root_norm(mixed_all, gain_mix).astype(LOW)
+    xz = jnp.dot(normed_all, xz_weight, preferred_element_type=FULL).astype(LOW)
+    bcdt = jnp.dot(normed_all, bcdt_weight, preferred_element_type=FULL).astype(LOW)
+    bc = bcdt[:, : 2 * STATE]
+    dt = lax.dynamic_slice_in_dim(bcdt[:, 2 * STATE :], device, 1, axis=1).astype(FULL)
+    mixed_in = lax.dynamic_slice_in_dim(mixed_all, device * patches, patches)
+
+    conv_x = lax.dynamic_slice_in_dim(conv_weight, device * HEAD_M, HEAD_M, axis=1)
+    bias_x = lax.dynamic_slice_in_dim(conv_bias, device * HEAD_M, HEAD_M)[None]
+    conv_x = jnp.pad(conv_x, ((0, 0), (0, HEAD_M)))
+    bias_x = jnp.pad(bias_x, ((0, 0), (0, HEAD_M)))
+    conv_bc = conv_weight[:, DI:]
+    bias_bc = conv_bias[None, DI:]
+
+    def own(values):
+        return lax.dynamic_index_in_dim(values, device, 0, False)
+
+    numbers = jnp.stack([own(step_bias), jnp.exp(own(log_rate)), own(skip_gain)])
+    mixer_args = (numbers, xz, bc, dt, marks, conv_x, bias_x, conv_bc, bias_bc)
+    u, y, states = mixer_forward(*mixer_args)
+    u_blocks = exchange(u.astype(LOW).reshape(devices, patches, HEAD_M), BOTH)
+    gated_rows = u_blocks.transpose(1, 0, 2).reshape(patches, DI).astype(FULL)
+    gated_scale = lax.rsqrt(jnp.mean(gated_rows * gated_rows, axis=-1, keepdims=True) + epsilon)
+    gated_low = (gated_rows * gated_scale * gated_gain).astype(LOW)
+
+    out_all = (
+        middle_all[:, 4 * D : 6 * D]
+        .reshape(devices, own_rows, 2, D)
+        .transpose(0, 2, 1, 3)
+        .reshape(DI, D)
+    )
+    local_all = middle_all[:, 6 * D :]
+    qkv_all = middle_all[:, : 3 * D]
+    attn_all = middle_all[:, 3 * D : 4 * D]
+    global_out = mixed_in + jnp.dot(gated_low, out_all, preferred_element_type=FULL)
+
+    local_rows = global_out.astype(LOW).reshape(rows, EMB)
+    stream = nt(local_rows, local_all)
+    normed_attn = root_norm(stream, gain_attn).astype(LOW)
+    qkv = jnp.dot(normed_attn, qkv_all, preferred_element_type=FULL).astype(LOW)
+    mixed_heads = attend_heads(qkv)
+    after_attn = stream + jnp.dot(mixed_heads, attn_all, preferred_element_type=FULL)
+    normed_feed = root_norm(after_attn, feed_gain).astype(LOW)
+    out_grad = cotangent.astype(FULL) * keep_rows[:, None]
+    feed_grad = out_grad.astype(LOW)
+
+    feed_width = wide * share
+    gate_up_all = feed_all[:, :2].reshape(wide, 2, share, D).transpose(1, 0, 2, 3)
+    gate_up_all = gate_up_all.reshape(2 * feed_width, D)
+    down_all = feed_all[:, 2].reshape(feed_width, D)
+
+    def over_narrow(values):
+        spread_out = jnp.broadcast_to(values[None], (narrow,) + values.shape)
+        return exchange(spread_out, "narrow").reshape((-1,) + values.shape[1:])
+
+    def back_over_narrow(values):
+        blocks = exchange(values.astype(LOW).reshape(narrow, rows, D), "narrow")
+        return jnp.sum(blocks.astype(FULL), axis=0)
+
+    grid_grad = over_narrow(feed_grad)
+    grid_in = over_narrow(normed_feed)
+    gate_up = nt(grid_in, gate_up_all)
+    gate, up = gate_up[:, :feed_width], gate_up[:, feed_width:]
+    hidden = (jax.nn.silu(gate) * up).astype(LOW)
+    feed_out = back_over_narrow(nn(hidden, down_all))
+    hidden_grad = nt(grid_grad, down_all)
+    gate_up_grad = silu_back(gate_up, hidden_grad, feed_width).astype(LOW)
+    grad_gate_up = tn(gate_up_grad, grid_in).reshape(2, wide, share, D)
+    grad_down_part = tn(hidden, grid_grad).reshape(1, wide, share, D)
+    feed_in_grad = back_over_narrow(nn(gate_up_grad, gate_up_all))
+    feed_grads = jnp.concatenate([grad_gate_up, grad_down_part]).transpose(1, 0, 2, 3).astype(LOW)
+    feed_sums = lax.psum_scatter(
+        feed_grads.reshape(-1, D), "wide", scatter_dimension=0, tiled=True
+    )
+    feed_sums = feed_sums.reshape(3, share, narrow, D // narrow).transpose(2, 0, 1, 3)
+    feed_sums = exchange(feed_sums, "narrow").transpose(1, 0, 2, 3).astype(FULL)
+    feed_sums = feed_sums.reshape(3, hidden_width, D // narrow)
+    grad_gate, grad_up, grad_down = feed_sums[0].T, feed_sums[1].T, feed_sums[2]
+    out_rows = ((after_attn + feed_out.astype(LOW).astype(FULL)) * keep_rows[:, None]).astype(LOW)
+
+    _, feed_norm_back = jax.vjp(root_norm, after_attn, feed_gain)
+    after_norm_grad, grad_feed_gain = feed_norm_back(feed_in_grad.astype(LOW).astype(FULL))
+    after_grad = out_grad + after_norm_grad
+    attn_grad = after_grad.astype(LOW)
+    heads_grad = nt(attn_grad, attn_all).astype(LOW)
+    query_grad, key_grad, value_grad = attend_heads_back(qkv, heads_grad)
+    qkv_grad = jnp.concatenate([query_grad, key_grad, value_grad], axis=1)
+    normed_grad = nt(qkv_grad, qkv_all)
+    _, attn_norm_back = jax.vjp(root_norm, stream, gain_attn)
+    stream_norm_grad, grad_gain_attn = attn_norm_back(normed_grad)
+    stream_grad = (after_grad + stream_norm_grad).astype(LOW)
+    middle_grads = jnp.concatenate(
+        [tn(normed_attn, qkv_grad), tn(mixed_heads, attn_grad), tn(stream_grad, local_rows)], axis=1
+    ).astype(LOW)
+    middle_sums = lax.psum_scatter(middle_grads, BOTH, scatter_dimension=0, tiled=True).astype(FULL)
+    global_grad = nn(stream_grad, local_all).reshape(patches, D)
+
+    mix_grad = global_grad.astype(LOW)
+    gated_grad = nt(mix_grad, out_all)
+    _, gated_back = jax.vjp(root_norm, gated_rows, gated_gain)
+    gated_rows_grad, grad_gated_gain = gated_back(gated_grad)
+    du_blocks = gated_rows_grad.astype(LOW).reshape(patches, devices, HEAD_M).transpose(1, 0, 2)
+    du = exchange(du_blocks, BOTH).reshape(everything, HEAD_M)
+    dxz, dbc, ddt, dwx, dwbc, dnumbers = mixer_backward(*mixer_args, y, states, du)
+    grad_xz = tn(normed_all, dxz).astype(LOW).reshape(devices, own_rows, 2 * HEAD_M)
+    grad_xz = exchange(grad_xz, BOTH).astype(FULL).transpose(1, 0, 2)
+    proj_blocks = jnp.concatenate(
+        [dxz, dbc, jnp.pad(ddt.astype(LOW), ((0, 0), (0, 127)))], axis=1
+    ).reshape(devices, patches, 4 * STATE)
+    proj_blocks = exchange(proj_blocks, BOTH)
+    xz_grad = proj_blocks[:, :, :STATE].transpose(1, 0, 2)
+    bc_grad = jnp.sum(proj_blocks[:, :, STATE : 3 * STATE].astype(FULL), axis=0).astype(LOW)
+    bcdt_grad = jnp.concatenate([bc_grad, proj_blocks[:, :, 3 * STATE].T], axis=1)
+    proj_low = jnp.concatenate(
+        [
+            xz_grad[:, :, HEAD_M:].reshape(patches, DI),
+            xz_grad[:, :, :HEAD_M].reshape(patches, DI),
+            bcdt_grad,
+        ],
+        axis=1,
+    )
+    normed_mix_grad = nt(proj_low, in_all)
+    _, mix_norm_back = jax.vjp(root_norm, mixed_in, gain_mix)
+    mixed_norm_grad, grad_gain_mix = mix_norm_back(normed_mix_grad)
+    embed_grad = (global_grad + mixed_norm_grad).astype(LOW)
+
+    end_pack = jnp.concatenate(
+        [
+            embed_grad,
+            mix_grad,
+            jnp.pad(bcdt_grad, ((0, 0), (0, 96))),
+            jnp.broadcast_to(gated_scale.astype(LOW), (patches, 128)),
+        ],
+        axis=1,
+    )
+    (end_all,) = gather_all([end_pack], 1)
+    embed_grad_all = end_all[:, :D]
+    mix_grad_all = end_all[:, D : 2 * D]
+    bcdt_grad_all = end_all[:, 2 * D : 2 * D + bcdt_width]
+    scale_all = end_all[:, 2 * D + 384 : 2 * D + 385].astype(FULL)
+    gain_own = lax.dynamic_slice_in_dim(gated_gain, device * HEAD_M, HEAD_M)
+    grad_out = tn((u * scale_all * gain_own).astype(LOW), mix_grad_all)
+    normed_own = lax.dynamic_slice_in_dim(normed_all, device * own_rows, own_rows, axis=1)
+    grad_bcdt = tn(normed_own, bcdt_grad_all)
+    grad_in = jnp.concatenate(
+        [
+            grad_xz[:, :, HEAD_M:].reshape(own_rows, DI),
+            grad_xz[:, :, :HEAD_M].reshape(own_rows, DI),
+            grad_bcdt,
+        ],
+        axis=1,
+    )
+    embedded_own = lax.dynamic_slice_in_dim(embedded, device * own_rows, own_rows, axis=1)
+    grad_patch = tn(embedded_own, embed_grad_all)
+    own_words = byte_table.shape[0]
+    words = device * own_words + jnp.arange(own_words, dtype=jnp.int32)
+    chosen = (ids_all[:, :, None] == words).astype(LOW) * keep_all[:, :, None].astype(LOW)
+    word_sums = tn(chosen.reshape(everything, PATCH * own_words), embed_grad_all)
+    grad_table = jnp.einsum(
+        "kvd,ked->ve",
+        word_sums.reshape(PATCH, own_words, D),
+        patch_all.astype(FULL).reshape(PATCH, EMB, D),
+        precision=highest,
+    )
+
+    conv_grads = jnp.zeros((CONV + 1, DI + 2 * STATE), FULL)
+    conv_grads = lax.dynamic_update_slice(
+        conv_grads, dwx[: CONV + 1, :HEAD_M], (0, device * HEAD_M)
+    )
+    conv_grads = lax.dynamic_update_slice(conv_grads, dwbc[: CONV + 1], (0, DI))
+    number_grads = jnp.where(
+        jnp.arange(HEADS_M)[None, :] == device, dnumbers[:3, :1], 0.0
+    )
+    small = lax.psum(
+        (conv_grads, number_grads, grad_gain_mix, grad_gated_gain, grad_gain_attn, grad_feed_gain),
+        BOTH,
+    )
+    conv_grads, number_grads = small[:2]
+    return (
+        out_rows,
+        grad_table,
+        grad_patch,
+        small[2],
+        grad_in,
+        conv_grads[:CONV],
+        conv_grads[CONV],
+        number_grads[0],
+        number_grads[1],
+        number_grads[2],
+        small[3],
+        grad_out,
+        middle_sums[:, 4 * D :].T,
+        small[4],
+        middle_sums[:, :D],
+        middle_sums[:, D : 2 * D],
+        middle_sums[:, 2 * D : 3 * D],
+        middle_sums[:, 3 * D : 4 * D],
+        small[5],
+        grad_gate,
+        grad_up,
+        grad_down,
+    )
+
+
 def solution(mesh):
     placed = (
         P(("narrow", "wide")),
@@ -539,7 +1301,7 @@
         P(("narrow", "wide"), None),
     )
     return jax.shard_map(
-        per_device,
+        per_device_heads if mesh.size == HEADS_M else per_device_rows,
         mesh=mesh,
         in_specs=placed,
         out_specs=(

time: 3040 us -> 793 us (0.26)
  waiting for transfers between devices: 2470 us -> 258 us
  Pallas kernels: 0 us -> 153 us
  blocking collectives: 145 us -> 29.3 us
  other arithmetic: 131 us -> 41.4 us
  matrix products: 168 us -> 118 us
  local copies, waits for them, and re-layouts: 75.3 us -> 119 us
    reduce_scatter x10 -> x2, waiting for transfers between devices: 1280 us -> 132 us  [the longest x1 132 us: per_device_heads(): lax.psum_scatter(middle_grads, BOTH, scatter_dimension=0, tiled=True)]
    psum x2 -> x1, waiting for transfers between devices: 583 us -> 28.4 us  [per_device_heads(): lax.psum((conv_grads, number_grads, grad_gain_mix, grad_gated_gain, grad_...]
    all_gather x11 -> x3, waiting for transfers between devices: 530 us -> 0.04 us  [the longest x1 0.02 us: per_device_heads(): in_all = lax.all_gather(in_weight, BOTH, axis=0, tiled=True)]
    pallas_call x0 -> x6, Pallas kernels: none -> 153 us  [the longest x2 110 us: gather_all(): pl.pallas_call(partial(gather_kernel, count, narrow, wide // 2), out_shap...]
    all_gather x3 -> x0, blocking collectives: 124 us -> none  [the longest x1 48.4 us: per_device(): lax.all_gather(local_weight, ('narrow', 'wide'), axis=1, tiled=True)]
    all_to_all x2 -> x9, waiting for transfers between devices: 3.93 us -> 96.5 us  [exchange(): return lax.all_to_all(blocks, axis, split_axis=0, concat_axis=0, tiled=True)]
    unnamed x25 -> x6, waiting for transfers between devices: 70.8 us -> 0.76 us
    dot_general x49 -> x28, matrix products: 163 us -> 118 us  [the longest x7 41.1 us: nt(): lax.dot_general(a, b, (((1,), (1,)), ((), ())), precision=precision, pref...]
  transfers between devices with their start and end apart: 28 -> 15, of which waited for: 25 -> 9; matrix products, arithmetic and copies ran while one was open for 5% -> 32% of each run, Pallas kernels for 0% -> 20%
where the time goes in v1:
time: 793 us; the launch traced here: 778 us
  waiting for transfers between devices  258 us (33%)
  Pallas kernels  153 us (19%)
  local copies, waits for them, and re-layouts  119 us (15%)
  matrix products  118 us (15%)
  starting transfers between devices  44.3 us (6%)
  other arithmetic  41.4 us (5%)
  blocking collectives  29.3 us (4%)
  between operations  16.1 us (2%)
    reduce_scatter x1, waiting for transfers between devices, per_device_heads(): lax.psum_scatter(middle_grads, BOTH, scatter_dimension=0, tiled=True)  132 us
    pallas_call x2, Pallas kernels, gather_all(): pl.pallas_call(partial(gather_kernel, count, narrow, wide // 2), out_shap...  110 us
    all_to_all x9, waiting for transfers between devices, exchange(): return lax.all_to_all(blocks, axis, split_axis=0, concat_axis=0, tiled=True)  96.5 us
    all_to_all x9, starting transfers between devices, exchange(): return lax.all_to_all(blocks, axis, split_axis=0, concat_axis=0, tiled=True)  43.4 us
    dot_general x7, matrix products, nt(): lax.dot_general(a, b, (((1,), (1,)), ((), ())), precision=precision, pref...  41.1 us
    unnamed x147, local copies, waits for them, and re-layouts  32.7 us
    dot_general x10, matrix products, tn(): lax.dot_general(a, b, (((0,), (0,)), ((), ())), precision=precision, pref...  29.3 us
    all_to_all x2, blocking collectives, exchange(): return lax.all_to_all(blocks, axis, split_axis=0, concat_axis=0, tiled=True)  29.3 us
  transfers between devices with their start and end apart: 15, of which 9 were waited for; matrix products, arithmetic and copies ran while one was open for 32% of the time, Pallas kernels for 20%

profile of v1, /device:TPU:9, one launch (start us, length us, event | category | flops | bytes accessed | tf_op | source)
XLA Modules:
  0.0 778.3 jit_solution(10767279412679231595)
XLA Ops:
  17.2 16.1 %all_to_all.55 = bf16[4,3,128,256]{3,2,1,0:T(8,128)(2,1)S(1)} all-to-all(bf16[4,3,128,256]{3,2,1,0:T(8,128)(2,1)S(1)} %copy.219), channel_id=1, replica_groups=mesh['narrow'=4,'wide'=8] {'narrow'}, dimensions={0} | all-to-all | bytes 1572864 | tf_op jit(solution)/shard_map/all_to_all | solution.py:617
  37.1 6.4 all-to-all-start
  46.1 56.9 %gather_all.2 = (bf16[4,4,2,32,1536]{4,3,2,1,0:T(8,128)(2,1)}, bf16[4,4,2,8,128]{4,3,2,1,0:T(8,128)(2,1)}) custom-call(bf16[32,1536]{1,0:T(8,128)(2,1)} %fusion.80.refs_0_, bf16[8,128]{1,0:T(8,128)(2,1)} %refs_1_.1), custom_call_target="tpu_custom_call" | custom-call | tf_op jit(solution)/shard_map/gather_all/pallas_call | solution.py:602
  104.3 6.0 convolution_convert_fusion
  113.3 4.6 multiply_reduce_fusion
  118.7 3.2 convolution_convert_fusion.5
  131.8 7.3 mixer_forward.1
  140.0 4.6 all-to-all-start.1
  148.6 5.2 all-to-all-done.1
  158.0 4.7 slice.219
  162.7 7.9 %reshape.443 = bf16[32,32,2,1024]{3,2,1,0:T(2,128)(2,1)} reshape(bf16[1024,2048]{1,0:T(8,128)(2,1)} %slice.219) | data formatting | bytes 8388608 | tf_op jit(solution)/shard_map/reshape | solution.py:1098
  170.6 3.7 copy.216
  180.9 5.9 fusion.7.q_ref.k_ref.v_ref
  186.8 8.7 %attend.1 = bf16[256,1024]{1,0:T(8,128)(2,1)} custom-call(bf16[256,3072]{1,0:T(8,128)(2,1)} %fusion.7.q_ref.k_ref.v_ref, bf16[256,3072]{1,0:T(8,128)(2,1)} %fusion.7.q_ref.k_ref.v_ref, bf16[256,3072]{1,0:T(8,128)(2,1)} %fusion.7.q_ref.k_ref.v_ref), custom_call_target="tpu_custom_call" | custom-call | tf_op jit(solution)/shard_map/attend/pallas_call | solution.py:933
  201.2 4.5 all-to-all-start.2
  208.5 23.8 %all-to-all-done.2 = bf16[4,256,1024]{2,1,0:T(8,128)(2,1)} async-done(((bf16[4,256,1024]{2,1,0:T(8,128)(2,1)}), bf16[4,256,1024]{2,1,0:T(8,128)(2,1)}, u32[]{:S(2)}, u32[]{:S(2)}) %all-to-all-start.2) | async-done | bytes 2097184 | tf_op jit(solution)/shard_map/all_to_all | solution.py:617
  235.0 4.4 all-to-all-start.5
  246.6 8.4 %fusion.111 = f32[1024,2048]{1,0:T(8,128)} fusion(bf16[1024,1024]{1,0:T(8,128)(2,1)} %bitcast.20, bf16[2048,1024]{1,0:T(8,128)(2,1)S(1)} %bitcast.171), kind=kOutput, calls=%fused_computation.221 | convolution fusion | flops 4294967296 | bytes 14680064 | tf_op jit(solution)/shard_map/dot_general | solution.py:538
  255.1 17.9 %all-to-all-done.5 = bf16[4,256,1024]{2,1,0:T(8,128)(2,1)} async-done(((bf16[4,256,1024]{2,1,0:T(8,128)(2,1)}), bf16[4,256,1024]{2,1,0:T(8,128)(2,1)}, u32[]{:S(2)}, u32[]{:S(2)}) %all-to-all-start.5) | async-done | bytes 2097184 | tf_op jit(solution)/shard_map/all_to_all | solution.py:617
  272.9 9.9 %multiply_convert_fusion.1 = (bf16[1024,1024]{1,0:T(8,128)(2,1)S(1)}, bf16[1024,1024]{1,0:T(8,128)(2,1)S(1)}, bf16[1024,1024]{1,0:T(8,128)(2,1)}) fusion(f32[1024,2048]{1,0:T(8,128)} %fusion.111, bf16[1024,1024]{1,0:T(8,128)(2,1)} %bitcast.36, bf16[1024,1024]{1,0:T(8,128)(2,1)} %bitcast.177), kind=kOutput, calls=%fused_computation.12 | convolution fusion | flops 2164260864 | bytes 18874368 | tf_op jit(solution)/shard_map/dot_general | solution.py:538
  287.4 6.5 copy.252
  294.0 4.0 copy.253
  297.9 6.0 convert_bitcast_fusion
  303.9 6.5 convolution_convert_fusion.2
  312.6 3.3 copy.242
  316.0 5.9 convolution_convert_fusion.4
  321.9 4.5 all-to-all-start.4
  326.4 9.4 %fusion.19 = bf16[1024,1024]{1,0:T(8,128)(2,1)} fusion(bf16[2048,1024]{1,0:T(8,128)(2,1)} %bitcast.172, bf16[1024,1024]{1,0:T(8,128)(2,1)} %copy-done.26, bf16[1024,1024]{1,0:T(8,128)(2,1)} %copy-done.25), kind=kOutput, calls=%fused_computation.31 | convolution fusion | flops 4304404480 | bytes 10485760 | tf_op jit(solution)/shard_map/dot_general | solution.py:532
  335.8 15.0 %all-to-all-done.4 = bf16[4,256,1024]{2,1,0:T(8,128)(2,1)} async-done(((bf16[4,256,1024]{2,1,0:T(8,128)(2,1)}), bf16[4,256,1024]{2,1,0:T(8,128)(2,1)}, u32[]{:S(2)}, u32[]{:S(2)}) %all-to-all-start.4) | async-done | bytes 2097184 | tf_op jit(solution)/shard_map/all_to_all | solution.py:617
  350.8 4.7 all-to-all-start.6
  359.7 20.2 %all-to-all-done.6 = bf16[4,256,1024]{2,1,0:T(8,128)(2,1)} async-done(((bf16[4,256,1024]{2,1,0:T(8,128)(2,1)}), bf16[4,256,1024]{2,1,0:T(8,128)(2,1)}, u32[]{:S(2)}, u32[]{:S(2)}) %all-to-all-start.6) | async-done | bytes 2097184 | tf_op jit(solution)/shard_map/all_to_all | solution.py:617
  387.9 3.2 fusion.30.g_ref
  391.1 11.5 %attend_back.1 = (bf16[256,1024]{1,0:T(8,128)(2,1)}, bf16[256,1024]{1,0:T(8,128)(2,1)}, bf16[256,1024]{1,0:T(8,128)(2,1)}) custom-call(bf16[256,3072]{1,0:T(8,128)(2,1)} %fusion.7.q_ref.k_ref.v_ref, bf16[256,3072]{1,0:T(8,128)(2,1)} %fusion.7.q_ref.k_ref.v_ref, bf16[256,3072]{1,0:T(8,128)(2,1)} %fusion.7.q_ref.k_ref.v_ref, bf16[256,1024]{1,0:T(8,128)(2,1)} %fusion.30.g_ref), custom_call_target="tpu_custom_call" | custom-call | tf_op jit(solution)/shard_map/attend_back/pallas_call | solution.py:950
  405.8 6.3 multiply_reduce_fusion.1
  415.1 4.2 multiply_reduce_fusion.5
  420.5 13.2 %all_to_all.56 = bf16[32,2,1024]{2,1,0:T(2,128)(2,1)S(1)} all-to-all(bf16[32,2,1024]{2,1,0:T(2,128)(2,1)S(1)} %reshape.482), channel_id=1, replica_groups=mesh['narrow'=4,'wide'=8] {'narrow','wide'}, dimensions={0} | all-to-all | bytes 262144 | tf_op jit(solution)/shard_map/all_to_all | solution.py:617
  434.9 14.6 %mixer_backward.1 = (bf16[1024,128]{1,0:T(8,128)(2,1)S(1)}, bf16[1024,256]{1,0:T(8,128)(2,1)S(1)}, f32[1024,1]{1,0:T(8,128)S(1)}, f32[8,128]{1,0:T(8,128)S(1)}, ...) custom-call(f32[3]{0:T(128)S(1)} %pad_maximum_fusion.8.numbers, bf16[1024,128]{1,0:T(8,128)(2,1)S(1)} %convolution_convert_fusion.8.xz, ...), custom_call_target="tpu_custom_call" | custom-call | tf_op jit(solution)/shard_map/mixer_backward/pallas_call | solution.py:850
  450.7 4.5 all-to-all-start.8
  461.4 4.5 convolution_convert_fusion.1
  467.1 12.3 %all-to-all-done.8 = bf16[32,32,512]{2,1,0:T(8,128)(2,1)} async-done(((bf16[32,32,512]{2,1,0:T(8,128)(2,1)}), bf16[32,32,512]{2,1,0:T(8,128)(2,1)}, u32[]{:S(2)}, u32[]{:S(2)}) %all-to-all-start.8) | async-done | bytes 1048608 | tf_op jit(solution)/shard_map/all_to_all | solution.py:617
  484.4 7.8 %multiply_reduce_fusion.7 = (f32[1024]{0:T(1024)}, f32[32]{0:T(128)}, f32[32,1024]{1,0:T(8,128)}) fusion(f32[32,1024]{1,0:T(8,128)S(1)} %copy-done.20, f32[32]{0:T(128)S(1)} %fusion.96, f32[1024]{0:T(1024)S(1)} %copy-done.39, bf16[1024,4384]{1,0:T(8,128)(2,1)} %all-gather.8.cloned.1.call-done, bf16[32,32]{1,0:T(8,128)(2,1)S(1)} %bitcast.204, ...), kind=kOutput, calls=%fused_computation.128 | convolution fusion | flops 288627680 | bytes 9529600 | tf_op jit(solution)/shard_map/dot_general | solution.py:538
  492.3 6.6 pad_maximum_fusion
  501.9 6.3 all-to-all-start.9
  525.0 53.6 %gather_all.3 = bf16[4,4,2,32,2560]{4,3,2,1,0:T(8,128)(2,1)} custom-call(bf16[32,2560]{1,0:T(8,128)(2,1)} %pad_maximum_fusion.7.refs_0_), custom_call_target="tpu_custom_call" | custom-call | tf_op jit(solution)/shard_map/gather_all/pallas_call | solution.py:602
  582.3 4.0 convolution_bitcast_fusion
  594.0 3.5 all-to-all-start.10
  597.5 28.4 %all-reduce.12.cloned.1.call-done = (f32[1024]{0:T(1024)}, f32[5,2304]{1,0:T(8,128)}, f32[3,32]{1,0:T(4,128)}, f32[2048]{0:T(1024)}, f32[1024]{0:T(1024)}, /*index=5*/f32[1024]{0:T(1024)}) async-done(((f32[1024]{0:T(1024)}, f32[5,2304]{1,0:T(8,128)}, f32[3,32]{1,0:T(4,128)}, f32[2048]{0:T(1024)}, f32[1024]{0:T(1024)}, /*index=5*/f32[1024]{0:T(1024)}), (f32[1024]{0:T(1024)}, f32[5,2304]{1,0:T(8,128)}, ...) | async-done | bytes 66960 | tf_op jit(solution)/shard_map/psum | solution.py:1244
  630.3 132.2 %reduce-scatter.3.cloned.1.call-done = bf16[32,4224]{1,0:T(8,128)(2,1)} async-done(((bf16[1024,4224]{1,0:T(8,128)(2,1)}), bf16[32,4224]{1,0:T(8,128)(2,1)}) %reduce-scatter.3.cloned.1.call-update) | async-done | bytes 270352 | tf_op jit(solution)/shard_map/reduce_scatter | solution.py:1165
  (322 shorter events, 149.6 us)
Async XLA Ops:
  7.2 150.8 %all-gather.4.cloned.1.call-start = ((), (), s32[]{:S(2)}) async-start(), calls=%async_computation.13 | async-start | bytes 13246464 | tf_op jit(solution)/shard_map/all_gather | solution.py:1046
  13.8 225.9 %all-gather.6.cloned.1.call-start = ((), (), s32[]{:S(2)}) async-start(), calls=%async_computation.14 | async-start | bytes 7077888 | tf_op jit(solution)/shard_map/all_gather | solution.py:1056
  16.0 19.6 %copy-start.27 = (bf16[32,4384]{1,0:T(8,128)(2,1)S(1)}, bf16[32,4384]{1,0:T(8,128)(2,1)}, u32[]{:S(2)}) copy-start(bf16[32,4384]{1,0:T(8,128)(2,1)} %param.31) | copy-start | bytes 841732
  17.2 26.4 %copy-start.56 = (s32[9]{0:T(128)S(1)}, s32[9]{0:T(128)}, u32[]{:S(2)}) copy-start(s32[9]{0:T(128)} %param.26) | copy-start | bytes 112
  17.2 27.0 %copy-start.54 = (s32[9]{0:T(128)S(1)}, s32[9]{0:T(128)}, u32[]{:S(2)}) copy-start(s32[9]{0:T(128)} %param.27) | copy-start | bytes 112
  33.3 12.0 %copy-start.55 = (s32[256]{0:T(256)S(1)}, s32[256]{0:T(256)}, u32[]{:S(2)}) copy-start(s32[256]{0:T(256)} %param.25) | copy-start | bytes 3076
  33.3 12.1 %copy-start.36 = (bf16[32,1024]{1,0:T(8,128)(2,1)S(1)}, bf16[32,1024]{1,0:T(8,128)(2,1)}, u32[]{:S(2)}) copy-start(bf16[32,1024]{1,0:T(8,128)(2,1)} %param.29) | copy-start | bytes 196612
  34.9 449.5 %all-gather.8.cloned.1.call-start = ((), (), s32[]{:S(2)}) async-start(), calls=%async_computation.15 | async-start | bytes 9461760 | tf_op jit(solution)/shard_map/all_gather | solution.py:1057
  37.1 92.3 %all-to-all-start = ((bf16[32,32,128]{2,1,0:T(8,128)(2,1)}), bf16[32,32,128]{2,1,0:T(8,128)(2,1)S(1)}, u32[]{:S(2)}, u32[]{:S(2)}) async-start(bf16[32,32,128]{2,1,0:T(8,128)(2,1)} %copy.211), calls=%async_computation | async-start | bytes 524288 | tf_op jit(solution)/shard_map/all_to_all | solution.py:617
  44.9 58.1 %copy-start.37 = (bf16[1024,8]{0,1:T(8,128)(2,1)}, bf16[1024,8]{0,1:T(8,128)(2,1)S(1)}, u32[]{:S(2)}) copy-start(bf16[1024,8]{0,1:T(8,128)(2,1)S(1)} %get-tuple-element.175) | copy-start | bytes 49156
  104.0 6.3 copy-start.15
  129.3 15.3 %copy-start.35 = (f32[2048]{0:T(1024)S(1)}, f32[2048]{0:T(1024)}, u32[]{:S(2)}) copy-start(f32[2048]{0:T(1024)} %param.37) | copy-start | bytes 24580
  139.1 23.6 %copy-start = (f32[8,64,128]{2,1,0:T(8,128)}, f32[8,64,128]{2,1,0:T(8,128)S(1)}, u32[]{:S(2)}) copy-start(f32[8,64,128]{2,1,0:T(8,128)S(1)} %get-tuple-element.43.states) | copy-start | bytes 786436
  140.0 13.8 %all-to-all-start.1 = ((bf16[32,2,1024]{2,1,0:T(2,128)(2,1)}), bf16[32,2,1024]{2,1,0:T(2,128)(2,1)}, u32[]{:S(2)}, u32[]{:S(2)}) async-start(bf16[32,2,1024]{2,1,0:T(2,128)(2,1)} %reshape.480), calls=%async_computation.1 | async-start | bytes 262144 | tf_op jit(solution)/shard_map/all_to_all | solution.py:617
  155.1 7.6 copy-start.48
  174.3 6.6 copy-start.33
  186.8 12.6 %copy-start.40 = (f32[1024]{0:T(1024)S(1)}, f32[1024]{0:T(1024)}, u32[]{:S(2)}) copy-start(f32[1024]{0:T(1024)} %param.45) | copy-start | bytes 12292
  201.2 31.2 %all-to-all-start.2 = ((bf16[4,256,1024]{2,1,0:T(8,128)(2,1)}), bf16[4,256,1024]{2,1,0:T(8,128)(2,1)}, u32[]{:S(2)}, u32[]{:S(2)}) async-start(bf16[4,256,1024]{2,1,0:T(8,128)(2,1)} %broadcast_in_dim.149), calls=%async_computation.2 | async-start | bytes 4194304 | tf_op jit(solution)/shard_map/all_to_all | solution.py:617
  235.0 38.0 %all-to-all-start.5 = ((bf16[4,256,1024]{2,1,0:T(8,128)(2,1)}), bf16[4,256,1024]{2,1,0:T(8,128)(2,1)}, u32[]{:S(2)}, u32[]{:S(2)}) async-start(bf16[4,256,1024]{2,1,0:T(8,128)(2,1)} %broadcast_in_dim.150), calls=%async_computation.5 | async-start | bytes 4194304 | tf_op jit(solution)/shard_map/all_to_all | solution.py:617
  239.4 351.6 %reduce-scatter.5.cloned.1.call-start = ((), (), s32[]{:S(2)}) async-start(), calls=%async_computation.17 | async-start | bytes 7077888 | tf_op jit(solution)/shard_map/reduce_scatter | solution.py:1142
  321.9 28.9 %all-to-all-start.4 = ((bf16[4,256,1024]{2,1,0:T(8,128)(2,1)}), bf16[4,256,1024]{2,1,0:T(8,128)(2,1)}, u32[]{:S(2)}, u32[]{:S(2)}) async-start(bf16[4,256,1024]{2,1,0:T(8,128)(2,1)} %bitcast.181), calls=%async_computation.4 | async-start | bytes 4194304 | tf_op jit(solution)/shard_map/all_to_all | solution.py:617
  350.8 29.1 %all-to-all-start.6 = ((bf16[4,256,1024]{2,1,0:T(8,128)(2,1)}), bf16[4,256,1024]{2,1,0:T(8,128)(2,1)}, u32[]{:S(2)}, u32[]{:S(2)}) async-start(bf16[4,256,1024]{2,1,0:T(8,128)(2,1)} %bitcast.180), calls=%async_computation.6 | async-start | bytes 4194304 | tf_op jit(solution)/shard_map/all_to_all | solution.py:617
  355.6 28.5 %copy-start.44 = (f32[256]{0:T(256)S(1)}, f32[256]{0:T(256)}, u32[]{:S(2)}) copy-start(f32[256]{0:T(256)} %copy-done.43) | copy-start | bytes 3076
  405.8 6.3 copy-start.21
  405.8 6.3 copy-start.7
  405.8 6.3 copy-start.11
  412.1 7.2 copy-start.49
  449.5 8.8 %copy-start.12 = (f32[256,1024]{1,0:T(8,128)S(1)}, f32[256,1024]{1,0:T(8,128)}, u32[]{:S(2)}) copy-start(f32[256,1024]{1,0:T(8,128)} %copy-done.10) | copy-start | bytes 3145732
  449.5 11.9 %copy-start.8 = (f32[256,1024]{1,0:T(8,128)S(1)}, f32[256,1024]{1,0:T(8,128)}, u32[]{:S(2)}) copy-start(f32[256,1024]{1,0:T(8,128)} %copy-done.6) | copy-start | bytes 3145732
  450.7 28.6 %all-to-all-start.8 = ((bf16[32,32,512]{2,1,0:T(8,128)(2,1)}), bf16[32,32,512]{2,1,0:T(8,128)(2,1)}, u32[]{:S(2)}, u32[]{:S(2)}) async-start(bf16[32,32,512]{2,1,0:T(8,128)(2,1)} %bitcast.174), calls=%async_computation.8 | async-start | bytes 2097152 | tf_op jit(solution)/shard_map/all_to_all | solution.py:617
  455.2 170.8 %all-reduce.12.cloned.1.call-start = ((), (), s32[]{:S(2)}) async-start(), calls=%async_computation.18 | async-start | bytes 192512 | tf_op jit(solution)/shard_map/psum | solution.py:1244
  456.8 9.1 %copy-start.51 = (f32[32]{0:T(128)}, f32[32]{0:T(128)S(1)}, u32[]{:S(2)}) copy-start(f32[32]{0:T(128)S(1)} %multiply_reduce_fusion.9) | copy-start | bytes 388
  456.9 27.5 %copy-start.50 = (f32[32]{0:T(128)}, f32[32]{0:T(128)S(1)}, u32[]{:S(2)}) copy-start(f32[32]{0:T(128)S(1)} %fusion.96) | copy-start | bytes 388
  466.0 18.4 %copy-start.20 = (f32[32,1024]{1,0:T(8,128)S(1)}, f32[32,1024]{1,0:T(8,128)}, u32[]{:S(2)}) copy-start(f32[32,1024]{1,0:T(8,128)} %copy.256) | copy-start | bytes 393220
  467.1 25.2 %copy-start.32 = (f32[5,2304]{1,0:T(8,128)}, f32[5,2304]{1,0:T(8,128)S(1)}, u32[]{:S(2)}) copy-start(f32[5,2304]{1,0:T(8,128)S(1)} %slice_dynamic-update-slice_fusion.2) | copy-start | bytes 138244
  483.2 9.0 %copy-start.34 = (bf16[32,32,1]{0,1,2:T(8,128)(2,1)}, bf16[32,32,1]{0,1,2:T(8,128)(2,1)S(1)}, u32[]{:S(2)}) copy-start(bf16[32,32,1]{0,1,2:T(8,128)(2,1)S(1)} %copy.258) | copy-start | bytes 6148
  484.4 7.9 %copy-start.13 = (bf16[1024,1024]{1,0:T(8,128)(2,1)S(1)}, bf16[1024,1024]{1,0:T(8,128)(2,1)}, u32[]{:S(2)}) copy-start(bf16[1024,1024]{1,0:T(8,128)(2,1)} %convolution_convert_fusion.3) | copy-start | bytes 6291460
  492.3 270.2 %reduce-scatter.3.cloned.1.call-start = ((), (), s32[]{:S(2)}) async-start(), calls=%async_computation.16 | async-start | bytes 8921088 | tf_op jit(solution)/shard_map/reduce_scatter | solution.py:1165
  500.5 13.9 %copy-start.31 = (f32[256,128]{1,0:T(8,128)S(1)}, f32[256,128]{1,0:T(8,128)}, u32[]{:S(2)}) copy-start(f32[256,128]{1,0:T(8,128)} %get-tuple-element.196) | copy-start | bytes 393220
  501.9 15.3 %all-to-all-start.9 = ((bf16[32,32,128]{2,1,0:T(8,128)(2,1)}), bf16[32,32,128]{2,1,0:T(8,128)(2,1)S(1)}, u32[]{:S(2)}, u32[]{:S(2)}) async-start(bf16[32,32,128]{2,1,0:T(8,128)(2,1)} %bitcast.51), calls=%async_computation.9 | async-start | bytes 524288 | tf_op jit(solution)/shard_map/all_to_all | solution.py:617
  521.0 58.8 %copy-start.38 = (bf16[1024,8]{0,1:T(8,128)(2,1)S(1)}, bf16[1024,8]{0,1:T(8,128)(2,1)}, u32[]{:S(2)}) copy-start(bf16[1024,8]{0,1:T(8,128)(2,1)} %copy-done.37) | copy-start | bytes 49156
  521.0 58.8 %copy-start.41 = (s32[1024,8]{0,1:T(8,128)S(1)}, s32[1024,8]{0,1:T(8,128)}, u32[]{:S(2)}) copy-start(s32[1024,8]{0,1:T(8,128)} %copy.225) | copy-start | bytes 98308
  521.0 58.8 %copy-start.53 = (s32[64]{0:T(128)S(1)}, s32[64]{0:T(128)}, u32[]{:S(2)}) copy-start(s32[64]{0:T(128)} %eq.144) | copy-start | bytes 772
  578.5 7.7 copy-start.5
  579.8 8.9 %copy-start.52 = (f32[64]{0:T(128)S(1)}, f32[64]{0:T(128)}, u32[]{:S(2)}) copy-start(f32[64]{0:T(128)} %dynamic_slice.44) | copy-start | bytes 772
  582.3 7.9 %copy-start.28 = (f32[32,2048]{1,0:T(8,128)S(1)}, f32[32,2048]{1,0:T(8,128)}, u32[]{:S(2)}) copy-start(f32[32,2048]{1,0:T(8,128)} %reshape.461) | copy-start | bytes 786436
  594.0 171.8 %all-to-all-start.10 = ((bf16[4,3,128,256]{3,2,1,0:T(8,128)(2,1)}), bf16[4,3,128,256]{3,2,1,0:T(8,128)(2,1)S(1)}, u32[]{:S(2)}, u32[]{:S(2)}) async-start(bf16[4,3,128,256]{3,2,1,0:T(8,128)(2,1)} %copy.243), calls=%async_computation.12 | async-start | bytes 1572864 | tf_op jit(solution)/shard_map/all_to_all | solution.py:617
  764.0 6.6 copy-start.45
  (30 other events, 99.7 us)
Sparse Core Ops, SparseCore 0:
  13.9 118.0 all-gather.3
  133.6 63.7 all-gather.5
  200.3 100.0 all-gather.7
  316.1 69.3 reduce-scatter.4
  492.4 133.4 all-reduce.11
  631.7 130.6 reduce-scatter.2

commit v2 on v1

--- a/solution.py
+++ b/solution.py
@@ -957,6 +957,168 @@
     )(qkv, qkv, qkv, heads_grad)
 
 
+def feed_kernel(
+    narrow,
+    x_in,
+    *refs,
+):
+    g_ins = refs[:narrow]
+    w_in, f_out, gx_out, grads, w, x, g, hid, gg, gu, sent, got = refs[narrow : narrow + 12]
+    w_sem, g_sem, x_sem, x_send, x_recv, r_send, r_recv = refs[narrow + 12 :]
+    n, wide_place = lax.axis_index("narrow"), lax.axis_index("wide")
+    barrier = pltpu.get_barrier_semaphore()
+    for k in range(1, narrow):
+        peer = (lax.rem(n + k, narrow), wide_place)
+        pl.semaphore_signal(barrier, inc=1, device_id=peer, device_id_type=MESH)
+    own_x = pltpu.make_async_copy(x_in, x.at[0], x_sem)
+    own_x.start()
+    g_copies = [pltpu.make_async_copy(g_ins[k], g.at[k], g_sem.at[k]) for k in range(narrow)]
+    w_copies = [pltpu.make_async_copy(w_in.at[:, i], w.at[i], w_sem.at[i]) for i in range(3)]
+    g_copies[0].start()
+    for copy in w_copies:
+        copy.start()
+    for copy in g_copies[1:]:
+        copy.start()
+    pl.semaphore_wait(barrier, narrow - 1)
+
+    def x_copy(k):
+        return pltpu.make_async_remote_copy(
+            src_ref=x_in,
+            dst_ref=x.at[k],
+            send_sem=x_send.at[k - 1],
+            recv_sem=x_recv.at[k - 1],
+            device_id=(lax.rem(n + narrow - k, narrow), wide_place),
+            device_id_type=MESH,
+        )
+
+    def r_copy(k):
+        return pltpu.make_async_remote_copy(
+            src_ref=sent.at[k - 1],
+            dst_ref=got.at[k - 1],
+            send_sem=r_send.at[k - 1],
+            recv_sem=r_recv.at[k - 1],
+            device_id=(lax.rem(n + k, narrow), wide_place),
+            device_id_type=MESH,
+        )
+
+    for k in range(1, narrow):
+        x_copy(k).start()
+    own_x.wait()
+    for copy in w_copies:
+        copy.wait()
+    for copy in g_copies:
+        copy.wait()
+    rows, width = x_in.shape
+    places, share = w.shape[1], w.shape[2]
+    hidden = places * share
+    chunk = 2 * share
+
+    def weights(i, start):
+        return w[i, pl.ds(start, 2)].reshape(chunk, width)
+
+    def columns(i, first):
+        return w[i, :, :, first : first + chunk].reshape(hidden, chunk)
+
+    def block(k, carry):
+        @pl.when(k > 0)
+        def _():
+            x_copy(k).wait_recv()
+
+        xk, gk = x[k], g[k]
+        for place in range(0, places, 2):
+            units = slice(place * share, place * share + chunk)
+            gate = nt(xk, weights(0, place))
+            up = nt(xk, weights(1, place))
+            dhid = nt(gk, weights(2, place))
+            s = jax.nn.sigmoid(gate)
+            act = gate * s
+            hid[k, :, units] = (act * up).astype(LOW)
+            gg[k, :, units] = (dhid * up * s * (1.0 + gate * (1.0 - s))).astype(LOW)
+            gu[k, :, units] = (dhid * act).astype(LOW)
+        ggk, guk, hidk = gg[k], gu[k], hid[k]
+        for first in range(0, width, chunk):
+            gx = nn(ggk, columns(0, first)) + nn(guk, columns(1, first))
+
+            @pl.when(k == 0)
+            def _():
+                gx_out[:, first : first + chunk] = gx
+
+            @pl.when(k > 0)
+            def _():
+                sent[k - 1, :, first : first + chunk] = gx.astype(LOW)
+
+        @pl.when(k > 0)
+        def _():
+            r_copy(k).start()
+
+        for first in range(0, width, chunk):
+            f_out[k, :, first : first + chunk] = nn(hidk, columns(2, first)).astype(LOW)
+        return carry
+
+    lax.fori_loop(0, narrow, block, 0)
+
+    def weight_grads(place, carry):
+        units = pl.ds(pl.multiple_of(place * share, share), share)
+        for i, (left, right) in enumerate(((gg, x), (gu, x), (hid, g))):
+            lhs = left[:, :, units].reshape(narrow * rows, share)
+            for first in range(0, width, 2 * chunk):
+                rhs = right[:, :, first : first + 2 * chunk].reshape(narrow * rows, 2 * chunk)
+                grads[place, i, :, first : first + 2 * chunk] = tn(lhs, rhs).astype(LOW)
+        return carry
+
+    lax.fori_loop(0, places, weight_grads, 0)
+    for k in range(1, narrow):
+        r_copy(k).wait_recv()
+        gx_out[...] += got[k - 1].astype(FULL)
+    for k in range(1, narrow):
+        x_copy(k).wait_send()
+        r_copy(k).wait_send()
+
+
+def feed_forward_back(x_own, g_blocks, feed_all, collective_id):
+    narrow = len(g_blocks)
+    rows, width = x_own.shape
+    places, _, share, _ = feed_all.shape
+    dma = pltpu.SemaphoreType.DMA
+    anywhere = pl.BlockSpec(memory_space=pl.ANY)
+
+    def rows_scratch(count, columns):
+        return pltpu.VMEM((count, rows, columns), LOW)
+
+    hidden = places * share
+    return pl.pallas_call(
+        partial(feed_kernel, narrow),
+        out_shape=[
+            jax.ShapeDtypeStruct((narrow, rows, width), LOW),
+            jax.ShapeDtypeStruct((rows, width), FULL),
+            jax.ShapeDtypeStruct(feed_all.shape, LOW),
+        ],
+        in_specs=[anywhere] * (narrow + 2),
+        out_specs=[in_vmem()] * 3,
+        scratch_shapes=[
+            pltpu.VMEM((3, places, share, width), LOW),
+            rows_scratch(narrow, width),
+            rows_scratch(narrow, width),
+            rows_scratch(narrow, hidden),
+            rows_scratch(narrow, hidden),
+            rows_scratch(narrow, hidden),
+            rows_scratch(narrow - 1, width),
+            rows_scratch(narrow - 1, width),
+            dma((3,)),
+            dma((narrow,)),
+            dma,
+            dma((narrow - 1,)),
+            dma((narrow - 1,)),
+            dma((narrow - 1,)),
+            dma((narrow - 1,)),
+        ],
+        compiler_params=pltpu.CompilerParams(
+            collective_id=collective_id, has_side_effects=True, vmem_limit_bytes=56 << 20
+        ),
+        name="feed",
+    )(x_own, *g_blocks, feed_all)
+
+
 def per_device_heads(
     byte_ids,
     doc_patches,
@@ -1114,31 +1276,15 @@
     out_grad = cotangent.astype(FULL) * keep_rows[:, None]
     feed_grad = out_grad.astype(LOW)
 
-    feed_width = wide * share
-    gate_up_all = feed_all[:, :2].reshape(wide, 2, share, D).transpose(1, 0, 2, 3)
-    gate_up_all = gate_up_all.reshape(2 * feed_width, D)
-    down_all = feed_all[:, 2].reshape(feed_width, D)
-
-    def over_narrow(values):
-        spread_out = jnp.broadcast_to(values[None], (narrow,) + values.shape)
-        return exchange(spread_out, "narrow").reshape((-1,) + values.shape[1:])
-
-    def back_over_narrow(values):
-        blocks = exchange(values.astype(LOW).reshape(narrow, rows, D), "narrow")
-        return jnp.sum(blocks.astype(FULL), axis=0)
-
-    grid_grad = over_narrow(feed_grad)
-    grid_in = over_narrow(normed_feed)
-    gate_up = nt(grid_in, gate_up_all)
-    gate, up = gate_up[:, :feed_width], gate_up[:, feed_width:]
-    hidden = (jax.nn.silu(gate) * up).astype(LOW)
-    feed_out = back_over_narrow(nn(hidden, down_all))
-    hidden_grad = nt(grid_grad, down_all)
-    gate_up_grad = silu_back(gate_up, hidden_grad, feed_width).astype(LOW)
-    grad_gate_up = tn(gate_up_grad, grid_in).reshape(2, wide, share, D)
-    grad_down_part = tn(hidden, grid_grad).reshape(1, wide, share, D)
-    feed_in_grad = back_over_narrow(nn(gate_up_grad, gate_up_all))
-    feed_grads = jnp.concatenate([grad_gate_up, grad_down_part]).transpose(1, 0, 2, 3).astype(LOW)
+    def passed_narrow(values, by):
+        pairs = [(i, (i + by) % narrow) for i in range(narrow)]
+        return lax.ppermute(values, "narrow", pairs)
+
+    g_blocks = [feed_grad] + [passed_narrow(feed_grad, narrow - k) for k in range(1, narrow)]
+    feed_parts, feed_in_grad, feed_grads = feed_forward_back(normed_feed, g_blocks, feed_all, 2)
+    feed_out = feed_parts[0].astype(FULL)
+    for k in range(1, narrow):
+        feed_out = feed_out + passed_narrow(feed_parts[k], k).astype(FULL)
     feed_sums = lax.psum_scatter(
         feed_grads.reshape(-1, D), "wide", scatter_dimension=0, tiled=True
     )
@@ -1203,7 +1349,21 @@
         ],
         axis=1,
     )
-    (end_all,) = gather_all([end_pack], 1)
+    sums_pack = jnp.concatenate(
+        [
+            grad_gain_mix,
+            grad_gated_gain,
+            grad_gain_attn,
+            grad_feed_gain,
+            dwbc[: CONV + 1].reshape(-1),
+            dwx[: CONV + 1, :HEAD_M].reshape(-1),
+            dnumbers[:3, 0],
+        ]
+    )
+    sums_width = -(-sums_pack.shape[0] // 1024) * 1024
+    sums_pack = jnp.pad(sums_pack, (0, sums_width - sums_pack.shape[0])).reshape(-1, 128)
+    end_all, sums_all = gather_all([end_pack, sums_pack], 1)
+    sums_all = sums_all.reshape(devices, sums_width)
     embed_grad_all = end_all[:, :D]
     mix_grad_all = end_all[:, D : 2 * D]
     bcdt_grad_all = end_all[:, 2 * D : 2 * D + bcdt_width]
@@ -1233,39 +1393,38 @@
         precision=highest,
     )
 
-    conv_grads = jnp.zeros((CONV + 1, DI + 2 * STATE), FULL)
-    conv_grads = lax.dynamic_update_slice(
-        conv_grads, dwx[: CONV + 1, :HEAD_M], (0, device * HEAD_M)
-    )
-    conv_grads = lax.dynamic_update_slice(conv_grads, dwbc[: CONV + 1], (0, DI))
-    number_grads = jnp.where(
-        jnp.arange(HEADS_M)[None, :] == device, dnumbers[:3, :1], 0.0
-    )
-    small = lax.psum(
-        (conv_grads, number_grads, grad_gain_mix, grad_gated_gain, grad_gain_attn, grad_feed_gain),
-        BOTH,
-    )
-    conv_grads, number_grads = small[:2]
+    owned = 3 * D + DI + (CONV + 1) * 2 * STATE
+    small = jnp.sum(sums_all[:, :owned], axis=0)
+    gain_grads = jnp.split(small[: 3 * D + DI], [D, D + DI, 2 * D + DI])
+    conv_own = sums_all[:, owned : owned + (CONV + 1) * HEAD_M].reshape(devices, CONV + 1, HEAD_M)
+    conv_grads = jnp.concatenate(
+        [
+            conv_own.transpose(1, 0, 2).reshape(CONV + 1, DI),
+            small[3 * D + DI :].reshape(CONV + 1, 2 * STATE),
+        ],
+        axis=1,
+    )
+    number_grads = sums_all[:, owned + (CONV + 1) * HEAD_M : owned + (CONV + 1) * HEAD_M + 3].T
     return (
         out_rows,
         grad_table,
         grad_patch,
-        small[2],
+        gain_grads[0],
         grad_in,
         conv_grads[:CONV],
         conv_grads[CONV],
         number_grads[0],
         number_grads[1],
         number_grads[2],
-        small[3],
+        gain_grads[1],
         grad_out,
         middle_sums[:, 4 * D :].T,
-        small[4],
+        gain_grads[2],
         middle_sums[:, :D],
         middle_sums[:, D : 2 * D],
         middle_sums[:, 2 * D : 3 * D],
         middle_sums[:, 3 * D : 4 * D],
-        small[5],
+        gain_grads[3],
         grad_gate,
         grad_up,
         grad_down,

time: 793 us -> 586 us (0.74)
  the two profiles are of different devices: /device:TPU:9 before, /device:TPU:0 now
where the time goes in v2:
time: 586 us; the launch traced here: 575 us
  Pallas kernels  206 us (35%)
  waiting for transfers between devices  99.5 us (17%)
  local copies, waits for them, and re-layouts  90.9 us (16%)
  matrix products  62.3 us (11%)
  starting transfers between devices  45.2 us (8%)
  blocking collectives  34 us (6%)
  other arithmetic  20.4 us (3%)
  between operations  16.1 us (3%)
    pallas_call x2, Pallas kernels, gather_all(): pl.pallas_call(partial(gather_kernel, count, narrow, wide // 2), out_shap...  107 us
    pallas_call x1, Pallas kernels, feed_forward_back(): pl.pallas_call(partial(feed_kernel, narrow), out_shape=[jax.ShapeDtypeStr...  57.5 us
    ppermute x6, waiting for transfers between devices, passed_narrow(): return lax.ppermute(values, 'narrow', pairs)  35.9 us
    all_to_all x5, waiting for transfers between devices, exchange(): return lax.all_to_all(blocks, axis, split_axis=0, concat_axis=0, tiled=True)  35.2 us
    all_to_all x2, blocking collectives, exchange(): return lax.all_to_all(blocks, axis, split_axis=0, concat_axis=0, tiled=True)  34 us
    all_to_all x5, starting transfers between devices, exchange(): return lax.all_to_all(blocks, axis, split_axis=0, concat_axis=0, tiled=True)  30.7 us
    reduce_scatter x1, waiting for transfers between devices, per_device_heads(): lax.psum_scatter(middle_grads, BOTH, scatter_dimension=0, tiled=True)  27.4 us
    unnamed x127, local copies, waits for them, and re-layouts  23.9 us
  transfers between devices with their start and end apart: 16, of which 8 were waited for; matrix products, arithmetic and copies ran while one was open for 27% of the time, Pallas kernels for 36%

profile of v2, /device:TPU:0, one launch (start us, length us, event | category | flops | bytes accessed | tf_op | source)
XLA Modules:
  0.0 574.8 jit_solution(8542376814094183172)
XLA Ops:
  17.1 19.3 %all_to_all.35 = bf16[4,3,128,256]{3,2,1,0:T(8,128)(2,1)S(1)} all-to-all(bf16[4,3,128,256]{3,2,1,0:T(8,128)(2,1)S(1)} %pad_maximum_fusion.1), channel_id=1, replica_groups=mesh['narrow'=4,'wide'=8] {'narrow'}, dimensions={0} | all-to-all | bytes 1572864 | tf_op jit(solution)/shard_map/all_to_all | solution.py:617
  40.2 4.3 all-to-all-start
  45.3 45.1 %gather_all.2 = (bf16[4,4,2,32,1536]{4,3,2,1,0:T(8,128)(2,1)}, bf16[4,4,2,8,128]{4,3,2,1,0:T(8,128)(2,1)}) custom-call(bf16[32,1536]{1,0:T(8,128)(2,1)} %fusion.80.refs_0_, bf16[8,128]{1,0:T(8,128)(2,1)} %refs_1_.1), custom_call_target="tpu_custom_call" | custom-call | tf_op jit(solution)/shard_map/gather_all/pallas_call | solution.py:602
  92.6 6.0 %convolution_convert_fusion = bf16[8192,128]{1,0:T(8,128)(2,1)} fusion(bf16[256,128]{1,0:T(8,128)(2,1)} %bitcast.190, s32[8192]{0:T(1024)S(1)} %eq.111, bf16[8192]{0:T(1024)(128)(2,1)S(1)} %sub.35), kind=kOutput, calls=%fused_computation | convolution fusion | flops 542113792 | bytes 2211840 | tf_op jit(solution)/shard_map/dot_general | solution.py:1228
  98.6 2.8 reshape.431
  102.1 4.0 multiply_reduce_fusion
  108.1 3.1 convolution_convert_fusion.3
  118.9 2.4 convolution_convert_fusion.6.xz
  121.3 7.3 %mixer_forward.1 = (f32[1024,64]{1,0:T(8,128)S(1)}, f32[1024,64]{1,0:T(8,128)S(1)}, f32[8,64,128]{2,1,0:T(8,128)S(1)}) custom-call(f32[3]{0:T(128)S(1)} %pad_maximum_fusion.4.numbers, bf16[1024,128]{1,0:T(8,128)(2,1)S(1)} %convolution_convert_fusion.6.xz, bf16[1024,256]{1,0:T(8,128)(2,1)S(1)} %slice.247.bc, f32[1024,1]{1,0:T(8,128)S(1)} %dynamic-slice_convert_fusion.dt, ...), custom_call_target="tpu_custom_call" | custom-call | tf_op jit(solution)/shard_map/mixer_forward/pallas_call | solution.py:829
  131.0 17.4 %all-to-all-start.1 = ((bf16[32,2,1024]{2,1,0:T(2,128)(2,1)}), bf16[32,2,1024]{2,1,0:T(2,128)(2,1)S(1)}, u32[]{:S(2)}, u32[]{:S(2)}) async-start(bf16[32,2,1024]{2,1,0:T(2,128)(2,1)} %reshape.472), calls=%async_computation.1 | async-start | bytes 262144 | tf_op jit(solution)/shard_map/all_to_all | solution.py:617
  149.5 2.7 collective-permute-start
  154.9 5.8 %all-to-all-done.1 = bf16[32,2,1024]{2,1,0:T(2,128)(2,1)S(1)} async-done(((bf16[32,2,1024]{2,1,0:T(2,128)(2,1)}), bf16[32,2,1024]{2,1,0:T(2,128)(2,1)S(1)}, u32[]{:S(2)}, u32[]{:S(2)}) %all-to-all-start.1) | async-done | bytes 131104 | tf_op jit(solution)/shard_map/all_to_all | solution.py:617
  161.8 4.7 slice.249
  166.5 7.9 %reshape.437 = bf16[32,32,2,1024]{3,2,1,0:T(2,128)(2,1)} reshape(bf16[1024,2048]{1,0:T(8,128)(2,1)} %slice.249) | data formatting | bytes 8388608 | tf_op jit(solution)/shard_map/reshape | solution.py:1260
  174.4 3.6 copy.223
  178.0 1.9 copy-done.6
  182.2 5.8 %fusion.7.q_ref.k_ref.v_ref = bf16[256,3072]{1,0:T(8,128)(2,1)} fusion(bf16[1024,6272]{1,0:T(8,128)(2,1)} %all-gather.4.cloned.1.call-done, f32[256,1024]{1,0:T(8,128)S(1)} %get-tuple-element.110, f32[1024]{0:T(1024)S(1)} %copy-done.35, f32[256]{0:T(256)S(1)} %fusion.93), kind=kOutput, calls=%fused_computation.12 | convolution fusion | flops 1612185600 | bytes 8918016 | tf_op jit(solution)/shard_map/dot_general | solution.py:1272
  188.0 8.7 %attend.1 = bf16[256,1024]{1,0:T(8,128)(2,1)} custom-call(bf16[256,3072]{1,0:T(8,128)(2,1)} %fusion.7.q_ref.k_ref.v_ref, bf16[256,3072]{1,0:T(8,128)(2,1)} %fusion.7.q_ref.k_ref.v_ref, bf16[256,3072]{1,0:T(8,128)(2,1)} %fusion.7.q_ref.k_ref.v_ref), custom_call_target="tpu_custom_call" | custom-call | tf_op jit(solution)/shard_map/attend/pallas_call | solution.py:933
  196.7 2.6 multiply_reduce_fusion.3
  201.4 57.5 %feed.1 = (bf16[4,256,1024]{2,1,0:T(8,128)(2,1)}, f32[256,1024]{1,0:T(8,128)}, bf16[8,3,128,1024]{3,2,1,0:T(8,128)(2,1)}) custom-call(bf16[256,1024]{1,0:T(8,128)(2,1)} %multiply_convert_fusion.2.x_in, bf16[256,1024]{1,0:T(8,128)(2,1)} %fusion.42.refs_0_, bf16[256,1024]{1,0:T(8,128)(2,1)} %collective-permute-done.refs_1_, ...), custom_call_target="tpu_custom_call" | custom-call | tf_op jit(solution)/shard_map/feed/pallas_call | solution.py:1089
  260.7 8.9 %collective-permute-start.5 = (bf16[256,1024]{1,0:T(8,128)(2,1)S(1)}, bf16[256,1024]{1,0:T(8,128)(2,1)S(1)}, u32[]{:S(2)}, u32[]{:S(2)}) collective-permute-start(bf16[256,1024]{1,0:T(8,128)(2,1)S(1)} %get-tuple-element.71), channel_id=1, source_target_pairs={{0,24},{8,0},{16,8},{24,16},{1,25},{9,1},{17,9},{25,17},{2,26},{10... | collective-permute-start | bytes 1572872 | tf_op jit(solution)/shard_map/ppermute | solution.py:1281
  271.3 19.1 %collective-permute-done.5 = bf16[256,1024]{1,0:T(8,128)(2,1)S(1)} collective-permute-done((bf16[256,1024]{1,0:T(8,128)(2,1)S(1)}, bf16[256,1024]{1,0:T(8,128)(2,1)S(1)}, u32[]{:S(2)}, u32[]{:S(2)}) %collective-permute-start.5) | collective-permute-done | bytes 524320 | tf_op jit(solution)/shard_map/ppermute | solution.py:1281
  290.4 7.8 %collective-permute-done.4 = bf16[256,1024]{1,0:T(8,128)(2,1)S(1)} collective-permute-done((bf16[256,1024]{1,0:T(8,128)(2,1)S(1)}, bf16[256,1024]{1,0:T(8,128)(2,1)S(1)}, u32[]{:S(2)}, u32[]{:S(2)}) %collective-permute-start.4) | collective-permute-done | bytes 524320 | tf_op jit(solution)/shard_map/ppermute | solution.py:1281
  298.3 8.9 %collective-permute-done.3 = bf16[256,1024]{1,0:T(8,128)(2,1)S(1)} collective-permute-done((bf16[256,1024]{1,0:T(8,128)(2,1)S(1)}, bf16[256,1024]{1,0:T(8,128)(2,1)S(1)}, u32[]{:S(2)}, u32[]{:S(2)}) %collective-permute-start.3) | collective-permute-done | bytes 524320 | tf_op jit(solution)/shard_map/ppermute | solution.py:1281
  307.2 2.5 fusion.35
  310.7 3.2 fusion.27.g_ref
  313.8 11.6 %attend_back.1 = (bf16[256,1024]{1,0:T(8,128)(2,1)}, bf16[256,1024]{1,0:T(8,128)(2,1)}, bf16[256,1024]{1,0:T(8,128)(2,1)}) custom-call(bf16[256,3072]{1,0:T(8,128)(2,1)} %fusion.7.q_ref.k_ref.v_ref, bf16[256,3072]{1,0:T(8,128)(2,1)} %fusion.7.q_ref.k_ref.v_ref, bf16[256,3072]{1,0:T(8,128)(2,1)} %fusion.7.q_ref.k_ref.v_ref, bf16[256,1024]{1,0:T(8,128)(2,1)} %fusion.27.g_ref), custom_call_target="tpu_custom_call" | custom-call | tf_op jit(solution)/shard_map/attend_back/pallas_call | solution.py:950
  328.8 5.1 multiply_reduce_fusion.1
  335.8 1.9 convolution_convert_fusion.1
  337.8 3.8 pad_maximum_fusion
  345.0 1.9 fusion.110
  346.9 3.7 multiply_reduce_fusion.5
  351.3 14.7 %all_to_all.36 = bf16[32,2,1024]{2,1,0:T(2,128)(2,1)S(1)} all-to-all(bf16[32,2,1024]{2,1,0:T(2,128)(2,1)S(1)} %reshape.474), channel_id=1, replica_groups=mesh['narrow'=4,'wide'=8] {'narrow','wide'}, dimensions={0} | all-to-all | bytes 262144 | tf_op jit(solution)/shard_map/all_to_all | solution.py:617
  368.3 14.7 %mixer_backward.1 = (bf16[1024,128]{1,0:T(8,128)(2,1)S(1)}, bf16[1024,256]{1,0:T(8,128)(2,1)S(1)}, f32[1024,1]{1,0:T(8,128)S(1)}, f32[8,128]{1,0:T(8,128)S(1)}, ...) custom-call(f32[3]{0:T(128)S(1)} %pad_maximum_fusion.4.numbers, bf16[1024,128]{1,0:T(8,128)(2,1)S(1)} %convolution_convert_fusion.6.xz, ...), custom_call_target="tpu_custom_call" | custom-call | tf_op jit(solution)/shard_map/mixer_backward/pallas_call | solution.py:850
  383.8 3.1 convolution_convert_fusion.5
  386.8 2.7 all-to-all-start.5
  390.8 9.9 %all-to-all-done.5 = bf16[32,32,128]{2,1,0:T(8,128)(2,1)S(1)} async-done(((bf16[32,32,128]{2,1,0:T(8,128)(2,1)}), bf16[32,32,128]{2,1,0:T(8,128)(2,1)S(1)}, u32[]{:S(2)}, u32[]{:S(2)}) %all-to-all-start.5) | async-done | bytes 262176 | tf_op jit(solution)/shard_map/all_to_all | solution.py:617
  400.7 2.8 all-to-all-start.4
  404.2 3.1 slice.245
  411.6 19.4 %all-to-all-done.4 = bf16[32,32,512]{2,1,0:T(8,128)(2,1)S(1)} async-done(((bf16[32,32,512]{2,1,0:T(8,128)(2,1)}), bf16[32,32,512]{2,1,0:T(8,128)(2,1)S(1)}, u32[]{:S(2)}, u32[]{:S(2)}) %all-to-all-start.4) | async-done | bytes 1048608 | tf_op jit(solution)/shard_map/all_to_all | solution.py:617
  432.6 6.8 %multiply_reduce_fusion.7 = (f32[1024]{0:T(1024)S(1)}, f32[32]{0:T(128)S(1)}, f32[32,1024]{1,0:T(8,128)S(1)}) fusion(f32[32,1024]{1,0:T(8,128)S(1)} %copy-done.23, f32[32]{0:T(128)S(1)} %fusion.96, f32[1024]{0:T(1024)S(1)} %copy-done.38, bf16[1024,4384]{1,0:T(8,128)(2,1)} %all-gather.8.cloned.1.call-done, bf16[32,32]{1,0:T(8,128)(2,1)S(1)} %bitcast.182, ...), kind=kOutput, calls=%fused_computation.125 | convolution fusion | flops 288627680 | bytes 9529600 | tf_op jit(solution)/shard_map/dot_general | solution.py:538
  440.9 61.6 %gather_all.3 = (bf16[4,4,2,32,2560]{4,3,2,1,0:T(8,128)(2,1)}, f32[4,4,2,56,128]{4,3,2,1,0:T(8,128)}) custom-call(bf16[32,2560]{1,0:T(8,128)(2,1)} %pad_maximum_fusion.3.refs_0_, f32[56,128]{1,0:T(8,128)} %pad_bitcast_fusion.refs_1_), custom_call_target="tpu_custom_call" | custom-call | tf_op jit(solution)/shard_map/gather_all/pallas_call | solution.py:602
  514.7 2.1 fusion.12
  516.9 2.3 convolution_bitcast_fusion
  520.4 2.2 fusion.17
  524.9 1.9 reshape.457
  527.9 3.5 all-to-all-start.6
  533.9 27.4 %reduce-scatter.3.cloned.1.call-done = bf16[32,4224]{1,0:T(8,128)(2,1)} async-done(((bf16[1024,4224]{1,0:T(8,128)(2,1)}), bf16[32,4224]{1,0:T(8,128)(2,1)}) %reduce-scatter.3.cloned.1.call-update) | async-done | bytes 270352 | tf_op jit(solution)/shard_map/reduce_scatter | solution.py:1311
  (299 shorter events, 88.8 us)
Async XLA Ops:
  7.2 154.6 %all-gather.4.cloned.1.call-start = ((), (), s32[]{:S(2)}) async-start(), calls=%async_computation.9 | async-start | bytes 13246464 | tf_op jit(solution)/shard_map/all_gather | solution.py:1208
  13.8 187.6 %all-gather.6.cloned.1.call-start = ((), (), s32[]{:S(2)}) async-start(), calls=%async_computation.10 | async-start | bytes 7077888 | tf_op jit(solution)/shard_map/all_gather | solution.py:1218
  17.1 21.7 %copy-start.28 = (bf16[32,4384]{1,0:T(8,128)(2,1)S(1)}, bf16[32,4384]{1,0:T(8,128)(2,1)}, u32[]{:S(2)}) copy-start(bf16[32,4384]{1,0:T(8,128)(2,1)} %param.31) | copy-start | bytes 841732
  36.7 7.8 %copy-start.50 = (s32[256]{0:T(256)S(1)}, s32[256]{0:T(256)}, u32[]{:S(2)}) copy-start(s32[256]{0:T(256)} %param.25) | copy-start | bytes 3076
  36.8 7.9 %copy-start.37 = (bf16[32,1024]{1,0:T(8,128)(2,1)S(1)}, bf16[32,1024]{1,0:T(8,128)(2,1)}, u32[]{:S(2)}) copy-start(bf16[32,1024]{1,0:T(8,128)(2,1)} %param.29) | copy-start | bytes 196612
  38.0 53.8 %copy-start.51 = (s32[9]{0:T(128)S(1)}, s32[9]{0:T(128)}, u32[]{:S(2)}) copy-start(s32[9]{0:T(128)} %param.26) | copy-start | bytes 112
  38.0 54.0 %copy-start.49 = (s32[9]{0:T(128)S(1)}, s32[9]{0:T(128)}, u32[]{:S(2)}) copy-start(s32[9]{0:T(128)} %param.27) | copy-start | bytes 112
  38.0 394.6 %all-gather.8.cloned.1.call-start = ((), (), s32[]{:S(2)}) async-start(), calls=%async_computation.11 | async-start | bytes 9461760 | tf_op jit(solution)/shard_map/all_gather | solution.py:1219
  40.2 78.7 %all-to-all-start = ((bf16[32,32,128]{2,1,0:T(8,128)(2,1)}), bf16[32,32,128]{2,1,0:T(8,128)(2,1)S(1)}, u32[]{:S(2)}, u32[]{:S(2)}) async-start(bf16[32,32,128]{2,1,0:T(8,128)(2,1)} %copy.218), calls=%async_computation | async-start | bytes 524288 | tf_op jit(solution)/shard_map/all_to_all | solution.py:617
  91.5 7.1 %copy-start.15 = (s32[1024,8]{1,0:T(8,128)}, s32[1024,8]{1,0:T(8,128)S(1)}, u32[]{:S(2)}) copy-start(s32[1024,8]{1,0:T(8,128)S(1)} %slice_convert_fusion) | copy-start | bytes 98308
  108.1 5.3 copy-start.53
  108.1 6.6 %copy-start.54 = (f32[32]{0:T(128)S(1)}, f32[32]{0:T(128)}, u32[]{:S(2)}) copy-start(f32[32]{0:T(128)} %param.34) | copy-start | bytes 388
  117.4 31.1 %copy-start.40 = (f32[256]{0:T(256)}, f32[256]{0:T(256)S(1)}, u32[]{:S(2)}) copy-start(f32[256]{0:T(256)S(1)} %mul.355) | copy-start | bytes 3076
  118.9 29.6 %copy-start.26 = (bf16[256,1024]{1,0:T(8,128)(2,1)S(1)}, bf16[256,1024]{1,0:T(8,128)(2,1)}, u32[]{:S(2)}) copy-start(bf16[256,1024]{1,0:T(8,128)(2,1)} %param.49) | copy-start | bytes 1572868
  121.3 33.5 %copy-start.36 = (f32[2048]{0:T(1024)S(1)}, f32[2048]{0:T(1024)}, u32[]{:S(2)}) copy-start(f32[2048]{0:T(1024)} %param.37) | copy-start | bytes 24580
  131.0 29.7 %all-to-all-start.1 = ((bf16[32,2,1024]{2,1,0:T(2,128)(2,1)}), bf16[32,2,1024]{2,1,0:T(2,128)(2,1)S(1)}, u32[]{:S(2)}, u32[]{:S(2)}) async-start(bf16[32,2,1024]{2,1,0:T(2,128)(2,1)} %reshape.472), calls=%async_computation.1 | async-start | bytes 262144 | tf_op jit(solution)/shard_map/all_to_all | solution.py:617
  148.5 376.5 %reduce-scatter.5.cloned.1.call-start = ((), (), s32[]{:S(2)}) async-start(), calls=%async_computation.13 | async-start | bytes 7077888 | tf_op jit(solution)/shard_map/reduce_scatter | solution.py:1288
  149.5 51.7 %collective-permute-start = (bf16[256,1024]{1,0:T(8,128)(2,1)}, bf16[256,1024]{1,0:T(8,128)(2,1)}, u32[]{:S(2)}, u32[]{:S(2)}) collective-permute-start(bf16[256,1024]{1,0:T(8,128)(2,1)} %fusion.42.refs_0_), channel_id=1, source_target_pairs={{0,24},{8,0},{16,8},{24,16},{1,25},{9,1},{17,9},{25,17},{2,26},{10... | collective-permute-start | bytes 1572872 | tf_op jit(solution)/shard_map/ppermute | solution.py:1281
  152.1 49.0 %collective-permute-start.1 = (bf16[256,1024]{1,0:T(8,128)(2,1)}, bf16[256,1024]{1,0:T(8,128)(2,1)}, u32[]{:S(2)}, u32[]{:S(2)}) collective-permute-start(bf16[256,1024]{1,0:T(8,128)(2,1)} %fusion.42.refs_0_), channel_id=1, source_target_pairs={{0,16},{8,24},{16,0},{24,8},{1,17},{9,25},{17,1},{25,9},{2,18},{10... | collective-permute-start | bytes 1572872 | tf_op jit(solution)/shard_map/ppermute | solution.py:1281
  152.7 48.5 %collective-permute-start.2 = (bf16[256,1024]{1,0:T(8,128)(2,1)}, bf16[256,1024]{1,0:T(8,128)(2,1)}, u32[]{:S(2)}, u32[]{:S(2)}) collective-permute-start(bf16[256,1024]{1,0:T(8,128)(2,1)} %fusion.42.refs_0_), channel_id=1, source_target_pairs={{0,8},{8,16},{16,24},{24,0},{1,9},{9,17},{17,25},{25,1},{2,10},{10... | collective-permute-start | bytes 1572872 | tf_op jit(solution)/shard_map/ppermute | solution.py:1281
  154.8 23.2 %copy-start.22 = (f32[32,1024]{1,0:T(8,128)}, f32[32,1024]{1,0:T(8,128)S(1)}, u32[]{:S(2)}) copy-start(f32[32,1024]{1,0:T(8,128)S(1)} %copy.251) | copy-start | bytes 393220
  161.0 5.5 copy-start.19
  161.2 5.3 copy-start.46
  161.2 5.3 copy-start.42
  199.2 59.7 %copy-start.44 = (f32[256]{0:T(256)}, f32[256]{0:T(256)S(1)}, u32[]{:S(2)}) copy-start(f32[256]{0:T(256)S(1)} %get-tuple-element.111) | copy-start | bytes 3076
  258.9 48.3 %copy-start.41 = (f32[256]{0:T(256)S(1)}, f32[256]{0:T(256)}, u32[]{:S(2)}) copy-start(f32[256]{0:T(256)} %copy-done.40) | copy-start | bytes 3076
  259.0 302.4 %reduce-scatter.3.cloned.1.call-start = ((), (), s32[]{:S(2)}) async-start(), calls=%async_computation.12 | async-start | bytes 8921088 | tf_op jit(solution)/shard_map/reduce_scatter | solution.py:1311
  259.0 12.0 %copy-start.9 = (f32[256,1024]{1,0:T(8,128)S(1)}, f32[256,1024]{1,0:T(8,128)}, u32[]{:S(2)}) copy-start(f32[256,1024]{1,0:T(8,128)} %copy-done.8) | copy-start | bytes 3145732
  259.0 12.0 %copy-start.21 = (f32[256,1024]{1,0:T(8,128)S(1)}, f32[256,1024]{1,0:T(8,128)}, u32[]{:S(2)}) copy-start(f32[256,1024]{1,0:T(8,128)} %get-tuple-element.45) | copy-start | bytes 3145732
  259.0 12.3 %copy-start.45 = (f32[256]{0:T(256)S(1)}, f32[256]{0:T(256)}, u32[]{:S(2)}) copy-start(f32[256]{0:T(256)} %copy-done.44) | copy-start | bytes 3076
  259.0 48.2 %copy-start.27 = (bf16[256,1024]{1,0:T(8,128)(2,1)S(1)}, bf16[256,1024]{1,0:T(8,128)(2,1)}, u32[]{:S(2)}) copy-start(bf16[256,1024]{1,0:T(8,128)(2,1)} %param.49) | copy-start | bytes 1572868
  260.7 29.8 %collective-permute-start.5 = (bf16[256,1024]{1,0:T(8,128)(2,1)S(1)}, bf16[256,1024]{1,0:T(8,128)(2,1)S(1)}, u32[]{:S(2)}, u32[]{:S(2)}) collective-permute-start(bf16[256,1024]{1,0:T(8,128)(2,1)S(1)} %get-tuple-element.71), channel_id=1, source_target_pairs={{0,24},{8,0},{16,8},{24,16},{1,25},{9,1},{17,9},{25,17},{2,26},{10... | collective-permute-start | bytes 1572872 | tf_op jit(solution)/shard_map/ppermute | solution.py:1281
  269.5 28.7 %collective-permute-start.4 = (bf16[256,1024]{1,0:T(8,128)(2,1)S(1)}, bf16[256,1024]{1,0:T(8,128)(2,1)S(1)}, u32[]{:S(2)}, u32[]{:S(2)}) collective-permute-start(bf16[256,1024]{1,0:T(8,128)(2,1)S(1)} %get-tuple-element.72), channel_id=1, source_target_pairs={{0,16},{8,24},{16,0},{24,8},{1,17},{9,25},{17,1},{25,9},{2,18},{10... | collective-permute-start | bytes 1572872 | tf_op jit(solution)/shard_map/ppermute | solution.py:1281
  271.0 36.2 %collective-permute-start.3 = (bf16[256,1024]{1,0:T(8,128)(2,1)S(1)}, bf16[256,1024]{1,0:T(8,128)(2,1)S(1)}, u32[]{:S(2)}, u32[]{:S(2)}) collective-permute-start(bf16[256,1024]{1,0:T(8,128)(2,1)S(1)} %get-tuple-element.70), channel_id=1, source_target_pairs={{0,8},{8,16},{16,24},{24,0},{1,9},{9,17},{17,25},{25,1},{2,10},{10... | collective-permute-start | bytes 1572872 | tf_op jit(solution)/shard_map/ppermute | solution.py:1281
  328.8 5.2 copy-start.11
  344.9 5.7 copy-start.47
  383.7 5.8 %copy-start.3 = (bf16[1024,256]{1,0:T(8,128)(2,1)S(1)}, bf16[1024,256]{1,0:T(8,128)(2,1)}, u32[]{:S(2)}) copy-start(bf16[1024,256]{1,0:T(8,128)(2,1)} %copy-done.2) | copy-start | bytes 1572868
  386.8 16.6 %copy-start.16 = (s32[1024,8]{1,0:T(8,128)S(1)}, s32[1024,8]{1,0:T(8,128)}, u32[]{:S(2)}) copy-start(s32[1024,8]{1,0:T(8,128)} %copy-done.15) | copy-start | bytes 98308
  386.8 13.8 %all-to-all-start.5 = ((bf16[32,32,128]{2,1,0:T(8,128)(2,1)}), bf16[32,32,128]{2,1,0:T(8,128)(2,1)S(1)}, u32[]{:S(2)}, u32[]{:S(2)}) async-start(bf16[32,32,128]{2,1,0:T(8,128)(2,1)} %bitcast.48), calls=%async_computation.5 | async-start | bytes 524288 | tf_op jit(solution)/shard_map/all_to_all | solution.py:617
  400.7 7.9 %copy-start.23 = (f32[32,1024]{1,0:T(8,128)S(1)}, f32[32,1024]{1,0:T(8,128)}, u32[]{:S(2)}) copy-start(f32[32,1024]{1,0:T(8,128)} %copy-done.22) | copy-start | bytes 393220
  400.7 8.0 %copy-start.32 = (f32[256,128]{1,0:T(8,128)S(1)}, f32[256,128]{1,0:T(8,128)}, u32[]{:S(2)}) copy-start(f32[256,128]{1,0:T(8,128)} %get-tuple-element.115) | copy-start | bytes 393220
  400.7 30.4 %all-to-all-start.4 = ((bf16[32,32,512]{2,1,0:T(8,128)(2,1)}), bf16[32,32,512]{2,1,0:T(8,128)(2,1)S(1)}, u32[]{:S(2)}, u32[]{:S(2)}) async-start(bf16[32,32,512]{2,1,0:T(8,128)(2,1)} %bitcast.149), calls=%async_computation.4 | async-start | bytes 2097152 | tf_op jit(solution)/shard_map/all_to_all | solution.py:617
  502.6 14.3 %copy-start.12 = (bf16[1024,1024]{1,0:T(8,128)(2,1)S(1)}, bf16[1024,1024]{1,0:T(8,128)(2,1)}, u32[]{:S(2)}) copy-start(bf16[1024,1024]{1,0:T(8,128)(2,1)} %slice.245) | copy-start | bytes 6291460
  510.8 8.4 %copy-start.33 = (f32[5,2048]{1,0:T(8,128)S(1)}, f32[5,2048]{1,0:T(8,128)}, u32[]{:S(2)}) copy-start(f32[5,2048]{1,0:T(8,128)} %reshape.455) | copy-start | bytes 122884
  511.6 7.6 %copy-start.14 = (bf16[4,4,2,32,2560]{4,3,2,1,0:T(8,128)(2,1)S(1)}, bf16[4,4,2,32,2560]{4,3,2,1,0:T(8,128)(2,1)}, u32[]{:S(2)}) copy-start(bf16[4,4,2,32,2560]{4,3,2,1,0:T(8,128)(2,1)} %get-tuple-element.57) | copy-start | bytes 15728644
  516.9 5.8 %copy-start.48 = (f32[64]{0:T(128)S(1)}, f32[64]{0:T(128)}, u32[]{:S(2)}) copy-start(f32[64]{0:T(128)} %dynamic_slice.44) | copy-start | bytes 772
  519.2 4.8 copy-start.29
  527.9 36.8 %all-to-all-start.6 = ((bf16[4,3,128,256]{3,2,1,0:T(8,128)(2,1)}), bf16[4,3,128,256]{3,2,1,0:T(8,128)(2,1)S(1)}, u32[]{:S(2)}, u32[]{:S(2)}) async-start(bf16[4,3,128,256]{3,2,1,0:T(8,128)(2,1)} %copy.244), calls=%async_computation.8 | async-start | bytes 1572864 | tf_op jit(solution)/shard_map/all_to_all | solution.py:617
  (23 other events, 51.6 us)
Sparse Core Ops, SparseCore 0:
  13.9 115.4 all-gather.3
  131.0 70.3 all-gather.5
  204.3 116.8 all-gather.7
  323.4 70.9 reduce-scatter.4
  400.1 161.1 reduce-scatter.2

commit v3 on v2

--- a/solution.py
+++ b/solution.py
@@ -7,6 +7,8 @@
 from jax.experimental.pallas import tpu as pltpu
 from jax.sharding import PartitionSpec as P
 
+NARROW = "narrow"
+WIDE = "wide"
 D = 1024
 PATCH = 8
 EMB = 128
@@ -207,22 +209,22 @@
 
 
 def spread(values):
-    by_rows = lax.all_to_all(values, "narrow", split_axis=1, concat_axis=0, tiled=True)
-    return lax.all_gather(by_rows, "wide", axis=0, tiled=True)
+    by_rows = lax.all_to_all(values, NARROW, split_axis=1, concat_axis=0, tiled=True)
+    return lax.all_gather(by_rows, WIDE, axis=0, tiled=True)
 
 
 def collect(term_fn, row_count):
     summed = lax.psum_scatter(
-        term_fn(jnp.int32(0), row_count * lax.axis_size("wide")).astype(jnp.bfloat16),
-        "wide",
+        term_fn(jnp.int32(0), row_count * lax.axis_size(WIDE)).astype(jnp.bfloat16),
+        WIDE,
         scatter_dimension=0,
         tiled=True,
     )
-    return lax.all_to_all(summed, "narrow", split_axis=0, concat_axis=1, tiled=True)
+    return lax.all_to_all(summed, NARROW, split_axis=0, concat_axis=1, tiled=True)
 
 
 def narrow_total(partial_rows):
-    return lax.psum(partial_rows, "narrow").astype(jnp.float32)
+    return lax.psum(partial_rows, NARROW).astype(jnp.float32)
 
 
 def silu_back(gate_up, hidden_grad, hidden_width):
@@ -263,23 +265,23 @@
 ):
     byte_rows = byte_ids.shape[0]
     patches = byte_rows // PATCH
-    device = lax.axis_index(("narrow", "wide"))
-    wide_count = lax.axis_size("wide")
+    device = lax.axis_index((NARROW, WIDE))
+    wide_count = lax.axis_size(WIDE)
     segment, first_patch, keep_mask = patch_layout(
         doc_patches, pad_bytes, device * patches, patches
     )
     rim_segment = patch_layout(doc_patches, pad_bytes, device * patches - (CONV - 1), CONV - 1)[0]
     layout = (segment, rim_segment, first_patch)
     gathered = (
-        lax.all_gather(byte_table, ("narrow", "wide"), axis=0, tiled=True),
-        lax.all_gather(patch_weight, ("narrow", "wide"), axis=0, tiled=True),
-        lax.all_gather(in_weight, ("narrow", "wide"), axis=0, tiled=True),
-        lax.all_gather(out_weight, ("narrow", "wide"), axis=0, tiled=True),
-        lax.all_gather(local_weight, ("narrow", "wide"), axis=1, tiled=True),
-        lax.all_gather(query_weight, ("narrow", "wide"), axis=0, tiled=True),
-        lax.all_gather(key_weight, ("narrow", "wide"), axis=0, tiled=True),
-        lax.all_gather(value_weight, ("narrow", "wide"), axis=0, tiled=True),
-        lax.all_gather(attn_weight, ("narrow", "wide"), axis=0, tiled=True),
+        lax.all_gather(byte_table, (NARROW, WIDE), axis=0, tiled=True),
+        lax.all_gather(patch_weight, (NARROW, WIDE), axis=0, tiled=True),
+        lax.all_gather(in_weight, (NARROW, WIDE), axis=0, tiled=True),
+        lax.all_gather(out_weight, (NARROW, WIDE), axis=0, tiled=True),
+        lax.all_gather(local_weight, (NARROW, WIDE), axis=1, tiled=True),
+        lax.all_gather(query_weight, (NARROW, WIDE), axis=0, tiled=True),
+        lax.all_gather(key_weight, (NARROW, WIDE), axis=0, tiled=True),
+        lax.all_gather(value_weight, (NARROW, WIDE), axis=0, tiled=True),
+        lax.all_gather(attn_weight, (NARROW, WIDE), axis=0, tiled=True),
     )
     table_all, patch_all, in_all, out_all, local_all, query_all, key_all, value_all, attn_all = (
         gathered
@@ -294,7 +296,7 @@
     normed_mix = root_norm(mixed_in, gain_mix).astype(jnp.bfloat16)
     projected = jnp.dot(normed_mix, in_all, preferred_element_type=jnp.float32).astype(jnp.bfloat16)
     rim_rows = passed_along(
-        projected[patches - (CONV - 1) :, DI : 2 * DI + 2 * STATE], ("narrow", "wide"), 1
+        projected[patches - (CONV - 1) :, DI : 2 * DI + 2 * STATE], (NARROW, WIDE), 1
     ).astype(jnp.float32)
     projected_f = projected.astype(jnp.float32)
     small_params = (conv_weight, conv_bias, step_bias, log_rate, skip_gain)
@@ -303,7 +305,7 @@
     )
     prefix = prefix_2(
         (decay_total, state_local),
-        ("narrow", "wide"),
+        (NARROW, WIDE),
         combine_states,
         (jnp.ones_like(decay_total), jnp.zeros_like(state_local)),
     )
@@ -445,14 +447,14 @@
     )
     suffix = carried_in_2(
         (decay_total, incoming_grad),
-        ("narrow", "wide"),
+        (NARROW, WIDE),
         combine_states,
         (jnp.ones_like(decay_total), jnp.zeros_like(incoming_grad)),
     )
     later_grad = suffix[1]
     decay_grad = jnp.sum(later_grad * incoming, axis=(1, 2))
     proj_grad_state, rim_grad_state, small_grad_state = state_back((decay_grad, later_grad))
-    rim_from_next = passed_along(rim_grad_mix + rim_grad_state, ("narrow", "wide"), -1)
+    rim_from_next = passed_along(rim_grad_mix + rim_grad_state, (NARROW, WIDE), -1)
     proj_grad = proj_grad_mix + proj_grad_state
     proj_grad = proj_grad.at[patches - (CONV - 1) :, DI : 2 * DI + 2 * STATE].add(rim_from_next)
     proj_low = proj_grad.astype(jnp.bfloat16)
@@ -470,15 +472,15 @@
     )
     grad_table = jnp.dot(onehot.astype(jnp.float32).T, byte_grad, precision=highest)
     shared = (
-        lax.psum_scatter(grad_table, ("narrow", "wide"), scatter_dimension=0, tiled=True),
-        lax.psum_scatter(grad_patch, ("narrow", "wide"), scatter_dimension=0, tiled=True),
-        lax.psum_scatter(grad_in, ("narrow", "wide"), scatter_dimension=0, tiled=True),
-        lax.psum_scatter(grad_out, ("narrow", "wide"), scatter_dimension=0, tiled=True),
-        lax.psum_scatter(grad_local, ("narrow", "wide"), scatter_dimension=1, tiled=True),
-        lax.psum_scatter(grad_query, ("narrow", "wide"), scatter_dimension=0, tiled=True),
-        lax.psum_scatter(grad_key, ("narrow", "wide"), scatter_dimension=0, tiled=True),
-        lax.psum_scatter(grad_value, ("narrow", "wide"), scatter_dimension=0, tiled=True),
-        lax.psum_scatter(grad_attn, ("narrow", "wide"), scatter_dimension=0, tiled=True),
+        lax.psum_scatter(grad_table, (NARROW, WIDE), scatter_dimension=0, tiled=True),
+        lax.psum_scatter(grad_patch, (NARROW, WIDE), scatter_dimension=0, tiled=True),
+        lax.psum_scatter(grad_in, (NARROW, WIDE), scatter_dimension=0, tiled=True),
+        lax.psum_scatter(grad_out, (NARROW, WIDE), scatter_dimension=0, tiled=True),
+        lax.psum_scatter(grad_local, (NARROW, WIDE), scatter_dimension=1, tiled=True),
+        lax.psum_scatter(grad_query, (NARROW, WIDE), scatter_dimension=0, tiled=True),
+        lax.psum_scatter(grad_key, (NARROW, WIDE), scatter_dimension=0, tiled=True),
+        lax.psum_scatter(grad_value, (NARROW, WIDE), scatter_dimension=0, tiled=True),
+        lax.psum_scatter(grad_attn, (NARROW, WIDE), scatter_dimension=0, tiled=True),
     )
     small_sum = lax.psum(
         (
@@ -492,7 +494,7 @@
             grad_gain_attn,
             grad_feed_gain,
         ),
-        ("narrow", "wide"),
+        (NARROW, WIDE),
     )
     return (
         out_rows,
@@ -525,7 +527,7 @@
 MESH = pl.DeviceIdType.MESH
 LOW = jnp.bfloat16
 FULL = jnp.float32
-BOTH = ("narrow", "wide")
+BOTH = (NARROW, WIDE)
 
 
 def nn(a, b, precision=None):
@@ -546,10 +548,52 @@
     )
 
 
-def gather_kernel(count, narrow, depth, *refs):
+def device_at(place, wide):
+    return (lax.div(place, wide), lax.rem(place, wide))
+
+
+def remote(src, dst, send, recv, peer):
+    return pltpu.make_async_remote_copy(
+        src_ref=src, dst_ref=dst, send_sem=send, recv_sem=recv, device_id=peer, device_id_type=MESH
+    )
+
+
+def greet_all(devices, wide):
+    me = lax.axis_index(NARROW) * wide + lax.axis_index(WIDE)
+    barrier = pltpu.get_barrier_semaphore()
+
+    def greet(k, carry):
+        peer = device_at(lax.rem(me + k, devices), wide)
+        pl.semaphore_signal(barrier, inc=1, device_id=peer, device_id_type=MESH)
+        return carry
+
+    lax.fori_loop(1, devices, greet, 0)
+    return me, lambda: pl.semaphore_wait(barrier, devices - 1)
+
+
+def send_blocks(me, devices, wide, src, dst, send, recv):
+    def one(k, carry):
+        place = lax.rem(me + k, devices)
+        remote(src.at[place], dst.at[me], send, recv, device_at(place, wide)).start()
+        return carry
+
+    lax.fori_loop(1, devices, one, 0)
+
+
+def wait_blocks(me, devices, wide, dst, send, recv):
+    part = dst.at[pl.ds(0, devices - 1)]
+    remote(part, part, send, recv, device_at(me, wide)).wait()
+
+
+def gather_kernel(count, narrow, depth, last, *refs):
+    if last:
+        middle, feed = refs[count : count + 2]
+        middle_out, feed_got = refs[2 * count + 2 : 2 * count + 4]
+        middle_got, m_send, m_recv, m_sem, f_send, f_recv, f_sem = refs[-7:]
+        refs = refs[:count] + refs[count + 2 : 2 * count + 2] + refs[2 * count + 4 : -7]
     ins, outs = refs[:count], refs[count : 2 * count]
     local, z_send, z_recv, n_send, n_recv, c_send, c_recv = refs[2 * count :]
-    n, w = lax.axis_index("narrow"), lax.axis_index("wide")
+    n, w = lax.axis_index(NARROW), lax.axis_index(WIDE)
     z, c = lax.div(w, 2), lax.rem(w, 2)
     z_peers = [(n, lax.rem(z + k, depth) * 2 + c) for k in range(1, depth)]
     n_peers = [lax.rem(n + k, narrow) for k in range(1, narrow)]
@@ -562,16 +606,37 @@
     pl.semaphore_signal(barrier, inc=1, device_id=twin, device_id_type=MESH)
     pl.semaphore_wait(barrier, len(z_peers) + len(n_peers) + 1)
 
-    def remote(src, dst, send, recv, peer):
-        return pltpu.make_async_remote_copy(
-            src_ref=src, dst_ref=dst, send_sem=send, recv_sem=recv, device_id=peer, device_id_type=MESH
-        )
-
     own = [pltpu.make_async_copy(ins[i], outs[i].at[n, z, c], local.at[i]) for i in range(count)]
     for i in range(count):
         own[i].start()
         for peer in z_peers:
             remote(ins[i], outs[i].at[n, z, c], z_send.at[i], z_recv.at[i], peer).start()
+    if last:
+        middle_copies, feed_copies = [], []
+        for k in range(1, depth):
+            place = lax.rem(z + k, depth)
+            middle_copies.append(
+                remote(
+                    middle.at[place],
+                    middle_got.at[k],
+                    m_send.at[k - 1],
+                    m_recv.at[k - 1],
+                    (n, place * 2 + c),
+                )
+            )
+        for k in range(1, narrow):
+            m = lax.rem(n + k, narrow)
+            feed_copies.append(
+                remote(feed.at[m], feed_got.at[n], f_send.at[k - 1], f_recv.at[k - 1], (m, w))
+            )
+        for copy in middle_copies + feed_copies:
+            copy.start()
+        own += [
+            pltpu.make_async_copy(middle.at[z], middle_got.at[0], m_sem),
+            pltpu.make_async_copy(feed.at[n], feed_got.at[n], f_sem),
+        ]
+        own[count].start()
+        own[count + 1].start()
     for i in range(count):
         own[i].wait()
         part = outs[i].at[n, pl.ds(0, depth - 1), c]
@@ -593,24 +658,49 @@
         remote(part, part, z_send.at[i], z_recv.at[i], twin).wait_send()
         part = outs[i].at[pl.ds(0, narrow - 1), :, c]
         remote(part, part, n_send.at[i], n_recv.at[i], twin).wait_send()
-
-
-def gather_all(arrays, collective_id):
-    narrow, wide = lax.axis_size("narrow"), lax.axis_size("wide")
+    if last:
+        own[count].wait()
+        own[count + 1].wait()
+        for copy in middle_copies:
+            copy.wait()
+        total = middle_got[0].astype(FULL)
+        for k in range(1, depth):
+            total += middle_got[k].astype(FULL)
+        middle_out[...] = total
+        for copy in feed_copies:
+            copy.wait()
+
+
+def gather_all(arrays, collective_id, middle=None, feed=None):
+    narrow, wide = lax.axis_size(NARROW), lax.axis_size(WIDE)
     count = len(arrays)
-    dma = pltpu.SemaphoreType.DMA((count,))
+    dma = pltpu.SemaphoreType.DMA
+    anywhere = pl.BlockSpec(memory_space=pl.ANY)
+    outs = [jax.ShapeDtypeStruct((narrow, wide // 2, 2) + a.shape, a.dtype) for a in arrays]
+    out_specs = [anywhere] * count
+    scratch = [dma((count,))] * 7
+    last = middle is not None
+    if last:
+        outs += [
+            jax.ShapeDtypeStruct(middle.shape[1:], FULL),
+            jax.ShapeDtypeStruct(feed.shape, feed.dtype),
+        ]
+        out_specs += [in_vmem(), anywhere]
+        scratch += [pltpu.VMEM(middle.shape, middle.dtype)]
+        scratch += [dma((wide // 2 - 1,))] * 2 + [dma] + [dma((narrow - 1,))] * 2 + [dma]
     outs = pl.pallas_call(
-        partial(gather_kernel, count, narrow, wide // 2),
-        out_shape=[
-            jax.ShapeDtypeStruct((narrow, wide // 2, 2) + a.shape, a.dtype) for a in arrays
-        ],
-        in_specs=[pl.BlockSpec(memory_space=pl.ANY)] * count,
-        out_specs=[pl.BlockSpec(memory_space=pl.ANY)] * count,
-        scratch_shapes=[dma] * 7,
-        compiler_params=pltpu.CompilerParams(collective_id=collective_id, has_side_effects=True),
+        partial(gather_kernel, count, narrow, wide // 2, last),
+        out_shape=outs,
+        in_specs=[anywhere] * (count + 2 * last),
+        out_specs=out_specs,
+        scratch_shapes=scratch,
+        compiler_params=pltpu.CompilerParams(
+            collective_id=collective_id, has_side_effects=True, vmem_limit_bytes=32 << 20
+        ),
         name="gather_all",
-    )(*arrays)
-    return [o.reshape((-1,) + a.shape[1:]) for o, a in zip(outs, arrays)]
+    )(*arrays, *((middle, feed) if last else ()))
+    gathered = [o.reshape((-1,) + a.shape[1:]) for o, a in zip(outs, arrays)]
+    return gathered + list(outs[count:])
 
 
 def exchange(blocks, axis):
@@ -686,6 +776,8 @@
 
 
 def mixer_backward_kernel(
+    narrow,
+    wide,
     numbers,
     xz,
     bc,
@@ -697,19 +789,59 @@
     bbc,
     y_in,
     states,
-    du_in,
-    dxz,
-    dbc,
-    ddt,
+    normed,
+    w_xz,
+    w_bcdt,
+    du_blocks,
+    feed_parts,
+    middle_parts,
     dwx,
     dwbc,
     dnumbers,
+    rows_grad,
+    xz_grads,
+    feed_sums,
+    middle_sums,
     xz_pad,
     bc_pad,
     dx_pad,
     dbc_pad,
     dstate,
+    du_got,
+    dxz,
+    dbcdt,
+    partial_rows,
+    core_got,
+    narrow_got,
+    z_rows,
+    z_got,
+    grads,
+    grads_got,
+    feed_got,
+    middle_got,
+    du_send,
+    du_recv,
+    core_send,
+    core_recv,
+    narrow_send,
+    narrow_recv,
+    z_send,
+    z_recv,
+    grads_send,
+    grads_recv,
+    feed_send,
+    feed_recv,
+    feed_sem,
+    middle_send,
+    middle_recv,
+    middle_sem,
 ):
+    devices = narrow * wide
+    depth = wide // 2
+    me, arrived = greet_all(devices, wide)
+    n, w = lax.axis_index(NARROW), lax.axis_index(WIDE)
+    z_place, core = lax.div(w, 2), lax.rem(w, 2)
+    twin = (n, z_place * 2 + 1 - core)
     count = xz.shape[0]
     blocks = count // QUERY
     xz_pad[pl.ds(0, 8), :] = jnp.zeros((8, xz_pad.shape[1]), FULL)
@@ -729,7 +861,40 @@
         bc_pad[pl.ds(start + 8, QUERY), :] = bc[rows, :].astype(FULL)
         return carry
 
+    arrived()
+    send_blocks(me, devices, wide, du_blocks, du_got, du_send, du_recv)
+    own_feed = pltpu.make_async_copy(feed_parts.at[z_place], feed_got.at[0], feed_sem)
+    own_feed.start()
+
+    def feed_copy(k):
+        place = lax.rem(z_place + k, depth)
+        return remote(
+            feed_parts.at[place],
+            feed_got.at[k],
+            feed_send.at[k - 1],
+            feed_recv.at[k - 1],
+            (n, place * 2 + core),
+        )
+
+    own_middle = pltpu.make_async_copy(middle_parts.at[n], middle_got.at[0], middle_sem)
+    own_middle.start()
+
+    def middle_copy(k):
+        m = lax.rem(n + k, narrow)
+        return remote(
+            middle_parts.at[m], middle_got.at[k], middle_send.at[k - 1], middle_recv.at[k - 1], (m, w)
+        )
+
+    for k in range(1, depth):
+        feed_copy(k).start()
+    for k in range(1, narrow):
+        middle_copy(k).start()
+    du_got[me] = du_blocks[me]
     lax.fori_loop(0, blocks, fill, 0)
+    wait_blocks(me, devices, wide, du_got, du_send, du_recv)
+    patches = du_blocks.shape[1]
+    group = QUERY // patches
+    own_lane = lax.broadcasted_iota(jnp.int32, (QUERY, STATE), 1) == me
 
     def slope(pre):
         s = jax.nn.sigmoid(pre)
@@ -771,7 +936,8 @@
         lower, delta, decay, begun, tail, kept = decays(mark, step, step_bias, rate_scale)
         held, dheld = states[i], dstate[...]
         z = xz[rows, :].astype(FULL)[:, HEAD_M:]
-        du, y = du_in[rows, :].astype(FULL), y_in[rows, :]
+        du = du_got[pl.ds(i * group, group)].astype(FULL).reshape(QUERY, HEAD_M)
+        y = y_in[rows, :]
         dy = du * jax.nn.silu(z)
         dz = du * y * slope(z)
         scores = nt(c, b, highest)
@@ -797,7 +963,7 @@
         dlog = tn(lower, jnp.broadcast_to(dtotal, (QUERY, QUERY)), highest)[:, :1] + dlast
         ddelta -= dlog * rate_scale
         dstep = ddelta * jax.nn.sigmoid(step + step_bias)
-        ddt[rows, :] = dstep
+        dbcdt[rows, 2 * STATE :] = jnp.where(own_lane, dstep, 0.0).astype(LOW)
         dnumbers[0:1, :] += jnp.broadcast_to(jnp.sum(dstep, axis=0, keepdims=True), (1, 128))
         dnumbers[1:2, :] -= jnp.broadcast_to(
             jnp.sum(dlog * delta[:, :1] * rate_scale, axis=0, keepdims=True), (1, 128)
@@ -808,12 +974,119 @@
         dpre = jnp.concatenate([db, dc], axis=1) * slope(pre)
         dx_pad[rows, :] = dpre_x
         dbc_pad[rows, :] = dpre
-        dxr = conv_back(xz_pad, start, dx_pad, dpre_x, wx[...], dwx)
-        dxz[rows, :] = jnp.concatenate([dxr[:, :HEAD_M], dz], axis=1).astype(dxz.dtype)
-        dbc[rows, :] = conv_back(bc_pad, start, dbc_pad, dpre, wbc[...], dwbc).astype(dbc.dtype)
+        dxz[rows, :] = jnp.concatenate([dz, dz], axis=1).astype(LOW)
         return carry
 
     lax.fori_loop(0, blocks, block, 0)
+
+    def unconvolve(i, carry):
+        start = pl.multiple_of(i * QUERY, QUERY)
+        rows = pl.ds(start, QUERY)
+        dxr = conv_back(xz_pad, start, dx_pad, dx_pad[rows, :], wx[...], dwx)
+        left = lax.broadcasted_iota(jnp.int32, dxr.shape, 1) < HEAD_M
+        dxz[rows, :] = jnp.where(left, dxr, dxz[rows, :].astype(FULL)).astype(LOW)
+        dbcdt[rows, : 2 * STATE] = conv_back(
+            bc_pad, start, dbc_pad, dbc_pad[rows, :], wbc[...], dwbc
+        ).astype(LOW)
+        return carry
+
+    lax.fori_loop(0, blocks, unconvolve, 0)
+
+    width = normed.shape[1]
+    own_rows = xz_grads.shape[1]
+
+    def rows_of(m, carry):
+        for z in range(depth):
+            start = (m * depth + z) * 2 * patches
+            rows = pl.ds(pl.multiple_of(start, 2 * patches), 2 * patches)
+            values = nt(dxz[rows, :], w_xz[...]) + nt(dbcdt[rows, :], w_bcdt[...])
+            partial_rows[m, z, :, :, :width] = values.astype(LOW).reshape(2, patches, width)
+        return carry
+
+    lax.fori_loop(0, narrow, rows_of, 0)
+
+    def weight_grads(m, carry):
+        span = width // narrow
+        columns = pl.ds(pl.multiple_of(m * span, span), span)
+        lhs = normed[:, columns]
+        grads[pl.ds(m * 2 * depth, 2 * depth)] = (
+            tn(lhs, dxz[...]).astype(LOW).reshape(2 * depth, own_rows, 2 * HEAD_M)
+        )
+        partial_rows[m, :, :, :, width:] = (
+            tn(lhs, dbcdt[...]).astype(LOW).reshape(depth, 2, own_rows, 3 * STATE)
+        )
+        return carry
+
+    lax.fori_loop(0, narrow, weight_grads, 0)
+    to_twin = remote(partial_rows.at[:, :, 1 - core], core_got, core_send, core_recv, twin)
+    to_twin.start()
+    to_twin.wait_recv()
+    for m in range(narrow):
+        for z in range(depth):
+            core_got[m, z] = (
+                core_got[m, z].astype(FULL) + partial_rows[m, z, core].astype(FULL)
+            ).astype(LOW)
+    for k in range(1, narrow):
+        m = lax.rem(n + k, narrow)
+        remote(core_got.at[m], narrow_got.at[k - 1], narrow_send.at[k - 1], narrow_recv.at[k - 1], (m, w)).start()
+    for k in range(1, narrow):
+        remote(
+            core_got.at[n], narrow_got.at[k - 1], narrow_send.at[k - 1], narrow_recv.at[k - 1], twin
+        ).wait_recv()
+    for z in range(depth):
+        total_rows = core_got[n, z].astype(FULL)
+        for k in range(1, narrow):
+            total_rows += narrow_got[k - 1, z].astype(FULL)
+        z_rows[z] = total_rows.astype(LOW)
+    for k in range(1, depth):
+        place = lax.rem(z_place + k, depth)
+        remote(
+            z_rows.at[place],
+            z_got.at[k - 1],
+            z_send.at[k - 1],
+            z_recv.at[k - 1],
+            (n, place * 2 + core),
+        ).start()
+    send_blocks(me, devices, wide, grads, grads_got, grads_send, grads_recv)
+    grads_got[me] = grads[me]
+    total_rows = z_rows[z_place].astype(FULL)
+    for k in range(1, depth):
+        remote(
+            z_rows.at[z_place], z_got.at[k - 1], z_send.at[k - 1], z_recv.at[k - 1], twin
+        ).wait_recv()
+        total_rows += z_got[k - 1].astype(FULL)
+    rows_grad[...] = total_rows
+    wait_blocks(me, devices, wide, grads_got, grads_send, grads_recv)
+    xz_grads[...] = grads_got[...]
+    own_middle.wait()
+    for k in range(1, narrow):
+        middle_copy(k).wait_recv()
+    for z in range(depth):
+        middle_total = middle_got[0, z].astype(FULL)
+        for k in range(1, narrow):
+            middle_total += middle_got[k, z].astype(FULL)
+        middle_sums[z] = middle_total.astype(LOW)
+    own_feed.wait()
+    for k in range(1, depth):
+        feed_copy(k).wait_recv()
+    for i in range(3):
+        feed_total = feed_got[0, i].astype(FULL)
+        for k in range(1, depth):
+            feed_total += feed_got[k, i].astype(FULL)
+        feed_sums[i] = feed_total.astype(LOW)
+    for k in range(1, depth):
+        feed_copy(k).wait_send()
+    for k in range(1, narrow):
+        middle_copy(k).wait_send()
+    to_twin.wait_send()
+    for k in range(1, narrow):
+        remote(
+            core_got.at[n], narrow_got.at[k - 1], narrow_send.at[k - 1], narrow_recv.at[k - 1], twin
+        ).wait_send()
+    for k in range(1, depth):
+        remote(
+            z_rows.at[z_place], z_got.at[k - 1], z_send.at[k - 1], z_recv.at[k - 1], twin
+        ).wait_send()
 
 
 def in_smem():
@@ -845,30 +1118,88 @@
     )(numbers, xz, bc, dt, marks, wx, bx, wbc, bbc)
 
 
-def mixer_backward(numbers, xz, bc, dt, marks, wx, bx, wbc, bbc, y, states, du):
-    count = xz.shape[0]
+def mixer_backward(
+    numbers, xz, bc, dt, marks, wx, bx, wbc, bbc, y, states, normed, w_xz, w_bcdt, du_blocks, feed_parts, middle_parts, collective_id
+):
+    narrow, wide = lax.axis_size(NARROW), lax.axis_size(WIDE)
+    devices = narrow * wide
+    count, width = normed.shape
+    patches = count // devices
+    own_rows = width // devices
+    dma = pltpu.SemaphoreType.DMA
+    low = partial(pltpu.VMEM, dtype=LOW)
+    every = width + w_bcdt.shape[1]
     return pl.pallas_call(
-        mixer_backward_kernel,
+        partial(mixer_backward_kernel, narrow, wide),
         out_shape=[
-            jax.ShapeDtypeStruct((count, 2 * HEAD_M), LOW),
-            jax.ShapeDtypeStruct((count, 2 * STATE), LOW),
-            jax.ShapeDtypeStruct((count, 1), FULL),
             jax.ShapeDtypeStruct((8, 2 * HEAD_M), FULL),
             jax.ShapeDtypeStruct((8, 2 * STATE), FULL),
             jax.ShapeDtypeStruct((8, 128), FULL),
+            jax.ShapeDtypeStruct((patches, every), FULL),
+            jax.ShapeDtypeStruct((devices, own_rows, 2 * HEAD_M), LOW),
+            jax.ShapeDtypeStruct(feed_parts.shape[1:], LOW),
+            jax.ShapeDtypeStruct(middle_parts.shape[1:], LOW),
         ],
-        in_specs=[in_smem()] + [in_vmem()] * 11,
-        out_specs=[in_vmem()] * 6,
+        in_specs=[in_smem()] + [in_vmem()] * 14 + [pl.BlockSpec(memory_space=pl.ANY)] * 2,
+        out_specs=[in_vmem()] * 7,
         scratch_shapes=[
             pltpu.VMEM((count + 8, 2 * HEAD_M), FULL),
             pltpu.VMEM((count + 8, 2 * STATE), FULL),
             pltpu.VMEM((count + 8, 2 * HEAD_M), FULL),
             pltpu.VMEM((count + 8, 2 * STATE), FULL),
             pltpu.VMEM((HEAD_M, STATE), FULL),
+            low((devices, patches, HEAD_M)),
+            low((count, 2 * HEAD_M)),
+            low((count, 3 * STATE)),
+            low((narrow, wide // 2, 2, patches, every)),
+            low((narrow, wide // 2, patches, every)),
+            low((narrow - 1, wide // 2, patches, every)),
+            low((wide // 2, patches, every)),
+            low((wide // 2 - 1, patches, every)),
+            low((devices, own_rows, 2 * HEAD_M)),
+            low((devices, own_rows, 2 * HEAD_M)),
+            low(feed_parts.shape),
+            low(middle_parts.shape),
+            dma,
+            dma,
+            dma,
+            dma,
+            dma((narrow - 1,)),
+            dma((narrow - 1,)),
+            dma((wide // 2 - 1,)),
+            dma((wide // 2 - 1,)),
+            dma,
+            dma,
+            dma((wide // 2 - 1,)),
+            dma((wide // 2 - 1,)),
+            dma,
+            dma((narrow - 1,)),
+            dma((narrow - 1,)),
+            dma,
         ],
-        compiler_params=pltpu.CompilerParams(vmem_limit_bytes=32 << 20),
+        compiler_params=pltpu.CompilerParams(
+            collective_id=collective_id, has_side_effects=True, vmem_limit_bytes=56 << 20
+        ),
         name="mixer_backward",
-    )(numbers, xz, bc, dt, marks, wx, bx, wbc, bbc, y, states, du)
+    )(
+        numbers,
+        xz,
+        bc,
+        dt,
+        marks,
+        wx,
+        bx,
+        wbc,
+        bbc,
+        y,
+        states,
+        normed,
+        w_xz,
+        w_bcdt,
+        du_blocks,
+        feed_parts,
+        middle_parts,
+    )
 
 
 def patch_causal():
@@ -888,73 +1219,427 @@
     return jnp.where(lax.div(lane, HEAD_A) == half, block, jnp.zeros_like(block))
 
 
-def attend_kernel(q_ref, k_ref, v_ref, out):
+def fetched(pack, places, blocks, sems):
+    copies = []
+    for i, place in enumerate(places):
+        width = place.shape[1]
+        start = blocks[i]
+        copies.append(
+            pltpu.make_async_copy(pack.at[:, pl.ds(start, width)], place, sems.at[i])
+        )
+        copies[-1].start()
+    return [copy.wait for copy in copies]
+
+
+def unit_rows(values):
+    scale = lax.rsqrt(jnp.mean(values * values, axis=1, keepdims=True) + epsilon)
+    return values * scale, scale
+
+
+def norm_back(grad, gain, unit, scale):
+    scaled = grad * gain
+    return scale * (scaled - unit * jnp.mean(scaled * unit, axis=1, keepdims=True))
+
+
+WEIGHT_STEP = 256
+
+
+def attend_pairs(qkv, mixed):
     causal = patch_causal()
-    for first in range(0, q_ref.shape[0], BYTE_BLOCK):
-        rows = pl.ds(first, BYTE_BLOCK)
-        q, k, v = q_ref[rows, :], k_ref[rows, :], v_ref[rows, :]
-        mixed = jnp.zeros(q.shape, FULL)
-        for half in range(2):
-            probs = head_probs(of_head(q, half), k, causal)
-            mixed += nn(probs.astype(LOW), of_head(v, half))
-        out[rows, :] = mixed.astype(LOW)
-
-
-def attend_back_kernel(q_ref, k_ref, v_ref, g_ref, dq_out, dk_out, dv_out):
+    blocks = qkv.shape[0] // BYTE_BLOCK
+
+    def pair(i, carry):
+        def lanes(part):
+            start = part * D + i * (2 * HEAD_A)
+            return pl.ds(pl.multiple_of(start, 2 * HEAD_A), 2 * HEAD_A)
+
+        for block in range(blocks):
+            rows = pl.ds(block * BYTE_BLOCK, BYTE_BLOCK)
+            q, k, v = qkv[rows, lanes(0)], qkv[rows, lanes(1)], qkv[rows, lanes(2)]
+            total = jnp.zeros(q.shape, FULL)
+            for half in range(2):
+                probs = head_probs(of_head(q, half), k, causal)
+                total += nn(probs.astype(LOW), of_head(v, half))
+            mixed[rows, lanes(0)] = total.astype(LOW)
+        return carry
+
+    lax.fori_loop(0, HEADS_A // 2, pair, 0)
+
+
+def attend_pairs_back(qkv, heads_grad, qkv_grad):
     causal = patch_causal()
+    blocks = qkv.shape[0] // BYTE_BLOCK
     scale = HEAD_A ** (-0.5)
-    for first in range(0, q_ref.shape[0], BYTE_BLOCK):
-        rows = pl.ds(first, BYTE_BLOCK)
-        q, k, v, g = q_ref[rows, :], k_ref[rows, :], v_ref[rows, :], g_ref[rows, :]
-        dq = jnp.zeros(q.shape, FULL)
-        dk = jnp.zeros(q.shape, FULL)
-        dv = jnp.zeros(q.shape, FULL)
-        for half in range(2):
-            own_q, own_k, own_g = of_head(q, half), of_head(k, half), of_head(g, half)
-            probs = head_probs(own_q, k, causal)
-            dprobs = nt(own_g, v)
-            dv += tn(probs.astype(LOW), own_g)
-            dscores = probs * (dprobs - jnp.sum(probs * dprobs, axis=1, keepdims=True))
-            dscores = dscores.astype(LOW)
-            dq += nn(dscores, own_k)
-            dk += tn(dscores, own_q)
-        dq_out[rows, :] = (dq * scale).astype(LOW)
-        dk_out[rows, :] = (dk * scale).astype(LOW)
-        dv_out[rows, :] = dv.astype(LOW)
-
-
-def attend_heads(qkv):
-    rows = qkv.shape[0]
-    pairs = HEADS_A // 2
-
-    def spec(offset):
-        return pl.BlockSpec((rows, 2 * HEAD_A), lambda i: (0, i + offset))
+
+    def pair(i, carry):
+        def lanes(part):
+            start = part * D + i * (2 * HEAD_A)
+            return pl.ds(pl.multiple_of(start, 2 * HEAD_A), 2 * HEAD_A)
+
+        for block in range(blocks):
+            rows = pl.ds(block * BYTE_BLOCK, BYTE_BLOCK)
+            q, k, v = qkv[rows, lanes(0)], qkv[rows, lanes(1)], qkv[rows, lanes(2)]
+            g = heads_grad[rows, lanes(0)]
+            dq = jnp.zeros(q.shape, FULL)
+            dk = jnp.zeros(q.shape, FULL)
+            dv = jnp.zeros(q.shape, FULL)
+            for half in range(2):
+                own_q, own_k, own_g = of_head(q, half), of_head(k, half), of_head(g, half)
+                probs = head_probs(own_q, k, causal)
+                dprobs = nt(own_g, v)
+                dv += tn(probs.astype(LOW), own_g)
+                dscores = probs * (dprobs - jnp.sum(probs * dprobs, axis=1, keepdims=True))
+                dscores = dscores.astype(LOW)
+                dq += nn(dscores, own_k)
+                dk += tn(dscores, own_q)
+            qkv_grad[rows, lanes(0)] = (dq * scale).astype(LOW)
+            qkv_grad[rows, lanes(1)] = (dk * scale).astype(LOW)
+            qkv_grad[rows, lanes(2)] = dv.astype(LOW)
+        return carry
+
+    lax.fori_loop(0, HEADS_A // 2, pair, 0)
+
+
+def bytes_forward_kernel(
+    u_blocks,
+    mixed_in,
+    gains,
+    gated_gain,
+    pack,
+    gated_out,
+    local_out,
+    stream_out,
+    normed_out,
+    qkv,
+    mixed,
+    after_out,
+    feed_out,
+    w_out0,
+    w_out1,
+    w_local,
+    w_q,
+    w_k,
+    w_v,
+    w_attn,
+    pieces,
+    sems,
+):
+    places = (w_out0, w_out1, w_local, w_q, w_k, w_v, w_attn)
+    blocks = [4 * D, 5 * D, 6 * D, 0, D, 2 * D, 3 * D]
+    waits = fetched(pack, places, blocks, sems)
+    patches = mixed_in.shape[0]
+    half = HEAD_M // 2
+    for i in range(2):
+        for first in range(0, HEADS_M, 4):
+            gated_out[i, :, first * half : (first + 4) * half] = jnp.concatenate(
+                [
+                    u_blocks[first + j].astype(FULL)[:, i * half : (i + 1) * half]
+                    for j in range(4)
+                ],
+                axis=1,
+            )
+    held = [gated_out[0], gated_out[1]]
+    square = sum(jnp.sum(v * v, axis=1, keepdims=True) for v in held)
+    scale = lax.rsqrt(square / (2 * D) + epsilon)
+    gated = [(held[i] * scale * gated_gain[i : i + 1, :]).astype(LOW) for i in range(2)]
+    waits[0]()
+    waits[1]()
+    joined = mixed_in[...] + nn(gated[0], w_out0[...]) + nn(gated[1], w_out1[...])
+    for k in range(PATCH):
+        pieces[pl.ds(k, patches, stride=PATCH), :] = joined[:, k * EMB : (k + 1) * EMB]
+    local = pieces[...].astype(LOW)
+    local_out[...] = local
+    waits[2]()
+    stream = nt(local, w_local[...])
+    stream_out[...] = stream
+    normed = (unit_rows(stream)[0] * gains[0:1, :]).astype(LOW)
+    normed_out[...] = normed
+    for i, weight in enumerate((w_q, w_k, w_v)):
+        waits[3 + i]()
+        for first in range(0, D, WEIGHT_STEP):
+            qkv[:, i * D + first : i * D + first + WEIGHT_STEP] = nn(
+                normed, weight[:, first : first + WEIGHT_STEP]
+            ).astype(LOW)
+    attend_pairs(qkv, mixed)
+    waits[6]()
+    heads = mixed[...]
+    for first in range(0, D, WEIGHT_STEP):
+        columns = slice(first, first + WEIGHT_STEP)
+        after_out[:, columns] = stream_out[:, columns] + nn(heads, w_attn[:, columns])
+    feed_out[...] = (unit_rows(after_out[...])[0] * gains[1:2, :]).astype(LOW)
+
+
+def bytes_forward(u_blocks, mixed_in, gains, gated_gain, pack):
+    patches = mixed_in.shape[0]
+    rows = patches * PATCH
+
+    def full(shape, kind):
+        return jax.ShapeDtypeStruct(shape, kind)
 
     return pl.pallas_call(
-        attend_kernel,
-        grid=(pairs,),
-        out_shape=jax.ShapeDtypeStruct((rows, D), LOW),
-        in_specs=[spec(0), spec(pairs), spec(2 * pairs)],
-        out_specs=spec(0),
-        name="attend",
-    )(qkv, qkv, qkv)
-
-
-def attend_heads_back(qkv, heads_grad):
-    rows = qkv.shape[0]
-    pairs = HEADS_A // 2
-
-    def spec(offset):
-        return pl.BlockSpec((rows, 2 * HEAD_A), lambda i: (0, i + offset))
+        bytes_forward_kernel,
+        out_shape=[
+            full((2, patches, D), FULL),
+            full((rows, EMB), LOW),
+            full((rows, D), FULL),
+            full((rows, D), LOW),
+            full((rows, 3 * D), LOW),
+            full((rows, D), LOW),
+            full((rows, D), FULL),
+            full((rows, D), LOW),
+        ],
+        in_specs=[in_vmem()] * 4 + [pl.BlockSpec(memory_space=pl.ANY)],
+        out_specs=[in_vmem()] * 8,
+        scratch_shapes=[pltpu.VMEM((D, D), LOW)] * 2
+        + [pltpu.VMEM((D, EMB), LOW)]
+        + [pltpu.VMEM((D, D), LOW)] * 4
+        + [pltpu.VMEM((rows, EMB), FULL), pltpu.SemaphoreType.DMA((7,))],
+        compiler_params=pltpu.CompilerParams(vmem_limit_bytes=48 << 20),
+        name="bytes_forward",
+    )(u_blocks, mixed_in, gains, gated_gain, pack)
+
+
+def bytes_backward_kernel(
+    narrow,
+    feed_in_grad,
+    cotangent,
+    keep,
+    after,
+    stream_in,
+    normed_in,
+    qkv,
+    mixed,
+    local_in,
+    gated_rows,
+    gains,
+    gated_gain,
+    pack,
+    feed_parts,
+    global_out,
+    scale_out,
+    sums,
+    gain_grads,
+    gated_gain_grads,
+    du_blocks,
+    rows_out,
+    w_attn,
+    w_q,
+    w_k,
+    w_v,
+    w_local,
+    w_out0,
+    w_out1,
+    after_grad,
+    heads_grad,
+    qkv_grad,
+    pieces,
+    parts_got,
+    grads,
+    grads_got,
+    sems,
+    p_send,
+    p_recv,
+    t_send,
+    t_recv,
+):
+    n, wide_place = lax.axis_index(NARROW), lax.axis_index(WIDE)
+    core = lax.rem(wide_place, 2)
+    twin = (n, wide_place + 1 - 2 * core)
+    barrier = pltpu.get_barrier_semaphore()
+    pl.semaphore_signal(barrier, inc=1, device_id=twin, device_id_type=MESH)
+    for k in range(1, narrow):
+        peer = (lax.rem(n + k, narrow), wide_place)
+        pl.semaphore_signal(barrier, inc=1, device_id=peer, device_id_type=MESH)
+
+    def twin_copy(i, columns):
+        return remote(
+            grads.at[:, 1 - core, :, columns],
+            grads_got.at[:, :, columns],
+            t_send.at[i],
+            t_recv.at[i],
+            twin,
+        )
+
+    def give(i, columns, part):
+        grads[:, :, :, columns] = part.astype(LOW).reshape(grads.shape[:3] + part.shape[1:])
+        twin_copy(i, columns).start()
+
+    def part_copy(k):
+        peer = (lax.rem(n + k, narrow), wide_place)
+        return remote(feed_parts.at[k], parts_got.at[k], p_send.at[k - 1], p_recv.at[k - 1], peer)
+
+    own_part = pltpu.make_async_copy(feed_parts.at[0], parts_got.at[0], sems.at[7])
+    own_part.start()
+    places = (w_attn, w_q, w_k, w_v, w_local, w_out0, w_out1)
+    blocks = [3 * D, 0, D, 2 * D, 6 * D, 4 * D, 5 * D]
+    waits = fetched(pack, places, blocks, sems)
+    pl.semaphore_wait(barrier, narrow)
+    for k in range(1, narrow):
+        part_copy(k).start()
+    patches = global_out.shape[0]
+    unit, scale = unit_rows(after[...])
+    grad = feed_in_grad[...].astype(LOW).astype(FULL)
+    gain_grads[1:2, :] = jnp.sum(grad * unit, axis=0, keepdims=True)
+    after_grad[...] = cotangent[...].astype(FULL) * keep[...] + norm_back(
+        grad, gains[1:2, :], unit, scale
+    )
+    attn_grad = after_grad[...].astype(LOW)
+    waits[0]()
+    for first in range(0, D, WEIGHT_STEP):
+        columns = slice(first, first + WEIGHT_STEP)
+        heads_grad[:, columns] = nt(attn_grad, w_attn[columns, :]).astype(LOW)
+        give(
+            (3 * D + first) // WEIGHT_STEP,
+            pl.ds(3 * D + first, WEIGHT_STEP),
+            tn(mixed[...], attn_grad[:, columns]),
+        )
+    attend_pairs_back(qkv, heads_grad, qkv_grad)
+    normed_grad = jnp.zeros(after_grad.shape, FULL)
+    for i, weight in enumerate((w_q, w_k, w_v)):
+        waits[1 + i]()
+        normed_grad += nt(qkv_grad[:, i * D : (i + 1) * D], weight[...])
+    unit, scale = unit_rows(stream_in[...])
+    gain_grads[0:1, :] = jnp.sum(normed_grad * unit, axis=0, keepdims=True)
+    stream_grad = (after_grad[...] + norm_back(normed_grad, gains[0:1, :], unit, scale)).astype(LOW)
+    waits[4]()
+    pieces[...] = nn(stream_grad, w_local[...])
+    for k in range(PATCH):
+        global_out[:, k * EMB : (k + 1) * EMB] = pieces[pl.ds(k, patches, stride=PATCH), :]
+    mix_grad = global_out[...].astype(LOW)
+    waits[5]()
+    waits[6]()
+    inner = [nt(mix_grad, w_out0[...]), nt(mix_grad, w_out1[...])]
+    held = [gated_rows[0], gated_rows[1]]
+    square = sum(jnp.sum(v * v, axis=1, keepdims=True) for v in held)
+    scale = lax.rsqrt(square / (2 * D) + epsilon)
+    units = [v * scale for v in held]
+    scaled = [inner[i] * gated_gain[i : i + 1, :] for i in range(2)]
+    mean = sum(jnp.sum(scaled[i] * units[i], axis=1, keepdims=True) for i in range(2)) / (2 * D)
+    for i in range(2):
+        gated_gain_grads[i : i + 1, :] = jnp.sum(inner[i] * units[i], axis=0, keepdims=True)
+    scale_out[...] = jnp.broadcast_to(scale, scale_out.shape)
+    rows_grads = [scale * (scaled[i] - units[i] * mean) for i in range(2)]
+    half = HEAD_M // 2
+    for head in range(HEADS_M):
+        lanes = slice(head * half, (head + 1) * half)
+        du_blocks[head] = jnp.concatenate([part[:, lanes] for part in rows_grads], axis=1).astype(LOW)
+    give(4 * D // WEIGHT_STEP, pl.ds(4 * D, EMB), tn(stream_grad, local_in[...]))
+
+    def weight_grads(i, carry):
+        columns = pl.ds(pl.multiple_of(i * WEIGHT_STEP, WEIGHT_STEP), WEIGHT_STEP)
+        give(i, columns, tn(normed_in[...], qkv_grad[:, columns]))
+        return carry
+
+    lax.fori_loop(0, 3 * D // WEIGHT_STEP, weight_grads, 0)
+    own_part.wait()
+    for k in range(1, narrow):
+        part_copy(k).wait_recv()
+    for first in range(0, D, WEIGHT_STEP):
+        columns = slice(first, first + WEIGHT_STEP)
+        feed = parts_got[0, :, columns].astype(FULL)
+        for k in range(1, narrow):
+            feed += parts_got[k, :, columns].astype(FULL)
+        feed = feed.astype(LOW).astype(FULL)
+        rows_out[:, columns] = ((after[:, columns] + feed) * keep[...]).astype(LOW)
+
+    def add_twin(i, columns):
+        twin_copy(i, columns).wait_recv()
+        sums[:, :, columns] = (
+            grads[:, core, :, columns].astype(FULL) + grads_got[:, :, columns].astype(FULL)
+        ).astype(LOW)
+
+    def add_one(i, carry):
+        add_twin(i, pl.ds(pl.multiple_of(i * WEIGHT_STEP, WEIGHT_STEP), WEIGHT_STEP))
+        return carry
+
+    def end_one(i, carry):
+        twin_copy(i, pl.ds(pl.multiple_of(i * WEIGHT_STEP, WEIGHT_STEP), WEIGHT_STEP)).wait_send()
+        return carry
+
+    steps = 4 * D // WEIGHT_STEP
+    add_twin(steps, pl.ds(4 * D, EMB))
+    lax.fori_loop(0, steps, add_one, 0)
+    twin_copy(steps, pl.ds(4 * D, EMB)).wait_send()
+    lax.fori_loop(0, steps, end_one, 0)
+    for k in range(1, narrow):
+        part_copy(k).wait_send()
+
+
+def bytes_backward(
+    feed_in_grad,
+    cotangent,
+    keep,
+    after,
+    stream,
+    normed,
+    qkv,
+    mixed,
+    local,
+    gated_rows,
+    gains,
+    gated_gain,
+    pack,
+    feed_parts,
+    collective_id,
+):
+    narrow = feed_parts.shape[0]
+    every = 4 * D + EMB
+    rows = after.shape[0]
+    patches = rows // PATCH
+
+    def full(shape, kind):
+        return jax.ShapeDtypeStruct(shape, kind)
 
     return pl.pallas_call(
-        attend_back_kernel,
-        grid=(pairs,),
-        out_shape=[jax.ShapeDtypeStruct((rows, D), LOW)] * 3,
-        in_specs=[spec(0), spec(pairs), spec(2 * pairs), spec(0)],
-        out_specs=[spec(0)] * 3,
-        name="attend_back",
-    )(qkv, qkv, qkv, heads_grad)
+        partial(bytes_backward_kernel, narrow),
+        out_shape=[
+            full((patches, D), FULL),
+            full((patches, 128), FULL),
+            full((HEADS_M // 2, D // HEADS_M, every), LOW),
+            full((2, D), FULL),
+            full((2, D), FULL),
+            full((HEADS_M, patches, HEAD_M), LOW),
+            full((rows, D), LOW),
+        ],
+        in_specs=[in_vmem()] * 12 + [pl.BlockSpec(memory_space=pl.ANY)] * 2,
+        out_specs=[in_vmem()] * 7,
+        scratch_shapes=[pltpu.VMEM((D, D), LOW)] * 4
+        + [pltpu.VMEM((D, EMB), LOW)]
+        + [pltpu.VMEM((D, D), LOW)] * 2
+        + [
+            pltpu.VMEM((rows, D), FULL),
+            pltpu.VMEM((rows, D), LOW),
+            pltpu.VMEM((rows, 3 * D), LOW),
+            pltpu.VMEM((rows, EMB), FULL),
+            pltpu.VMEM((narrow, rows, D), LOW),
+            pltpu.VMEM((HEADS_M // 2, 2, D // HEADS_M, every), LOW),
+            pltpu.VMEM((HEADS_M // 2, D // HEADS_M, every), LOW),
+            pltpu.SemaphoreType.DMA((8,)),
+            pltpu.SemaphoreType.DMA((narrow - 1,)),
+            pltpu.SemaphoreType.DMA((narrow - 1,)),
+            pltpu.SemaphoreType.DMA((4 * D // WEIGHT_STEP + 1,)),
+            pltpu.SemaphoreType.DMA((4 * D // WEIGHT_STEP + 1,)),
+        ],
+        compiler_params=pltpu.CompilerParams(
+            collective_id=collective_id, has_side_effects=True, vmem_limit_bytes=56 << 20
+        ),
+        name="bytes_backward",
+    )(
+        feed_in_grad,
+        cotangent,
+        keep,
+        after,
+        stream,
+        normed,
+        qkv,
+        mixed,
+        local,
+        gated_rows,
+        gains,
+        gated_gain,
+        pack,
+        feed_parts,
+    )
 
 
 def feed_kernel(
@@ -964,9 +1649,13 @@
 ):
     g_ins = refs[:narrow]
     w_in, f_out, gx_out, grads, w, x, g, hid, gg, gu, sent, got = refs[narrow : narrow + 12]
-    w_sem, g_sem, x_sem, x_send, x_recv, r_send, r_recv = refs[narrow + 12 :]
-    n, wide_place = lax.axis_index("narrow"), lax.axis_index("wide")
+    twin_out, twin_got = refs[narrow + 12 : narrow + 14]
+    w_sem, g_sem, x_sem, x_send, x_recv, r_send, r_recv, t_send, t_recv = refs[narrow + 14 :]
+    n, wide_place = lax.axis_index(NARROW), lax.axis_index(WIDE)
+    core = lax.rem(wide_place, 2)
+    twin = (n, wide_place + 1 - 2 * core)
     barrier = pltpu.get_barrier_semaphore()
+    pl.semaphore_signal(barrier, inc=1, device_id=twin, device_id_type=MESH)
     for k in range(1, narrow):
         peer = (lax.rem(n + k, narrow), wide_place)
         pl.semaphore_signal(barrier, inc=1, device_id=peer, device_id_type=MESH)
@@ -979,7 +1668,7 @@
         copy.start()
     for copy in g_copies[1:]:
         copy.start()
-    pl.semaphore_wait(barrier, narrow - 1)
+    pl.semaphore_wait(barrier, narrow)
 
     def x_copy(k):
         return pltpu.make_async_remote_copy(
@@ -1057,22 +1746,48 @@
 
     lax.fori_loop(0, narrow, block, 0)
 
-    def weight_grads(place, carry):
+    depth = places // 2
+
+    def weight_grads(place, i, first, columns):
+        left, right = ((gg, x), (gu, x), (hid, g))[i]
         units = pl.ds(pl.multiple_of(place * share, share), share)
-        for i, (left, right) in enumerate(((gg, x), (gu, x), (hid, g))):
-            lhs = left[:, :, units].reshape(narrow * rows, share)
+        lhs = left[:, :, units].reshape(narrow * rows, share)
+        rhs = right[:, :, first : first + columns].reshape(narrow * rows, columns)
+        return tn(lhs, rhs)
+
+    def t_copy(j):
+        return remote(twin_out.at[j], twin_got.at[j], t_send.at[j], t_recv.at[j], twin)
+
+    def for_twin(j, carry):
+        for i in range(3):
             for first in range(0, width, 2 * chunk):
-                rhs = right[:, :, first : first + 2 * chunk].reshape(narrow * rows, 2 * chunk)
-                grads[place, i, :, first : first + 2 * chunk] = tn(lhs, rhs).astype(LOW)
+                twin_out[j, i, :, first : first + 2 * chunk] = weight_grads(
+                    2 * j + 1 - core, i, first, 2 * chunk
+                ).astype(LOW)
+        t_copy(j).start()
         return carry
 
-    lax.fori_loop(0, places, weight_grads, 0)
+    def for_own(j, carry):
+        t_copy(j).wait_recv()
+        for i in range(3):
+            for first in range(0, width, 2 * chunk):
+                columns = slice(first, first + 2 * chunk)
+                part = weight_grads(2 * j + core, i, first, 2 * chunk)
+                grads[j, i, :, columns] = (
+                    part + twin_got[j, i, :, columns].astype(FULL)
+                ).astype(LOW)
+        return carry
+
+    lax.fori_loop(0, depth, for_twin, 0)
+    lax.fori_loop(0, depth, for_own, 0)
     for k in range(1, narrow):
         r_copy(k).wait_recv()
         gx_out[...] += got[k - 1].astype(FULL)
     for k in range(1, narrow):
         x_copy(k).wait_send()
         r_copy(k).wait_send()
+    for j in range(depth):
+        t_copy(j).wait_send()
 
 
 def feed_forward_back(x_own, g_blocks, feed_all, collective_id):
@@ -1091,7 +1806,7 @@
         out_shape=[
             jax.ShapeDtypeStruct((narrow, rows, width), LOW),
             jax.ShapeDtypeStruct((rows, width), FULL),
-            jax.ShapeDtypeStruct(feed_all.shape, LOW),
+            jax.ShapeDtypeStruct((places // 2,) + feed_all.shape[1:], LOW),
         ],
         in_specs=[anywhere] * (narrow + 2),
         out_specs=[in_vmem()] * 3,
@@ -1104,6 +1819,8 @@
             rows_scratch(narrow, hidden),
             rows_scratch(narrow - 1, width),
             rows_scratch(narrow - 1, width),
+            pltpu.VMEM((places // 2,) + feed_all.shape[1:], LOW),
+            pltpu.VMEM((places // 2,) + feed_all.shape[1:], LOW),
             dma((3,)),
             dma((narrow,)),
             dma,
@@ -1111,9 +1828,11 @@
             dma((narrow - 1,)),
             dma((narrow - 1,)),
             dma((narrow - 1,)),
+            dma((places // 2,)),
+            dma((places // 2,)),
         ],
         compiler_params=pltpu.CompilerParams(
-            collective_id=collective_id, has_side_effects=True, vmem_limit_bytes=56 << 20
+            collective_id=collective_id, has_side_effects=True, vmem_limit_bytes=58 << 20
         ),
         name="feed",
     )(x_own, *g_blocks, feed_all)
@@ -1146,7 +1865,7 @@
     down_weight,
     cotangent,
 ):
-    narrow, wide = lax.axis_size("narrow"), lax.axis_size("wide")
+    narrow, wide = lax.axis_size(NARROW), lax.axis_size(WIDE)
     devices = narrow * wide
     device = lax.axis_index(BOTH)
     rows = byte_ids.shape[0]
@@ -1214,9 +1933,8 @@
         ],
         axis=1,
     )
-    feed_turned = exchange(feed_blocks, "narrow").transpose(1, 2, 0, 3).reshape(3, share, D)
-    feed_all = lax.all_gather(feed_turned, "wide")
-    in_all = lax.all_gather(in_weight, BOTH, axis=0, tiled=True)
+    feed_turned = exchange(feed_blocks, NARROW).transpose(1, 2, 0, 3).reshape(3, share, D)
+    feed_all = lax.all_gather(feed_turned, WIDE)
 
     patch_all = start_all[:, :D]
     bcdt_weight = start_all[:, D : D + bcdt_width]
@@ -1251,91 +1969,75 @@
     mixer_args = (numbers, xz, bc, dt, marks, conv_x, bias_x, conv_bc, bias_bc)
     u, y, states = mixer_forward(*mixer_args)
     u_blocks = exchange(u.astype(LOW).reshape(devices, patches, HEAD_M), BOTH)
-    gated_rows = u_blocks.transpose(1, 0, 2).reshape(patches, DI).astype(FULL)
-    gated_scale = lax.rsqrt(jnp.mean(gated_rows * gated_rows, axis=-1, keepdims=True) + epsilon)
-    gated_low = (gated_rows * gated_scale * gated_gain).astype(LOW)
-
-    out_all = (
-        middle_all[:, 4 * D : 6 * D]
-        .reshape(devices, own_rows, 2, D)
-        .transpose(0, 2, 1, 3)
-        .reshape(DI, D)
-    )
-    local_all = middle_all[:, 6 * D :]
-    qkv_all = middle_all[:, : 3 * D]
-    attn_all = middle_all[:, 3 * D : 4 * D]
-    global_out = mixed_in + jnp.dot(gated_low, out_all, preferred_element_type=FULL)
-
-    local_rows = global_out.astype(LOW).reshape(rows, EMB)
-    stream = nt(local_rows, local_all)
-    normed_attn = root_norm(stream, gain_attn).astype(LOW)
-    qkv = jnp.dot(normed_attn, qkv_all, preferred_element_type=FULL).astype(LOW)
-    mixed_heads = attend_heads(qkv)
-    after_attn = stream + jnp.dot(mixed_heads, attn_all, preferred_element_type=FULL)
-    normed_feed = root_norm(after_attn, feed_gain).astype(LOW)
-    out_grad = cotangent.astype(FULL) * keep_rows[:, None]
-    feed_grad = out_grad.astype(LOW)
+    half = HEAD_M // 2
+    gated_gain_split = gated_gain.reshape(devices, 2, half).transpose(1, 0, 2).reshape(2, D)
+
+    byte_gains = jnp.stack([gain_attn, feed_gain])
+    (
+        gated_rows,
+        local_rows,
+        stream,
+        normed_attn,
+        qkv,
+        mixed_heads,
+        after_attn,
+        normed_feed,
+    ) = bytes_forward(u_blocks, mixed_in, byte_gains, gated_gain_split, middle_all)
+    feed_grad = (cotangent.astype(FULL) * keep_rows[:, None]).astype(LOW)
 
     def passed_narrow(values, by):
         pairs = [(i, (i + by) % narrow) for i in range(narrow)]
-        return lax.ppermute(values, "narrow", pairs)
+        return lax.ppermute(values, NARROW, pairs)
 
     g_blocks = [feed_grad] + [passed_narrow(feed_grad, narrow - k) for k in range(1, narrow)]
     feed_parts, feed_in_grad, feed_grads = feed_forward_back(normed_feed, g_blocks, feed_all, 2)
-    feed_out = feed_parts[0].astype(FULL)
-    for k in range(1, narrow):
-        feed_out = feed_out + passed_narrow(feed_parts[k], k).astype(FULL)
-    feed_sums = lax.psum_scatter(
-        feed_grads.reshape(-1, D), "wide", scatter_dimension=0, tiled=True
-    )
+
+    (
+        global_grad,
+        gated_scale,
+        middle_parts,
+        byte_gain_grads,
+        gated_gain_grads,
+        du_blocks,
+        out_rows,
+    ) = bytes_backward(
+        feed_in_grad,
+        cotangent,
+        keep_rows[:, None],
+        after_attn,
+        stream,
+        normed_attn,
+        qkv,
+        mixed_heads,
+        local_rows,
+        gated_rows,
+        byte_gains,
+        gated_gain_split,
+        middle_all,
+        feed_parts,
+        4,
+    )
+    middle_parts = middle_parts.reshape(narrow, wide // 2, own_rows, -1)
+    grad_gated_gain = gated_gain_grads.reshape(2, devices, half).transpose(1, 0, 2).reshape(DI)
+    grad_gain_attn, grad_feed_gain = byte_gain_grads[0], byte_gain_grads[1]
+
+    mix_grad = global_grad.astype(LOW)
+    bcdt_padded = start_all[:, D : D + 3 * STATE]
+    dwx, dwbc, dnumbers, rows_grad, xz_grads, feed_sums, middle_sums = mixer_backward(
+        *mixer_args,
+        y,
+        states,
+        normed_all,
+        xz_weight,
+        bcdt_padded,
+        du_blocks,
+        feed_grads,
+        middle_parts,
+        3,
+    )
+    normed_mix_grad, bcdt_grads = rows_grad[:, :D], rows_grad[:, D:]
     feed_sums = feed_sums.reshape(3, share, narrow, D // narrow).transpose(2, 0, 1, 3)
-    feed_sums = exchange(feed_sums, "narrow").transpose(1, 0, 2, 3).astype(FULL)
-    feed_sums = feed_sums.reshape(3, hidden_width, D // narrow)
-    grad_gate, grad_up, grad_down = feed_sums[0].T, feed_sums[1].T, feed_sums[2]
-    out_rows = ((after_attn + feed_out.astype(LOW).astype(FULL)) * keep_rows[:, None]).astype(LOW)
-
-    _, feed_norm_back = jax.vjp(root_norm, after_attn, feed_gain)
-    after_norm_grad, grad_feed_gain = feed_norm_back(feed_in_grad.astype(LOW).astype(FULL))
-    after_grad = out_grad + after_norm_grad
-    attn_grad = after_grad.astype(LOW)
-    heads_grad = nt(attn_grad, attn_all).astype(LOW)
-    query_grad, key_grad, value_grad = attend_heads_back(qkv, heads_grad)
-    qkv_grad = jnp.concatenate([query_grad, key_grad, value_grad], axis=1)
-    normed_grad = nt(qkv_grad, qkv_all)
-    _, attn_norm_back = jax.vjp(root_norm, stream, gain_attn)
-    stream_norm_grad, grad_gain_attn = attn_norm_back(normed_grad)
-    stream_grad = (after_grad + stream_norm_grad).astype(LOW)
-    middle_grads = jnp.concatenate(
-        [tn(normed_attn, qkv_grad), tn(mixed_heads, attn_grad), tn(stream_grad, local_rows)], axis=1
-    ).astype(LOW)
-    middle_sums = lax.psum_scatter(middle_grads, BOTH, scatter_dimension=0, tiled=True).astype(FULL)
-    global_grad = nn(stream_grad, local_all).reshape(patches, D)
-
-    mix_grad = global_grad.astype(LOW)
-    gated_grad = nt(mix_grad, out_all)
-    _, gated_back = jax.vjp(root_norm, gated_rows, gated_gain)
-    gated_rows_grad, grad_gated_gain = gated_back(gated_grad)
-    du_blocks = gated_rows_grad.astype(LOW).reshape(patches, devices, HEAD_M).transpose(1, 0, 2)
-    du = exchange(du_blocks, BOTH).reshape(everything, HEAD_M)
-    dxz, dbc, ddt, dwx, dwbc, dnumbers = mixer_backward(*mixer_args, y, states, du)
-    grad_xz = tn(normed_all, dxz).astype(LOW).reshape(devices, own_rows, 2 * HEAD_M)
-    grad_xz = exchange(grad_xz, BOTH).astype(FULL).transpose(1, 0, 2)
-    proj_blocks = jnp.concatenate(
-        [dxz, dbc, jnp.pad(ddt.astype(LOW), ((0, 0), (0, 127)))], axis=1
-    ).reshape(devices, patches, 4 * STATE)
-    proj_blocks = exchange(proj_blocks, BOTH)
-    xz_grad = proj_blocks[:, :, :STATE].transpose(1, 0, 2)
-    bc_grad = jnp.sum(proj_blocks[:, :, STATE : 3 * STATE].astype(FULL), axis=0).astype(LOW)
-    bcdt_grad = jnp.concatenate([bc_grad, proj_blocks[:, :, 3 * STATE].T], axis=1)
-    proj_low = jnp.concatenate(
-        [
-            xz_grad[:, :, HEAD_M:].reshape(patches, DI),
-            xz_grad[:, :, :HEAD_M].reshape(patches, DI),
-            bcdt_grad,
-        ],
-        axis=1,
-    )
-    normed_mix_grad = nt(proj_low, in_all)
+    grad_xz = xz_grads.astype(FULL).transpose(1, 0, 2)
     _, mix_norm_back = jax.vjp(root_norm, mixed_in, gain_mix)
     mixed_norm_grad, grad_gain_mix = mix_norm_back(normed_mix_grad)
     embed_grad = (global_grad + mixed_norm_grad).astype(LOW)
@@ -1344,8 +2046,7 @@
         [
             embed_grad,
             mix_grad,
-            jnp.pad(bcdt_grad, ((0, 0), (0, 96))),
-            jnp.broadcast_to(gated_scale.astype(LOW), (patches, 128)),
+            gated_scale.astype(LOW),
         ],
         axis=1,
     )
@@ -1362,21 +2063,22 @@
     )
     sums_width = -(-sums_pack.shape[0] // 1024) * 1024
     sums_pack = jnp.pad(sums_pack, (0, sums_width - sums_pack.shape[0])).reshape(-1, 128)
-    end_all, sums_all = gather_all([end_pack, sums_pack], 1)
+    end_all, sums_all, middle_sums, feed_sums = gather_all(
+        [end_pack, sums_pack], 1, middle_sums, feed_sums
+    )
+    feed_sums = feed_sums.transpose(1, 0, 2, 3).astype(FULL).reshape(3, hidden_width, D // narrow)
+    grad_gate, grad_up, grad_down = feed_sums[0].T, feed_sums[1].T, feed_sums[2]
     sums_all = sums_all.reshape(devices, sums_width)
     embed_grad_all = end_all[:, :D]
     mix_grad_all = end_all[:, D : 2 * D]
-    bcdt_grad_all = end_all[:, 2 * D : 2 * D + bcdt_width]
-    scale_all = end_all[:, 2 * D + 384 : 2 * D + 385].astype(FULL)
+    scale_all = end_all[:, 2 * D : 2 * D + 1].astype(FULL)
     gain_own = lax.dynamic_slice_in_dim(gated_gain, device * HEAD_M, HEAD_M)
     grad_out = tn((u * scale_all * gain_own).astype(LOW), mix_grad_all)
-    normed_own = lax.dynamic_slice_in_dim(normed_all, device * own_rows, own_rows, axis=1)
-    grad_bcdt = tn(normed_own, bcdt_grad_all)
     grad_in = jnp.concatenate(
         [
             grad_xz[:, :, HEAD_M:].reshape(own_rows, DI),
             grad_xz[:, :, :HEAD_M].reshape(own_rows, DI),
-            grad_bcdt,
+            bcdt_grads[:, :bcdt_width],
         ],
         axis=1,
     )
@@ -1433,59 +2135,59 @@
 
 def solution(mesh):
     placed = (
-        P(("narrow", "wide")),
+        P((NARROW, WIDE)),
         P(),
         P(),
-        P(("narrow", "wide"), None),
-        P(("narrow", "wide"), None),
+        P((NARROW, WIDE), None),
+        P((NARROW, WIDE), None),
         P(),
-        P(("narrow", "wide"), None),
+        P((NARROW, WIDE), None),
         P(),
         P(),
         P(),
         P(),
         P(),
         P(),
-        P(("narrow", "wide"), None),
-        P(None, ("narrow", "wide")),
+        P((NARROW, WIDE), None),
+        P(None, (NARROW, WIDE)),
         P(),
-        P(("narrow", "wide"), None),
-        P(("narrow", "wide"), None),
-        P(("narrow", "wide"), None),
-        P(("narrow", "wide"), None),
+        P((NARROW, WIDE), None),
+        P((NARROW, WIDE), None),
+        P((NARROW, WIDE), None),
+        P((NARROW, WIDE), None),
         P(),
-        P("narrow", "wide"),
-        P("narrow", "wide"),
-        P("wide", "narrow"),
-        P(("narrow", "wide"), None),
+        P(NARROW, WIDE),
+        P(NARROW, WIDE),
+        P(WIDE, NARROW),
+        P((NARROW, WIDE), None),
     )
     return jax.shard_map(
         per_device_heads if mesh.size == HEADS_M else per_device_rows,
         mesh=mesh,
         in_specs=placed,
         out_specs=(
-            P(("narrow", "wide"), None),
-            P(("narrow", "wide"), None),
-            P(("narrow", "wide"), None),
+            P((NARROW, WIDE), None),
+            P((NARROW, WIDE), None),
+            P((NARROW, WIDE), None),
             P(),
-            P(("narrow", "wide"), None),
+            P((NARROW, WIDE), None),
             P(),
             P(),
             P(),
             P(),
             P(),
             P(),
-            P(("narrow", "wide"), None),
-            P(None, ("narrow", "wide")),
+            P((NARROW, WIDE), None),
+            P(None, (NARROW, WIDE)),
             P(),
-            P(("narrow", "wide"), None),
-            P(("narrow", "wide"), None),
-            P(("narrow", "wide"), None),
-            P(("narrow", "wide"), None),
+            P((NARROW, WIDE), None),
+            P((NARROW, WIDE), None),
+            P((NARROW, WIDE), None),
+            P((NARROW, WIDE), None),
             P(),
-            P("narrow", "wide"),
-            P("narrow", "wide"),
-            P("wide", "narrow"),
+            P(NARROW, WIDE),
+            P(NARROW, WIDE),
+            P(WIDE, NARROW),
         ),
         check_vma=False,
     )

time: 586 us -> 508 us (0.87)
  the two profiles are of different devices: /device:TPU:0 before, /device:TPU:9 now
where the time goes in v3:
time: 508 us; the launch traced here: 500 us
  Pallas kernels  340 us (67%)
  local copies, waits for them, and re-layouts  59.2 us (12%)
  matrix products  23.8 us (5%)
  waiting for transfers between devices  17.9 us (4%)
  between operations  16.2 us (3%)
  blocking collectives  15.7 us (3%)
  starting transfers between devices  15.4 us (3%)
  other arithmetic  11.5 us (2%)
    pallas_call x2, Pallas kernels, gather_all(): pl.pallas_call(partial(gather_kernel, count, narrow, wide // 2, last), ou...  118 us
    pallas_call x1, Pallas kernels, mixer_backward(): pl.pallas_call(partial(mixer_backward_kernel, narrow, wide), out_shape=[j...  111 us
    pallas_call x1, Pallas kernels, feed_forward_back(): pl.pallas_call(partial(feed_kernel, narrow), out_shape=[jax.ShapeDtypeStr...  51.9 us
    pallas_call x1, Pallas kernels, bytes_backward(): pl.pallas_call(partial(bytes_backward_kernel, narrow), out_shape=[full((p...  37.9 us
    unnamed x130, local copies, waits for them, and re-layouts  18.6 us
    all_gather x1, waiting for transfers between devices, per_device_heads(): feed_all = lax.all_gather(feed_turned, WIDE)  17.8 us
    all_to_all x1, blocking collectives, exchange(): return lax.all_to_all(blocks, axis, split_axis=0, concat_axis=0, tiled=True)  15.7 us
    pallas_call x1, Pallas kernels, bytes_forward(): pl.pallas_call(bytes_forward_kernel, out_shape=[full((2, patches, D), FUL...  13.4 us
  transfers between devices with their start and end apart: 7, of which 2 were waited for; matrix products, arithmetic and copies ran while one was open for 10% of the time, Pallas kernels for 15%

profile of v3, /device:TPU:9, one launch (start us, length us, event | category | flops | bytes accessed | tf_op | source)
XLA Modules:
  0.0 499.5 jit_solution(16575014305797172878)
XLA Ops:
  7.2 0.9 constant_dynamic-update-slice_fusion.4
  13.9 1.1 copy.189
  15.0 1.1 copy.190
  16.2 15.7 %all_to_all.15 = bf16[4,3,128,256]{3,2,1,0:T(8,128)(2,1)S(1)} all-to-all(bf16[4,3,128,256]{3,2,1,0:T(8,128)(2,1)S(1)} %pad_maximum_fusion), channel_id=1, replica_groups=mesh['narrow'=4,'wide'=8] {'narrow'}, dimensions={0} | all-to-all | bytes 1572864 | tf_op jit(solution)/shard_map/all_to_all | solution.py:707
  32.2 1.2 copy.192
  34.1 0.9 multiply_convert_fusion.1.refs_0_
  35.0 1.1 collective-permute-start.2
  36.4 2.2 collective-permute-start
  39.3 0.9 maximum_bitcast_fusion
  40.2 7.4 %all-to-all-start = ((bf16[32,32,128]{2,1,0:T(8,128)(2,1)}), bf16[32,32,128]{2,1,0:T(8,128)(2,1)}, u32[]{:S(2)}, u32[]{:S(2)}) async-start(bf16[32,32,128]{2,1,0:T(8,128)(2,1)} %maximum_bitcast_fusion), calls=%async_computation | async-start | bytes 524288 | tf_op jit(solution)/shard_map/all_to_all | solution.py:707
  48.6 53.4 %gather_all.2 = (bf16[4,4,2,32,1536]{4,3,2,1,0:T(8,128)(2,1)S(1)}, bf16[4,4,2,8,128]{4,3,2,1,0:T(8,128)(2,1)S(1)}) custom-call(bf16[32,1536]{1,0:T(8,128)(2,1)S(1)} %fusion.28.refs_0_, bf16[8,128]{1,0:T(8,128)(2,1)S(1)} %copy-done.27), custom_call_target="tpu_custom_call" | custom-call | tf_op jit(solution)/shard_map/gather_all/pallas_call | solution.py:691
  102.0 0.9 slice_convert_fusion
  103.0 1.6 eq.111
  104.5 5.1 %convolution_convert_fusion = bf16[8192,128]{1,0:T(8,128)(2,1)} fusion(bf16[256,128]{1,0:T(8,128)(2,1)S(1)} %bitcast.115, s32[8192]{0:T(1024)S(1)} %eq.111, bf16[8192]{0:T(1024)(128)(2,1)S(1)} %sub.35), kind=kOutput, calls=%fused_computation | convolution fusion | flops 542113792 | bytes 2211840 | tf_op jit(solution)/shard_map/dot_general | solution.py:1946
  109.7 4.2 reshape.332
  115.0 4.0 multiply_reduce_fusion
  119.8 1.2 copy-done.30
  121.0 2.1 convolution_convert_fusion.1
  125.4 1.1 slice.213.bc
  129.4 1.4 pad_maximum_fusion.4.numbers
  130.9 1.5 multiply_reduce_fusion.3
  132.6 2.5 convolution_convert_fusion.2.xz
  135.1 7.3 %mixer_forward.1 = (f32[1024,64]{1,0:T(8,128)S(1)}, f32[1024,64]{1,0:T(8,128)S(1)}, f32[8,64,128]{2,1,0:T(8,128)S(1)}) custom-call(f32[3]{0:T(128)S(1)} %pad_maximum_fusion.4.numbers, bf16[1024,128]{1,0:T(8,128)(2,1)S(1)} %convolution_convert_fusion.2.xz, bf16[1024,256]{1,0:T(8,128)(2,1)S(1)} %slice.213.bc, f32[1024,1]{1,0:T(8,128)S(1)} %dynamic-slice_convert_fusion.dt, ...), custom_call_target="tpu_custom_call" | custom-call | tf_op jit(solution)/shard_map/mixer_forward/pallas_call | solution.py:1102
  144.0 2.2 reshape.365
  146.2 4.4 all-to-all-start.1
  151.1 1.5 broadcast_in_dim_reshape.3.keep
  152.5 1.8 copy.195
  154.4 2.1 slice.215.w_bcdt
  156.5 1.7 slice.211
  159.9 1.1 reshape.366.u_blocks
  161.1 13.4 %bytes_forward.1 = (f32[2,32,1024]{2,1,0:T(8,128)S(1)}, bf16[256,128]{1,0:T(8,128)(2,1)S(1)}, f32[256,1024]{1,0:T(8,128)S(1)}, bf16[256,1024]{1,0:T(8,128)(2,1)S...) custom-call(bf16[32,32,64]{2,1,0:T(8,128)(2,1)S(1)} %reshape.366.u_b, ...), custom_call_target="tpu_custom_call" | custom-call | tf_op jit(solution)/shard_map/bytes_forward/pallas_call | solution.py:1379
  174.6 1.2 copy-done.9
  175.7 1.0 copy-done.11
  176.7 1.0 copy-done.12
  180.8 17.8 %all-gather.5.cloned.1.call-done.refs_4_ = bf16[8,3,128,1024]{3,2,1,0:T(8,128)(2,1)} async-done(((bf16[1,3,128,1024]{3,2,1,0:T(8,128)(2,1)}), bf16[8,3,128,1024]{3,2,1,0:T(8,128)(2,1)}) %all-gather.5.cloned.1.call-update) | async-done | bytes 6291472 | tf_op jit(solution)/shard_map/all_gather | solution.py:1937
  198.6 51.9 %feed.1 = (bf16[4,256,1024]{2,1,0:T(8,128)(2,1)}, f32[256,1024]{1,0:T(8,128)}, bf16[4,3,128,1024]{3,2,1,0:T(8,128)(2,1)}) custom-call(bf16[256,1024]{1,0:T(8,128)(2,1)} %copy-done.16, bf16[256,1024]{1,0:T(8,128)(2,1)} %multiply_convert_fusion.1.refs_0_, bf16[256,1024]{1,0:T(8,128)(2,1)} %collective-permute-done.refs_1_, ...), custom_call_target="tpu_custom_call" | custom-call | tf_op jit(solution)/shard_map/feed/pallas_call | solution.py:1804
  250.5 37.9 %bytes_backward.1 = (f32[32,1024]{1,0:T(8,128)}, f32[32,128]{1,0:T(8,128)}, bf16[16,32,4224]{2,1,0:T(8,128)(2,1)}, f32[2,1024]{1,0:T(2,128)}, f32[2,1024]{1,0:T(...) custom-call(f32[256,1024]{1,0:T(8,128)} %get-tuple-element.60.feed_in_grad, bf16[256,1024]{1,0:T(8,128)(2,1)} %cotangent.1, ...), custom_call_target="tpu_custom_call" | custom-call | tf_op jit(solution)/shard_map/bytes_backward/pallas_call | solution.py:1593
  288.5 111.5 %mixer_backward.1 = (f32[8,128]{1,0:T(8,128)}, f32[8,256]{1,0:T(8,128)}, f32[8,128]{1,0:T(8,128)}, f32[32,1408]{1,0:T(8,128)}, bf16[32,32,128]{2,1,0:T(8,128)(2,...) custom-call(f32[3]{0:T(128)} %copy-done.25, bf16[1024,128]{1,0:T(8,128)(2,1)} %copy-done.6, ...), custom_call_target="tpu_custom_call" | custom-call | tf_op jit(solution)/shard_map/mixer_backward/pallas_call | solution.py:1132
  403.0 1.1 multiply_reduce_fusion.1
  404.5 1.6 copy.197
  406.6 64.4 %gather_all.3 = (bf16[4,4,2,32,2176]{4,3,2,1,0:T(8,128)(2,1)S(1)}, f32[4,4,2,56,128]{4,3,2,1,0:T(8,128)S(1)}, f32[32,4224]{1,0:T(8,128)S(1)}, bf16[4,3,128,256]{3,2,1,0:T(8,128)(2,1)S(1)}) custom-call(bf16[32,2176]{1,0:T(8,128)(2,1)S(1)} %pad_maximum_fusion.2.refs_0_, f32[56,128]{1,0:T(8,128)S(1)} %pad_bitcast_fusion.refs_1_, ...), custom_call_target="tpu_custom_call" | custom-call | tf_op jit(solution)/shard_map/gather_all/pallas_call | solution.py:691
  471.0 2.4 fusion.9
  480.1 0.9 fusion.42
  481.0 1.0 copy.204
  482.0 1.0 copy.203
  483.0 3.1 fusion.3
  486.1 2.1 fusion.5
  488.3 2.3 convolution_bitcast_fusion
  (238 shorter events, 34.1 us)
Async XLA Ops:
  7.2 8.9 %copy-start.37 = (bf16[512,256]{1,0:T(8,128)(2,1)S(1)}, bf16[512,256]{1,0:T(8,128)(2,1)}, u32[]{:S(2)}) copy-start(bf16[512,256]{1,0:T(8,128)(2,1)} %param.48) | copy-start | bytes 786436
  7.2 153.9 %all-gather.3.cloned.1.call-start = ((), (), s32[]{:S(2)}) async-start(), calls=%async_computation.3 | async-start | bytes 13246464 | tf_op jit(solution)/shard_map/all_gather | solution.py:1927
  13.8 184.7 %all-gather.5.cloned.1.call-start = ((), (), s32[]{:S(2)}) async-start(), calls=%async_computation.4 | async-start | bytes 7077888 | tf_op jit(solution)/shard_map/all_gather | solution.py:1937
  32.2 6.4 %copy-start.35 = (bf16[32,4384]{1,0:T(8,128)(2,1)S(1)}, bf16[32,4384]{1,0:T(8,128)(2,1)}, u32[]{:S(2)}) copy-start(bf16[32,4384]{1,0:T(8,128)(2,1)} %param.31) | copy-start | bytes 841732
  33.8 14.3 %copy-start.41 = (bf16[1024,8]{0,1:T(8,128)(2,1)}, bf16[1024,8]{0,1:T(8,128)(2,1)S(1)}, u32[]{:S(2)}) copy-start(bf16[1024,8]{0,1:T(8,128)(2,1)S(1)} %get-tuple-element.115) | copy-start | bytes 49156
  34.0 6.2 %copy-start.38 = (f32[32,8]{1,0:T(8,128)}, f32[32,8]{1,0:T(8,128)S(1)}, u32[]{:S(2)}) copy-start(f32[32,8]{1,0:T(8,128)S(1)} %copy.188) | copy-start | bytes 3076
  35.0 12.6 %copy-start.54 = (s32[256]{0:T(256)S(1)}, s32[256]{0:T(256)}, u32[]{:S(2)}) copy-start(s32[256]{0:T(256)} %param.25) | copy-start | bytes 3076
  35.0 13.5 %slice-start.1 = ((bf16[32,4384]{1,0:T(8,128)(2,1)}), bf16[32,288]{1,0:T(8,128)(2,1)S(1)}, s32[]{:S(2)}) async-start(bf16[32,4384]{1,0:T(8,128)(2,1)} %param.31), calls=%async_computation.6 | async-start | bytes 49152 | tf_op jit(solution)/shard_map/slice | solution.py:1901
  35.0 13.5 %copy-start.40 = (bf16[32,1024]{1,0:T(8,128)(2,1)S(1)}, bf16[32,1024]{1,0:T(8,128)(2,1)}, u32[]{:S(2)}) copy-start(bf16[32,1024]{1,0:T(8,128)(2,1)} %param.29) | copy-start | bytes 196612
  35.0 145.8 %collective-permute-start.2 = (bf16[256,1024]{1,0:T(8,128)(2,1)}, bf16[256,1024]{1,0:T(8,128)(2,1)}, u32[]{:S(2)}, u32[]{:S(2)}) collective-permute-start(bf16[256,1024]{1,0:T(8,128)(2,1)} %multiply_convert_fusion.1.refs_0_), channel_id=1, source_target_pairs={{0,8},{8,16},{16,24},{24,0},{1,9},{9,17},{17,25},{25,1},{2,10},{10... | collective-permute-start | bytes 1572872 | tf_op jit(solution)/shard_map/ppermute | solution.py:1990
  36.1 144.7 %collective-permute-start.1 = (bf16[256,1024]{1,0:T(8,128)(2,1)}, bf16[256,1024]{1,0:T(8,128)(2,1)}, u32[]{:S(2)}, u32[]{:S(2)}) collective-permute-start(bf16[256,1024]{1,0:T(8,128)(2,1)} %multiply_convert_fusion.1.refs_0_), channel_id=1, source_target_pairs={{0,16},{8,24},{16,0},{24,8},{1,17},{9,25},{17,1},{25,9},{2,18},{10... | collective-permute-start | bytes 1572872 | tf_op jit(solution)/shard_map/ppermute | solution.py:1990
  36.4 144.4 %collective-permute-start = (bf16[256,1024]{1,0:T(8,128)(2,1)}, bf16[256,1024]{1,0:T(8,128)(2,1)}, u32[]{:S(2)}, u32[]{:S(2)}) collective-permute-start(bf16[256,1024]{1,0:T(8,128)(2,1)} %multiply_convert_fusion.1.refs_0_), channel_id=1, source_target_pairs={{0,24},{8,0},{16,8},{24,16},{1,25},{9,1},{17,9},{25,17},{2,26},{10... | collective-permute-start | bytes 1572872 | tf_op jit(solution)/shard_map/ppermute | solution.py:1990
  38.6 10.0 %copy-start.27 = (bf16[8,128]{1,0:T(8,128)(2,1)S(1)}, bf16[8,128]{1,0:T(8,128)(2,1)}, u32[]{:S(2)}) copy-start(bf16[8,128]{1,0:T(8,128)(2,1)} %refs_1_.1) | copy-start | bytes 6148
  40.2 92.4 %all-to-all-start = ((bf16[32,32,128]{2,1,0:T(8,128)(2,1)}), bf16[32,32,128]{2,1,0:T(8,128)(2,1)}, u32[]{:S(2)}, u32[]{:S(2)}) async-start(bf16[32,32,128]{2,1,0:T(8,128)(2,1)} %maximum_bitcast_fusion), calls=%async_computation | async-start | bytes 524288 | tf_op jit(solution)/shard_map/all_to_all | solution.py:707
  102.0 17.8 %copy-start.4 = (bf16[4,4,2,32,1536]{4,3,2,1,0:T(8,128)(2,1)}, bf16[4,4,2,32,1536]{4,3,2,1,0:T(8,128)(2,1)S(1)}, u32[]{:S(2)}) copy-start(bf16[4,4,2,32,1536]{4,3,2,1,0:T(8,128)(2,1)S(1)} %get-tuple-element.56) | copy-start | bytes 9437188
  115.0 4.3 copy-start.43
  121.0 5.4 %copy-start.56 = (f32[32]{0:T(128)S(1)}, f32[32]{0:T(128)}, u32[]{:S(2)}) copy-start(f32[32]{0:T(128)} %param.36) | copy-start | bytes 388
  121.0 6.1 %copy-start.57 = (f32[32]{0:T(128)S(1)}, f32[32]{0:T(128)}, u32[]{:S(2)}) copy-start(f32[32]{0:T(128)} %param.35) | copy-start | bytes 388
  121.0 7.4 %copy-start.58 = (f32[32]{0:T(128)S(1)}, f32[32]{0:T(128)}, u32[]{:S(2)}) copy-start(f32[32]{0:T(128)} %param.34) | copy-start | bytes 388
  123.2 7.7 %copy-start.50 = (f32[1024]{0:T(1024)S(1)}, f32[1024]{0:T(1024)}, u32[]{:S(2)}) copy-start(f32[1024]{0:T(1024)} %param.45) | copy-start | bytes 12292
  123.2 7.7 %copy-start.51 = (f32[1024]{0:T(1024)S(1)}, f32[1024]{0:T(1024)}, u32[]{:S(2)}) copy-start(f32[1024]{0:T(1024)} %param.40) | copy-start | bytes 12292
  123.2 9.3 %slice-start = ((bf16[1024,288]{1,0:T(8,128)(2,1)}), bf16[1024,32]{1,0:T(8,128)(2,1)S(1)}, s32[]{:S(2)}) async-start(bf16[1024,288]{1,0:T(8,128)(2,1)} %convolution_convert_fusion.1), calls=%async_computation.5 | async-start | bytes 524288 | tf_op jit(solution)/shard_map/slice | solution.py:1955
  124.7 10.4 %copy-start.24 = (f32[256]{0:T(256)}, f32[256]{0:T(256)S(1)}, u32[]{:S(2)}) copy-start(f32[256]{0:T(256)S(1)} %slice.176) | copy-start | bytes 3076
  125.4 9.7 %copy-start.22 = (f32[4,256]{1,0:T(4,128)}, f32[4,256]{1,0:T(4,128)S(1)}, u32[]{:S(2)}) copy-start(f32[4,256]{1,0:T(4,128)S(1)} %slice.175.wbc) | copy-start | bytes 12292
  126.5 8.7 %copy-start.1 = (bf16[1024,256]{1,0:T(8,128)(2,1)}, bf16[1024,256]{1,0:T(8,128)(2,1)S(1)}, u32[]{:S(2)}) copy-start(bf16[1024,256]{1,0:T(8,128)(2,1)S(1)} %slice.213.bc) | copy-start | bytes 1572868
  129.0 6.1 %copy-start.26 = (f32[1,128]{1,0:T(1,128)}, f32[1,128]{1,0:T(1,128)S(1)}, u32[]{:S(2)}) copy-start(f32[1,128]{1,0:T(1,128)S(1)} %pad.30.bx) | copy-start | bytes 1540
  129.0 6.1 %copy-start.23 = (f32[4,128]{1,0:T(4,128)}, f32[4,128]{1,0:T(4,128)S(1)}, u32[]{:S(2)}) copy-start(f32[4,128]{1,0:T(4,128)S(1)} %pad.29.wx) | copy-start | bytes 6148
  129.4 13.0 %copy-start = (f32[1032,8]{1,0:T(8,128)}, f32[1032,8]{1,0:T(8,128)S(1)}, u32[]{:S(2)}) copy-start(f32[1032,8]{1,0:T(8,128)S(1)} %pad.28.marks) | copy-start | bytes 99076
  130.8 11.6 %copy-start.25 = (f32[3]{0:T(128)}, f32[3]{0:T(128)S(1)}, u32[]{:S(2)}) copy-start(f32[3]{0:T(128)S(1)} %pad_maximum_fusion.4.numbers) | copy-start | bytes 40
  130.9 30.2 %copy-start.20 = (f32[2,1024]{1,0:T(2,128)}, f32[2,1024]{1,0:T(2,128)S(1)}, u32[]{:S(2)}) copy-start(f32[2,1024]{1,0:T(2,128)S(1)} %pad_maximum_fusion.3.gains) | copy-start | bytes 24580
  132.6 9.9 %copy-start.2 = (f32[1024,1]{1,0:T(8,128)}, f32[1024,1]{1,0:T(8,128)S(1)}, u32[]{:S(2)}) copy-start(f32[1024,1]{1,0:T(8,128)S(1)} %dynamic-slice_convert_fusion.dt) | copy-start | bytes 12292
  135.1 21.4 %copy-start.6 = (bf16[1024,128]{1,0:T(8,128)(2,1)}, bf16[1024,128]{1,0:T(8,128)(2,1)S(1)}, u32[]{:S(2)}) copy-start(bf16[1024,128]{1,0:T(8,128)(2,1)S(1)} %convolution_convert_fusion.2.xz) | copy-start | bytes 786436
  143.3 13.2 %copy-start.5 = (bf16[4,4,2,32,1536]{4,3,2,1,0:T(8,128)(2,1)S(1)}, bf16[4,4,2,32,1536]{4,3,2,1,0:T(8,128)(2,1)}, u32[]{:S(2)}) copy-start(bf16[4,4,2,32,1536]{4,3,2,1,0:T(8,128)(2,1)} %copy-done.4) | copy-start | bytes 9437188
  146.2 13.8 %all-to-all-start.1 = ((bf16[32,2,1024]{2,1,0:T(2,128)(2,1)}), bf16[32,2,1024]{2,1,0:T(2,128)(2,1)}, u32[]{:S(2)}, u32[]{:S(2)}) async-start(bf16[32,2,1024]{2,1,0:T(2,128)(2,1)} %reshape.365), calls=%async_computation.1 | async-start | bytes 262144 | tf_op jit(solution)/shard_map/all_to_all | solution.py:707
  159.2 15.4 %copy-start.19 = (f32[2,1024]{1,0:T(2,128)}, f32[2,1024]{1,0:T(2,128)S(1)}, u32[]{:S(2)}) copy-start(f32[2,1024]{1,0:T(2,128)S(1)} %reshape.339.gated_gain) | copy-start | bytes 24580
  180.8 69.7 %copy-start.21 = (bf16[256,128]{1,0:T(8,128)(2,1)}, bf16[256,128]{1,0:T(8,128)(2,1)S(1)}, u32[]{:S(2)}) copy-start(bf16[256,128]{1,0:T(8,128)(2,1)S(1)} %get-tuple-element.66.local_in) | copy-start | bytes 196612
  288.4 114.6 %copy-start.44 = (f32[1024]{0:T(1024)S(1)}, f32[1024]{0:T(1024)}, u32[]{:S(2)}) copy-start(f32[1024]{0:T(1024)} %param.30) | copy-start | bytes 12292
  288.4 115.7 %copy-start.52 = (f32[32]{0:T(128)S(1)}, f32[32]{0:T(128)}, u32[]{:S(2)}) copy-start(f32[32]{0:T(128)} %get-tuple-element.94) | copy-start | bytes 388
  288.5 115.7 %copy-start.46 = (f32[32,128]{1,0:T(8,128)S(1)}, f32[32,128]{1,0:T(8,128)}, u32[]{:S(2)}) copy-start(f32[32,128]{1,0:T(8,128)} %get-tuple-element.77) | copy-start | bytes 49156
  288.5 115.7 %copy-start.49 = (f32[2,1024]{1,0:T(2,128)S(1)}, f32[2,1024]{1,0:T(2,128)}, u32[]{:S(2)}) copy-start(f32[2,1024]{1,0:T(2,128)} %get-tuple-element.79) | copy-start | bytes 24580
  288.5 115.8 %copy-start.48 = (f32[2,1024]{1,0:T(2,128)S(1)}, f32[2,1024]{1,0:T(2,128)}, u32[]{:S(2)}) copy-start(f32[2,1024]{1,0:T(2,128)} %get-tuple-element.78) | copy-start | bytes 24580
  399.9 6.5 %copy-start.33 = (f32[32,1408]{1,0:T(8,128)S(1)}, f32[32,1408]{1,0:T(8,128)}, u32[]{:S(2)}) copy-start(f32[32,1408]{1,0:T(8,128)} %get-tuple-element.76) | copy-start | bytes 540676
  399.9 6.5 %copy-start.39 = (f32[32,1024]{1,0:T(8,128)S(1)}, f32[32,1024]{1,0:T(8,128)}, u32[]{:S(2)}) copy-start(f32[32,1024]{1,0:T(8,128)} %get-tuple-element.70) | copy-start | bytes 393220
  471.0 4.2 copy-start.3
  482.0 4.1 copy-start.42
  482.0 4.1 copy-start.45
  483.0 5.3 %copy-start.29 = (bf16[1024,1024]{1,0:T(8,128)(2,1)S(1)}, bf16[1024,1024]{1,0:T(8,128)(2,1)}, u32[]{:S(2)}) copy-start(bf16[1024,1024]{1,0:T(8,128)(2,1)} %slice.211) | copy-start | bytes 6291460
  488.3 3.2 copy-start.34
  (20 other events, 30.5 us)
Sparse Core Ops, SparseCore 0:
  13.9 119.1 all-gather.2
  134.8 63.7 all-gather.4

commit v4 on v3

--- a/solution.py
+++ b/solution.py
@@ -525,6 +525,7 @@
 QUERY = 128
 BYTE_BLOCK = 128
 MESH = pl.DeviceIdType.MESH
+SUM_ROWS = (3 * D + DI + (CONV + 1) * 2 * STATE) // 128
 LOW = jnp.bfloat16
 FULL = jnp.float32
 BOTH = (NARROW, WIDE)
@@ -585,126 +586,367 @@
     remote(part, part, send, recv, device_at(me, wide)).wait()
 
 
-def gather_kernel(count, narrow, depth, last, *refs):
-    if last:
-        middle, feed = refs[count : count + 2]
-        middle_out, feed_got = refs[2 * count + 2 : 2 * count + 4]
-        middle_got, m_send, m_recv, m_sem, f_send, f_recv, f_sem = refs[-7:]
-        refs = refs[:count] + refs[count + 2 : 2 * count + 2] + refs[2 * count + 4 : -7]
-    ins, outs = refs[:count], refs[count : 2 * count]
-    local, z_send, z_recv, n_send, n_recv, c_send, c_recv = refs[2 * count :]
+class StagedGather:
+    def __init__(self, block, out, sems, narrow, depth):
+        n, w = lax.axis_index(NARROW), lax.axis_index(WIDE)
+        z, c = lax.div(w, 2), lax.rem(w, 2)
+        self.out, self.narrow, self.depth = out, narrow, depth
+        self.n, self.c = n, c
+        self.sems = [sems.at[i] for i in range(7)]
+        self.twin = (n, z * 2 + 1 - c)
+        self.n_peers = [lax.rem(n + k, narrow) for k in range(1, narrow)]
+        self.w = w
+        self.own = pltpu.make_async_copy(block, out.at[n, z, c], self.sems[0])
+        self.first = [
+            remote(
+                block,
+                out.at[n, z, c],
+                self.sems[1],
+                self.sems[2],
+                (n, lax.rem(z + k, depth) * 2 + c),
+            )
+            for k in range(1, depth)
+        ]
+
+    def wait_for(self, part, i):
+        return remote(part, part, self.sems[i], self.sems[i + 1], self.twin)
+
+    def z_part(self):
+        return self.wait_for(self.out.at[self.n, pl.ds(0, self.depth - 1), self.c], 1)
+
+    def n_part(self):
+        return self.wait_for(self.out.at[pl.ds(0, self.narrow - 1), :, self.c], 3)
+
+    def start(self):
+        self.own.start()
+        for copy in self.first:
+            copy.start()
+
+    def spread(self):
+        self.own.wait()
+        self.z_part().wait_recv()
+        mine = self.out.at[self.n, :, self.c]
+        for m in self.n_peers:
+            remote(mine, mine, self.sems[3], self.sems[4], (m, self.w)).start()
+        self.wait_for(mine, 5).start()
+
+    def cross(self):
+        self.n_part().wait_recv()
+        for m in self.n_peers:
+            self.wait_for(self.out.at[m, :, self.c], 5).start()
+
+    def finish(self):
+        self.wait_for(self.out.at[:, :, 1 - self.c], 5).wait()
+        self.z_part().wait_send()
+        self.n_part().wait_send()
+
+
+def greet_lines(narrow, depth):
     n, w = lax.axis_index(NARROW), lax.axis_index(WIDE)
     z, c = lax.div(w, 2), lax.rem(w, 2)
-    z_peers = [(n, lax.rem(z + k, depth) * 2 + c) for k in range(1, depth)]
-    n_peers = [lax.rem(n + k, narrow) for k in range(1, narrow)]
-    twin = (n, z * 2 + 1 - c)
+    peers = [(n, lax.rem(z + k, depth) * 2 + c) for k in range(1, depth)]
+    peers += [(lax.rem(n + k, narrow), w) for k in range(1, narrow)]
+    peers += [(n, z * 2 + 1 - c)]
     barrier = pltpu.get_barrier_semaphore()
-    for peer in z_peers:
+    for peer in peers:
         pl.semaphore_signal(barrier, inc=1, device_id=peer, device_id_type=MESH)
-    for m in n_peers:
-        pl.semaphore_signal(barrier, inc=1, device_id=(m, w), device_id_type=MESH)
-    pl.semaphore_signal(barrier, inc=1, device_id=twin, device_id_type=MESH)
-    pl.semaphore_wait(barrier, len(z_peers) + len(n_peers) + 1)
-
-    own = [pltpu.make_async_copy(ins[i], outs[i].at[n, z, c], local.at[i]) for i in range(count)]
-    for i in range(count):
-        own[i].start()
-        for peer in z_peers:
-            remote(ins[i], outs[i].at[n, z, c], z_send.at[i], z_recv.at[i], peer).start()
-    if last:
-        middle_copies, feed_copies = [], []
-        for k in range(1, depth):
-            place = lax.rem(z + k, depth)
-            middle_copies.append(
+    pl.semaphore_wait(barrier, len(peers))
+
+
+class LineSum:
+    def __init__(self, parts, got, sems, place, length, peer_of):
+        self.got, self.length = got, length
+        self.own = pltpu.make_async_copy(parts.at[place], got.at[0], sems.at[0])
+        self.copies = []
+        for k in range(1, length):
+            there = lax.rem(place + k, length)
+            self.copies.append(
                 remote(
-                    middle.at[place],
-                    middle_got.at[k],
-                    m_send.at[k - 1],
-                    m_recv.at[k - 1],
-                    (n, place * 2 + c),
+                    parts.at[there], got.at[k], sems.at[2 * k - 1], sems.at[2 * k], peer_of(there)
                 )
             )
+
+    def start(self):
+        self.own.start()
+        for copy in self.copies:
+            copy.start()
+
+    def arrive(self):
+        self.own.wait()
+        for copy in self.copies:
+            copy.wait_recv()
+
+    def total(self, *index):
+        summed = self.got[(0,) + index].astype(FULL)
+        for k in range(1, self.length):
+            summed += self.got[(k,) + index].astype(FULL)
+        return summed
+
+    def finish(self):
+        for copy in self.copies:
+            copy.wait_send()
+
+
+def start_kernel(
+    narrow,
+    wide,
+    pack,
+    table,
+    xz_blocks,
+    gate,
+    up,
+    down,
+    middle,
+    cotangent,
+    pack_all,
+    table_all,
+    xz_all,
+    gate_turned,
+    up_turned,
+    down_turned,
+    middle_line,
+    others,
+    pack_sems,
+    table_sems,
+    xz_sems,
+    turn_send,
+    turn_recv,
+    own_sems,
+    line_send,
+    line_recv,
+    other_send,
+    other_recv,
+):
+    devices, depth = narrow * wide, wide // 2
+    me, arrived = greet_all(devices, wide)
+    n, w = lax.axis_index(NARROW), lax.axis_index(WIDE)
+    z, c = lax.div(w, 2), lax.rem(w, 2)
+    twin = (n, z * 2 + 1 - c)
+    rows, units = gate.shape[0], gate.shape[1] // narrow
+    columns = down.shape[1]
+    gathers = [
+        StagedGather(pack, pack_all, pack_sems, narrow, depth),
+        StagedGather(table, table_all, table_sems, narrow, depth),
+    ]
+
+    def pieces(m):
+        mine = pl.ds(m * units, units)
+        return (gate.at[:, mine], up.at[:, mine], down.at[mine, :])
+
+    landing = (
+        gate_turned.at[pl.ds(n * rows, rows), :],
+        up_turned.at[pl.ds(n * rows, rows), :],
+        down_turned.at[:, pl.ds(n * columns, columns)],
+    )
+    turns = []
+    for k in range(1, narrow):
+        m = lax.rem(n + k, narrow)
+        for i, piece in enumerate(pieces(m)):
+            turns.append(
+                remote(piece, landing[i], turn_send.at[k - 1, i], turn_recv.at[k - 1, i], (m, w))
+            )
+    own = [
+        pltpu.make_async_copy(piece, landing[i], own_sems.at[i])
+        for i, piece in enumerate(pieces(n))
+    ]
+    own.append(pltpu.make_async_copy(xz_blocks.at[me], xz_all.at[me], own_sems.at[3]))
+    own.append(pltpu.make_async_copy(middle, middle_line.at[z], own_sems.at[4]))
+    lines = [
+        remote(middle, middle_line.at[z], line_send, line_recv, (n, lax.rem(z + k, depth) * 2 + c))
+        for k in range(1, depth)
+    ]
+    for k in range(1, narrow):
+        peer = (lax.rem(n + narrow - k, narrow), w)
+        turns.append(
+            remote(cotangent, others.at[k - 1], other_send.at[k - 1], other_recv.at[k - 1], peer)
+        )
+    arrived()
+    for gather in gathers:
+        gather.start()
+    for copy in turns + own:
+        copy.start()
+    send_blocks(me, devices, wide, xz_blocks, xz_all, xz_sems.at[0], xz_sems.at[1])
+    for copy in lines:
+        copy.start()
+    for gather in gathers:
+        gather.spread()
+    for gather in gathers:
+        gather.cross()
+    for copy in own:
+        copy.wait()
+    for copy in turns:
+        copy.wait()
+    for gather in gathers:
+        gather.finish()
+    wait_blocks(me, devices, wide, xz_all, xz_sems.at[0], xz_sems.at[1])
+    part = middle_line.at[pl.ds(0, depth - 1)]
+    remote(part, part, line_send, line_recv, twin).wait()
+
+
+def start_weights(pack, table, xz_blocks, gate, up, down, middle, cotangent, collective_id):
+    narrow, wide = lax.axis_size(NARROW), lax.axis_size(WIDE)
+    depth = wide // 2
+    units = gate.shape[1] // narrow
+    dma = pltpu.SemaphoreType.DMA
+    anywhere = pl.BlockSpec(memory_space=pl.ANY)
+
+    def low(*shape):
+        return jax.ShapeDtypeStruct(shape, LOW)
+
+    outs = pl.pallas_call(
+        partial(start_kernel, narrow, wide),
+        out_shape=[
+            low(narrow, depth, 2, *pack.shape),
+            low(narrow, depth, 2, *table.shape),
+            low(*xz_blocks.shape),
+            low(D, units),
+            low(D, units),
+            low(units, D),
+            low(depth, *middle.shape),
+            low(narrow - 1, *cotangent.shape),
+        ],
+        in_specs=[anywhere] * 8,
+        out_specs=[anywhere] * 8,
+        scratch_shapes=[
+            dma((7,)),
+            dma((7,)),
+            dma((2,)),
+            dma((narrow - 1, 3)),
+            dma((narrow - 1, 3)),
+            dma((5,)),
+            dma,
+            dma,
+            dma((narrow - 1,)),
+            dma((narrow - 1,)),
+        ],
+        compiler_params=pltpu.CompilerParams(collective_id=collective_id, has_side_effects=True),
+        name="start_weights",
+    )(pack, table, xz_blocks, gate, up, down, middle, cotangent)
+    return (
+        outs[0].reshape(-1, pack.shape[1]),
+        outs[1].reshape(-1, table.shape[1]),
+        outs[2].reshape(D, -1),
+    ) + tuple(outs[3:])
+
+
+def end_kernel(
+    narrow,
+    depth,
+    pack,
+    sums,
+    middle,
+    down_sum,
+    pack_all,
+    sums_all,
+    middle_out,
+    down_out,
+    middle_got,
+    down_got,
+    pack_sems,
+    sums_sems,
+    middle_sems,
+    down_send,
+    down_recv,
+    down_own,
+):
+    n, w = lax.axis_index(NARROW), lax.axis_index(WIDE)
+    z, c = lax.div(w, 2), lax.rem(w, 2)
+    greet_lines(narrow, depth)
+    gathers = [
+        StagedGather(pack, pack_all, pack_sems, narrow, depth),
+        StagedGather(sums, sums_all, sums_sems, narrow, depth),
+    ]
+    line = LineSum(middle, middle_got, middle_sems, z, depth, lambda there: (n, there * 2 + c))
+    back = Returned(down_sum, down_got, down_send, down_recv, down_own, n, w, narrow, 1)
+    for gather in gathers:
+        gather.start()
+    line.start()
+    back.start()
+    for gather in gathers:
+        gather.spread()
+    line.arrive()
+    middle_out[...] = line.total()
+    for gather in gathers:
+        gather.cross()
+    back.arrive()
+    down_out[...] = down_got[...].astype(FULL)
+    for gather in gathers:
+        gather.finish()
+    line.finish()
+    back.finish()
+
+
+class Returned:
+    def __init__(self, values, got, send, recv, own, n, w, narrow, axis):
+        span = values.shape[axis] // narrow
+        other = values.shape[1 - axis]
+
+        def block(m):
+            mine = pl.ds(m * span, span)
+            return values.at[mine, :] if axis == 0 else values.at[:, mine]
+
+        there = pl.ds(n * other, other)
+        landing = got.at[:, there] if axis == 0 else got.at[there, :]
+        self.own = pltpu.make_async_copy(block(n), landing, own)
+        self.copies = []
         for k in range(1, narrow):
             m = lax.rem(n + k, narrow)
-            feed_copies.append(
-                remote(feed.at[m], feed_got.at[n], f_send.at[k - 1], f_recv.at[k - 1], (m, w))
+            self.copies.append(
+                remote(block(m), landing, send.at[k - 1], recv.at[k - 1], (m, w))
             )
-        for copy in middle_copies + feed_copies:
+
+    def start(self):
+        self.own.start()
+        for copy in self.copies:
             copy.start()
-        own += [
-            pltpu.make_async_copy(middle.at[z], middle_got.at[0], m_sem),
-            pltpu.make_async_copy(feed.at[n], feed_got.at[n], f_sem),
-        ]
-        own[count].start()
-        own[count + 1].start()
-    for i in range(count):
-        own[i].wait()
-        part = outs[i].at[n, pl.ds(0, depth - 1), c]
-        remote(part, part, z_send.at[i], z_recv.at[i], twin).wait_recv()
-        mine = outs[i].at[n, :, c]
-        for m in n_peers:
-            remote(mine, mine, n_send.at[i], n_recv.at[i], (m, w)).start()
-        remote(mine, mine, c_send.at[i], c_recv.at[i], twin).start()
-    for i in range(count):
-        part = outs[i].at[pl.ds(0, narrow - 1), :, c]
-        remote(part, part, n_send.at[i], n_recv.at[i], twin).wait_recv()
-        for m in n_peers:
-            theirs = outs[i].at[m, :, c]
-            remote(theirs, theirs, c_send.at[i], c_recv.at[i], twin).start()
-    for i in range(count):
-        half = outs[i].at[:, :, 1 - c]
-        remote(half, half, c_send.at[i], c_recv.at[i], twin).wait()
-        part = outs[i].at[n, pl.ds(0, depth - 1), c]
-        remote(part, part, z_send.at[i], z_recv.at[i], twin).wait_send()
-        part = outs[i].at[pl.ds(0, narrow - 1), :, c]
-        remote(part, part, n_send.at[i], n_recv.at[i], twin).wait_send()
-    if last:
-        own[count].wait()
-        own[count + 1].wait()
-        for copy in middle_copies:
-            copy.wait()
-        total = middle_got[0].astype(FULL)
-        for k in range(1, depth):
-            total += middle_got[k].astype(FULL)
-        middle_out[...] = total
-        for copy in feed_copies:
-            copy.wait()
-
-
-def gather_all(arrays, collective_id, middle=None, feed=None):
+
+    def arrive(self):
+        self.own.wait()
+        for copy in self.copies:
+            copy.wait_recv()
+
+    def finish(self):
+        for copy in self.copies:
+            copy.wait_send()
+
+
+def end_gather(pack, sums, middle, down_sum, collective_id):
     narrow, wide = lax.axis_size(NARROW), lax.axis_size(WIDE)
-    count = len(arrays)
+    depth = wide // 2
     dma = pltpu.SemaphoreType.DMA
     anywhere = pl.BlockSpec(memory_space=pl.ANY)
-    outs = [jax.ShapeDtypeStruct((narrow, wide // 2, 2) + a.shape, a.dtype) for a in arrays]
-    out_specs = [anywhere] * count
-    scratch = [dma((count,))] * 7
-    last = middle is not None
-    if last:
-        outs += [
+    down_shape = (down_sum.shape[0] * narrow, down_sum.shape[1] // narrow)
+    outs = pl.pallas_call(
+        partial(end_kernel, narrow, depth),
+        out_shape=[
+            jax.ShapeDtypeStruct((narrow, depth, 2) + pack.shape, pack.dtype),
+            jax.ShapeDtypeStruct((narrow, depth, 2) + sums.shape, sums.dtype),
             jax.ShapeDtypeStruct(middle.shape[1:], FULL),
-            jax.ShapeDtypeStruct(feed.shape, feed.dtype),
-        ]
-        out_specs += [in_vmem(), anywhere]
-        scratch += [pltpu.VMEM(middle.shape, middle.dtype)]
-        scratch += [dma((wide // 2 - 1,))] * 2 + [dma] + [dma((narrow - 1,))] * 2 + [dma]
-    outs = pl.pallas_call(
-        partial(gather_kernel, count, narrow, wide // 2, last),
-        out_shape=outs,
-        in_specs=[anywhere] * (count + 2 * last),
-        out_specs=out_specs,
-        scratch_shapes=scratch,
+            jax.ShapeDtypeStruct(down_shape, FULL),
+        ],
+        in_specs=[anywhere] * 4,
+        out_specs=[anywhere] * 2 + [in_vmem()] * 2,
+        scratch_shapes=[
+            pltpu.VMEM(middle.shape, middle.dtype),
+            pltpu.VMEM(down_shape, LOW),
+            dma((7,)),
+            dma((7,)),
+            dma((2 * depth,)),
+            dma((narrow - 1,)),
+            dma((narrow - 1,)),
+            dma,
+        ],
         compiler_params=pltpu.CompilerParams(
             collective_id=collective_id, has_side_effects=True, vmem_limit_bytes=32 << 20
         ),
-        name="gather_all",
-    )(*arrays, *((middle, feed) if last else ()))
-    gathered = [o.reshape((-1,) + a.shape[1:]) for o, a in zip(outs, arrays)]
-    return gathered + list(outs[count:])
-
-
-def exchange(blocks, axis):
-    return lax.all_to_all(blocks, axis, split_axis=0, concat_axis=0, tiled=True)
+        name="end_gather",
+    )(pack, sums, middle, down_sum)
+    return [
+        outs[0].reshape(-1, pack.shape[1]),
+        outs[1].reshape((-1,) + sums.shape),
+        outs[2],
+        outs[3],
+    ]
 
 
 def softplus(v):
@@ -738,24 +980,228 @@
     return lower, delta, decay, begun, tail, kept
 
 
-def mixer_forward_kernel(
-    numbers, xz, bc, dt, marks, wx, bx, wbc, bbc, u_out, y_out, states, xz_pad, bc_pad, state
+def head_numbers(step_bias, log_rate, skip_gain, me):
+    return step_bias[me], jnp.exp(jnp.full((1, QUERY), log_rate[me], FULL)), skip_gain[me]
+
+
+def head_columns(values, me):
+    start = pl.multiple_of(lax.div(me, 2) * 2 * HEAD_M, 2 * HEAD_M)
+    pair = values[:, pl.ds(start, 2 * HEAD_M)]
+    lane = lax.broadcasted_iota(jnp.int32, pair.shape, 1)
+    moved = jnp.concatenate([pair[:, HEAD_M:], pair[:, :HEAD_M]], axis=1)
+    odd = jnp.full(pair.shape, lax.rem(me, 2), jnp.int32) == 1
+    return jnp.where(lane < HEAD_M, jnp.where(odd, moved, pair), 0.0)
+
+
+def documents(doc_patches, pad_bytes):
+    ends, end = [], 0
+    for d in range(doc_patches.shape[0]):
+        end = end + doc_patches[d]
+        ends.append(end)
+
+    def document(place):
+        return sum((place >= end).astype(jnp.int32) for end in ends)
+
+    def kept(place, offset):
+        padded = [
+            ((place == end - 1) & (offset >= PATCH - pad_bytes[d])).astype(FULL)
+            for d, end in enumerate(ends)
+        ]
+        return 1.0 - sum(padded)
+
+    return document, kept
+
+
+def patch_marks(document, first, count):
+    place = first + lax.broadcasted_iota(jnp.int32, (count, 8), 0)
+    kind = lax.broadcasted_iota(jnp.int32, (count, 8), 1)
+    opening = lax.div(place, QUERY) * QUERY
+    block_mark = jnp.where(kind == CONV, opening - 1, opening + QUERY - 1)
+    ahead = jnp.where(kind < CONV, place - kind, block_mark)
+    facing = jnp.where(kind == CONV + 2, opening - 1, place)
+    same = (document(ahead) == document(facing)) & (ahead >= 0) & (facing >= 0)
+    return jnp.where(kind == 0, document(place).astype(FULL), same.astype(FULL))
+
+
+def mixer_front_kernel(
+    narrow,
+    wide,
+    doc_patches,
+    pad_bytes,
+    step_biases,
+    log_rates,
+    skip_gains,
+    start,
+    table,
+    w_xz,
+    gain,
+    conv_weight,
+    conv_bias,
+    gate,
+    up,
+    down,
+    middle,
+    embedded,
+    normed,
+    xz,
+    bc,
+    dt,
+    u_out,
+    y_out,
+    states,
+    mixed_in,
+    u_got,
+    marks,
+    keep_rows,
+    keep_all,
+    gate_all,
+    up_all,
+    down_all,
+    middle_all,
+    mixed_all,
+    xz_pad,
+    bc_pad,
+    state,
+    u_blocks,
+    u_send,
+    u_recv,
+    own_sems,
+    line_send,
+    line_recv,
+    cross_send,
+    cross_recv,
+    middle_sems,
 ):
-    count = xz.shape[0]
+    devices, depth = narrow * wide, wide // 2
+    me, arrived = greet_all(devices, wide)
+    n, w = lax.axis_index(NARROW), lax.axis_index(WIDE)
+    z, c = lax.div(w, 2), lax.rem(w, 2)
+    twin = (n, z * 2 + 1 - c)
+    turned = (gate, up, down)
+    results = (gate_all, up_all, down_all)
+    own = [pltpu.make_async_copy(turned[i], results[i].at[z, c], own_sems.at[i]) for i in range(3)]
+    own.append(pltpu.make_async_copy(middle, middle_all.at[n, :, c], own_sems.at[3]))
+    for copy in own:
+        copy.start()
+    beside = n + 1 - 2 * lax.rem(n, 2)
+    across = n + 2 - 4 * lax.div(n, 2)
+    corner = narrow - 1 - n
+    arrived()
+
+    def middle_copy(j, way, owner, src=None):
+        there = middle_all.at[owner, j, c]
+        peer = twin if way >= 4 else ((beside if way in (0, 3) else across), w)
+        return remote(
+            there if src is None else src, there, middle_sems.at[0, way, j], middle_sems.at[1, way, j], peer
+        )
+
+    for j in range(depth):
+        middle_copy(j, 0, n, middle.at[j]).start()
+        middle_copy(j, 1, n, middle.at[j]).start()
+
+    def line_copy(i, source, step, src=None):
+        there = results[i].at[source, c]
+        return remote(
+            there if src is None else src,
+            there,
+            line_send.at[i, source, max(step, 0)],
+            line_recv.at[i, source],
+            (n, (z + step) * 2 + c),
+        )
+
+    def along(i, source, step, src=None):
+        @pl.when((z + step >= 0) & (z + step < depth))
+        def _():
+            line_copy(i, source, step, src).start()
+
+    for i in range(3):
+        along(i, z, 1, turned[i])
+        along(i, z, -1, turned[i])
+    own_middle = remote(
+        middle, middle_all.at[n, :, c], middle_sems.at[0, 7, 0], middle_sems.at[1, 7, 0], twin
+    )
+    own_middle.start()
+
+    def middle_on(j):
+        middle_copy(j, 0, beside).wait_recv()
+        if j % 2 == 0:
+            middle_copy(j, 2, beside).start()
+        middle_copy(j, 4, beside).start()
+        middle_copy(j, 1, across).wait_recv()
+        if j % 2 == 1:
+            middle_copy(j, 3, across).start()
+        middle_copy(j, 5, across).start()
+
+    def line_on(distance):
+        for step in (1, -1):
+            source = z - step * distance
+
+            @pl.when((source >= 0) & (source < depth))
+            def _():
+                for i in range(3):
+                    line_copy(i, source, step).wait_recv()
+                    along(i, source, step)
+                    theirs = results[i].at[source, c]
+                    remote(theirs, theirs, cross_send.at[i], cross_recv.at[i], twin).start()
+
+    count = embedded.shape[0]
+    patches = u_blocks.shape[1]
+    block_rows = 2 * QUERY
     xz_pad[pl.ds(0, 8), :] = jnp.zeros((8, xz_pad.shape[1]), FULL)
     bc_pad[pl.ds(0, 8), :] = jnp.zeros((8, bc_pad.shape[1]), FULL)
     state[...] = jnp.zeros_like(state)
-    step_bias, rate_scale, skip = numbers[0], numbers[1], numbers[2]
-
-    xz_pad[pl.ds(8, count), :] = xz[...].astype(FULL)
-    bc_pad[pl.ds(8, count), :] = bc[...].astype(FULL)
+    step_bias, rate_scale, skip = head_numbers(step_biases, log_rates, skip_gains, me)
+    document, kept_bytes = documents(doc_patches, pad_bytes)
+    for first in range(0, count + 8, (count + 8) // 3):
+        part = (count + 8) // 3
+        marks[first : first + part, :] = patch_marks(document, first, part)
+    byte = lax.broadcasted_iota(jnp.int32, keep_rows.shape[1:], 0)
+    for k in range(narrow):
+        there = (lax.rem(n + k, narrow) * wide + w) * patches
+        keep_rows[k] = kept_bytes(there + lax.div(byte, PATCH), lax.rem(byte, PATCH))
+    wx, bx = head_columns(conv_weight, me), head_columns(conv_bias, me)
+    wbc, bbc = conv_weight[:, DI:], conv_bias[:, DI:]
+    words = lax.broadcasted_iota(jnp.int32, (block_rows, VOCAB), 1).astype(FULL)
+    own_lane = lax.broadcasted_iota(jnp.int32, (block_rows, STATE), 1) == me
+
+    def project(i, carry):
+        rows = pl.ds(pl.multiple_of(i * block_rows, block_rows), block_rows)
+        ids = start[rows, 3 * STATE : 4 * STATE].astype(FULL)
+        place = i * block_rows + lax.broadcasted_iota(jnp.int32, (block_rows, PATCH), 0)
+        kept = kept_bytes(place, lax.broadcasted_iota(jnp.int32, (block_rows, PATCH), 1))
+        keep_all[rows, :] = kept
+        for k in range(PATCH):
+            chosen = jnp.where(ids[:, k : k + 1] == words, kept[:, k : k + 1], 0.0).astype(LOW)
+            embedded[rows, k * EMB : (k + 1) * EMB] = nn(chosen, table[...]).astype(LOW)
+        row_embedded = embedded[rows, :]
+        for first in range(0, D, WEIGHT_STEP):
+            columns = slice(first, first + WEIGHT_STEP)
+            weight = start[:, 4 * STATE + first : 4 * STATE + first + WEIGHT_STEP]
+            mixed_all[rows, columns] = nn(row_embedded, weight)
+        row_normed = (unit_rows(mixed_all[rows, :])[0] * gain[...]).astype(LOW)
+        normed[rows, :] = row_normed
+        row_xz = nn(row_normed, w_xz[...]).astype(LOW)
+        row_bcdt = nn(row_normed, start[:, : 3 * STATE]).astype(LOW)
+        xz[rows, :] = row_xz
+        bc[rows, :] = row_bcdt[:, : 2 * STATE]
+        own_dt = jnp.where(own_lane, row_bcdt[:, 2 * STATE :].astype(FULL), 0.0)
+        dt[rows, :] = jnp.sum(own_dt, axis=1, keepdims=True)
+        padded = pl.ds(pl.multiple_of(i * block_rows + 8, 8), block_rows)
+        xz_pad[padded, :] = row_xz.astype(FULL)
+        bc_pad[padded, :] = row_bcdt[:, : 2 * STATE].astype(FULL)
+        return carry
+
+    lax.fori_loop(0, count // block_rows, project, 0)
+    middle_on(0)
+    mixed_in[...] = mixed_all[pl.ds(pl.multiple_of(me * patches, patches), patches), :]
+    group = QUERY // patches
 
     def block(i, carry):
-        start = pl.multiple_of(i * QUERY, QUERY)
-        rows = pl.ds(start, QUERY)
+        first = pl.multiple_of(i * QUERY, QUERY)
+        rows = pl.ds(first, QUERY)
         mark = marks[rows, :]
-        act_x = jax.nn.silu(convolved(xz_pad[pl.ds(start, QUERY + 8), :], mark, wx[...], bx[...]))
-        act = jax.nn.silu(convolved(bc_pad[pl.ds(start, QUERY + 8), :], mark, wbc[...], bbc[...]))
+        act_x = jax.nn.silu(convolved(xz_pad[pl.ds(first, QUERY + 8), :], mark, wx, bx))
+        act = jax.nn.silu(convolved(bc_pad[pl.ds(first, QUERY + 8), :], mark, wbc, bbc))
         x, b, c = act_x[:, :HEAD_M], act[:, :STATE], act[:, STATE:]
         lower, delta, decay, begun, tail, kept = decays(mark, dt[rows, :], step_bias, rate_scale)
         weight = nt(c, b, highest) * decay * delta.T
@@ -768,40 +1214,92 @@
         )
         state[...] = held * kept + tn(x * (tail * delta)[:, :HEAD_M], b, highest)
         z = xz[rows, :].astype(FULL)[:, HEAD_M:]
+        u = y * jax.nn.silu(z)
         y_out[rows, :] = y
-        u_out[rows, :] = y * jax.nn.silu(z)
+        u_out[rows, :] = u
+        u_blocks[pl.ds(i * group, group)] = u.astype(LOW).reshape(group, patches, HEAD_M)
         return carry
 
     lax.fori_loop(0, count // QUERY, block, 0)
+    send_blocks(me, devices, wide, u_blocks, u_got, u_send, u_recv)
+    u_got[me] = u_blocks[me]
+    line_on(1)
+    middle_on(1)
+    for copy in own:
+        copy.wait()
+    for i in range(3):
+        mine = results[i].at[z, c]
+        remote(mine, mine, cross_send.at[i], cross_recv.at[i], twin).start()
+    middle_on(2)
+    line_on(2)
+    middle_on(3)
+    for j in range(depth):
+        middle_copy(j, 2 + j % 2, corner).wait_recv()
+        middle_copy(j, 6, corner).start()
+    line_on(3)
+    wait_blocks(me, devices, wide, u_got, u_send, u_recv)
+    for i in range(3):
+        theirs = results[i].at[:, 1 - c]
+        remote(theirs, theirs, cross_send.at[i], cross_recv.at[i], twin).wait()
+    own_middle.wait()
+    for j in range(depth):
+        for way, owner in ((4, beside), (5, across), (6, corner)):
+            middle_copy(j, way, owner).wait()
+        middle_copy(j, 0, n, middle.at[j]).wait_send()
+        middle_copy(j, 1, n, middle.at[j]).wait_send()
+        middle_copy(j, 2 + j % 2, n).wait_send()
+    for i in range(3):
+        for source in range(depth):
+            for step in (1, -1):
+
+                @pl.when((step * (z - source) >= 0) & (z + step >= 0) & (z + step < depth))
+                def _():
+                    line_copy(i, source, step).wait_send()
 
 
 def mixer_backward_kernel(
     narrow,
     wide,
-    numbers,
+    step_biases,
+    log_rates,
+    skip_gains,
     xz,
     bc,
     dt,
     marks,
-    wx,
-    bx,
-    wbc,
-    bbc,
+    conv_weight,
+    conv_bias,
     y_in,
     states,
     normed,
     w_xz,
+    start,
+    mixed_in,
+    global_grad,
+    gain,
+    gated_scale,
+    gain_grads,
+    gated_gain_grads,
+    du_blocks,
+    down_parts,
+    middle_parts,
+    gate_sum,
+    up_sum,
+    mix_grad,
+    end_pack,
+    sums,
+    bcdt_grads,
+    xz_grads,
+    down_sum,
+    middle_sums,
+    gate_out,
+    up_out,
+    mix_all,
     w_bcdt,
-    du_blocks,
-    feed_parts,
-    middle_parts,
+    w_sem,
     dwx,
     dwbc,
     dnumbers,
-    rows_grad,
-    xz_grads,
-    feed_sums,
-    middle_sums,
     xz_pad,
     bc_pad,
     dx_pad,
@@ -817,8 +1315,10 @@
     z_got,
     grads,
     grads_got,
-    feed_got,
+    down_got,
     middle_got,
+    gate_got,
+    up_got,
     du_send,
     du_recv,
     core_send,
@@ -829,12 +1329,12 @@
     z_recv,
     grads_send,
     grads_recv,
-    feed_send,
-    feed_recv,
-    feed_sem,
-    middle_send,
-    middle_recv,
-    middle_sem,
+    down_sems,
+    middle_sems,
+    back_send,
+    back_recv,
+    back_own,
+    mix_sems,
 ):
     devices = narrow * wide
     depth = wide // 2
@@ -852,43 +1352,37 @@
     dwx[...] = jnp.zeros_like(dwx)
     dwbc[...] = jnp.zeros_like(dwbc)
     dnumbers[...] = jnp.zeros_like(dnumbers)
-    step_bias, rate_scale, skip = numbers[0], numbers[1], numbers[2]
+    step_bias, rate_scale, skip = head_numbers(step_biases, log_rates, skip_gains, me)
+    wx, bx = head_columns(conv_weight, me), head_columns(conv_bias, me)
+    wbc, bbc = conv_weight[:, DI:], conv_bias[:, DI:]
+    weight_copy = pltpu.make_async_copy(start.at[:, pl.ds(0, 3 * STATE)], w_bcdt, w_sem)
+    weight_copy.start()
 
     def fill(i, carry):
-        start = pl.multiple_of(i * QUERY, QUERY)
-        rows = pl.ds(start, QUERY)
-        xz_pad[pl.ds(start + 8, QUERY), :] = xz[rows, :].astype(FULL)
-        bc_pad[pl.ds(start + 8, QUERY), :] = bc[rows, :].astype(FULL)
+        first = pl.multiple_of(i * QUERY, QUERY)
+        rows = pl.ds(first, QUERY)
+        xz_pad[pl.ds(first + 8, QUERY), :] = xz[rows, :].astype(FULL)
+        bc_pad[pl.ds(first + 8, QUERY), :] = bc[rows, :].astype(FULL)
         return carry
 
     arrived()
     send_blocks(me, devices, wide, du_blocks, du_got, du_send, du_recv)
-    own_feed = pltpu.make_async_copy(feed_parts.at[z_place], feed_got.at[0], feed_sem)
-    own_feed.start()
-
-    def feed_copy(k):
-        place = lax.rem(z_place + k, depth)
-        return remote(
-            feed_parts.at[place],
-            feed_got.at[k],
-            feed_send.at[k - 1],
-            feed_recv.at[k - 1],
-            (n, place * 2 + core),
+    down_line = LineSum(
+        down_parts, down_got, down_sems, z_place, depth, lambda there: (n, there * 2 + core)
+    )
+    middle_line = LineSum(middle_parts, middle_got, middle_sems, n, narrow, lambda there: (there, w))
+    backs = [
+        Returned(
+            values, landed, back_send.at[i], back_recv.at[i], back_own.at[i], n, w, narrow, 0
         )
-
-    own_middle = pltpu.make_async_copy(middle_parts.at[n], middle_got.at[0], middle_sem)
-    own_middle.start()
-
-    def middle_copy(k):
-        m = lax.rem(n + k, narrow)
-        return remote(
-            middle_parts.at[m], middle_got.at[k], middle_send.at[k - 1], middle_recv.at[k - 1], (m, w)
-        )
-
-    for k in range(1, depth):
-        feed_copy(k).start()
-    for k in range(1, narrow):
-        middle_copy(k).start()
+        for i, (values, landed) in enumerate(((gate_sum, gate_got), (up_sum, up_got)))
+    ]
+    mix_gather = StagedGather(mix_grad, mix_all, mix_sems, narrow, depth)
+    mix_gather.start()
+    for back in backs:
+        back.start()
+    middle_line.start()
+    down_line.start()
     du_got[me] = du_blocks[me]
     lax.fori_loop(0, blocks, fill, 0)
     wait_blocks(me, devices, wide, du_got, du_send, du_recv)
@@ -903,11 +1397,11 @@
     def total(v):
         return jnp.sum(jnp.sum(v, axis=1, keepdims=True), axis=0, keepdims=True)
 
-    def conv_back(pad, start, dpre_pad, dpre, weight, dw):
-        mark = marks[pl.ds(start, QUERY), :]
-        window = pad[pl.ds(start, QUERY + 8), :]
-        later = dpre_pad[pl.ds(start, QUERY + 8), :]
-        later_marks = marks[pl.ds(start, QUERY + 8), :]
+    def conv_back(pad, first, dpre_pad, dpre, weight, dw):
+        mark = marks[pl.ds(first, QUERY), :]
+        window = pad[pl.ds(first, QUERY + 8), :]
+        later = dpre_pad[pl.ds(first, QUERY + 8), :]
+        later_marks = marks[pl.ds(first, QUERY + 8), :]
         out = weight[CONV - 1 :] * dpre
         dw[CONV - 1 : CONV, :] += jnp.sum(dpre * window[8:], axis=0, keepdims=True)
         dw[CONV : CONV + 1, :] += jnp.sum(dpre, axis=0, keepdims=True)
@@ -925,11 +1419,11 @@
 
     def block(k, carry):
         i = blocks - 1 - k
-        start = pl.multiple_of(i * QUERY, QUERY)
-        rows = pl.ds(start, QUERY)
+        first = pl.multiple_of(i * QUERY, QUERY)
+        rows = pl.ds(first, QUERY)
         mark = marks[rows, :]
-        pre_x = convolved(xz_pad[pl.ds(start, QUERY + 8), :], mark, wx[...], bx[...])
-        pre = convolved(bc_pad[pl.ds(start, QUERY + 8), :], mark, wbc[...], bbc[...])
+        pre_x = convolved(xz_pad[pl.ds(first, QUERY + 8), :], mark, wx, bx)
+        pre = convolved(bc_pad[pl.ds(first, QUERY + 8), :], mark, wbc, bbc)
         act = jax.nn.silu(pre)
         x, b, c = jax.nn.silu(pre_x)[:, :HEAD_M], act[:, :STATE], act[:, STATE:]
         step = dt[rows, :]
@@ -961,12 +1455,12 @@
         dtotal -= dtail
         dlast = jnp.sum(dtail, axis=0, keepdims=True) + total(dheld * held * kept)
         dlog = tn(lower, jnp.broadcast_to(dtotal, (QUERY, QUERY)), highest)[:, :1] + dlast
-        ddelta -= dlog * rate_scale
+        ddelta -= dlog * rate_scale[:, :1]
         dstep = ddelta * jax.nn.sigmoid(step + step_bias)
         dbcdt[rows, 2 * STATE :] = jnp.where(own_lane, dstep, 0.0).astype(LOW)
         dnumbers[0:1, :] += jnp.broadcast_to(jnp.sum(dstep, axis=0, keepdims=True), (1, 128))
         dnumbers[1:2, :] -= jnp.broadcast_to(
-            jnp.sum(dlog * delta[:, :1] * rate_scale, axis=0, keepdims=True), (1, 128)
+            jnp.sum(dlog * delta[:, :1] * rate_scale[:, :1], axis=0, keepdims=True), (1, 128)
         )
         dnumbers[2:3, :] += jnp.broadcast_to(total(dy * x), (1, 128))
         dstate[...] = dheld * kept + tn(begun_dy, c, highest)
@@ -980,25 +1474,28 @@
     lax.fori_loop(0, blocks, block, 0)
 
     def unconvolve(i, carry):
-        start = pl.multiple_of(i * QUERY, QUERY)
-        rows = pl.ds(start, QUERY)
-        dxr = conv_back(xz_pad, start, dx_pad, dx_pad[rows, :], wx[...], dwx)
+        first = pl.multiple_of(i * QUERY, QUERY)
+        rows = pl.ds(first, QUERY)
+        dxr = conv_back(xz_pad, first, dx_pad, dx_pad[rows, :], wx, dwx)
         left = lax.broadcasted_iota(jnp.int32, dxr.shape, 1) < HEAD_M
         dxz[rows, :] = jnp.where(left, dxr, dxz[rows, :].astype(FULL)).astype(LOW)
         dbcdt[rows, : 2 * STATE] = conv_back(
-            bc_pad, start, dbc_pad, dbc_pad[rows, :], wbc[...], dwbc
+            bc_pad, first, dbc_pad, dbc_pad[rows, :], wbc, dwbc
         ).astype(LOW)
         return carry
 
+    mix_gather.spread()
     lax.fori_loop(0, blocks, unconvolve, 0)
 
     width = normed.shape[1]
     own_rows = xz_grads.shape[1]
 
+    weight_copy.wait()
+
     def rows_of(m, carry):
         for z in range(depth):
-            start = (m * depth + z) * 2 * patches
-            rows = pl.ds(pl.multiple_of(start, 2 * patches), 2 * patches)
+            first = (m * depth + z) * 2 * patches
+            rows = pl.ds(pl.multiple_of(first, 2 * patches), 2 * patches)
             values = nt(dxz[rows, :], w_xz[...]) + nt(dbcdt[rows, :], w_bcdt[...])
             partial_rows[m, z, :, :, :width] = values.astype(LOW).reshape(2, patches, width)
         return carry
@@ -1020,73 +1517,82 @@
     lax.fori_loop(0, narrow, weight_grads, 0)
     to_twin = remote(partial_rows.at[:, :, 1 - core], core_got, core_send, core_recv, twin)
     to_twin.start()
+    send_blocks(me, devices, wide, grads, grads_got, grads_send, grads_recv)
+    grads_got[me] = grads[me]
+    for back, landed, out in zip(backs, (gate_got, up_got), (gate_out, up_out)):
+        back.arrive()
+        out[...] = landed[...].astype(FULL)
     to_twin.wait_recv()
-    for m in range(narrow):
+
+    def narrow_copy(k, m):
+        return remote(
+            core_got.at[m], narrow_got.at[k - 1], narrow_send.at[k - 1], narrow_recv.at[k - 1], (m, w)
+        )
+
+    for k in range(1, narrow):
+        m = lax.rem(n + k, narrow)
         for z in range(depth):
             core_got[m, z] = (
                 core_got[m, z].astype(FULL) + partial_rows[m, z, core].astype(FULL)
             ).astype(LOW)
+        narrow_copy(k, m).start()
+    mix_gather.cross()
+    middle_line.arrive()
+    for z in range(depth):
+        middle_sums[z] = middle_line.total(z).astype(LOW)
     for k in range(1, narrow):
-        m = lax.rem(n + k, narrow)
-        remote(core_got.at[m], narrow_got.at[k - 1], narrow_send.at[k - 1], narrow_recv.at[k - 1], (m, w)).start()
-    for k in range(1, narrow):
-        remote(
-            core_got.at[n], narrow_got.at[k - 1], narrow_send.at[k - 1], narrow_recv.at[k - 1], twin
-        ).wait_recv()
+        narrow_copy(k, n).wait_recv()
     for z in range(depth):
-        total_rows = core_got[n, z].astype(FULL)
+        total_rows = core_got[n, z].astype(FULL) + partial_rows[n, z, core].astype(FULL)
         for k in range(1, narrow):
             total_rows += narrow_got[k - 1, z].astype(FULL)
         z_rows[z] = total_rows.astype(LOW)
+
+    def z_copy(k, place):
+        return remote(
+            z_rows.at[place], z_got.at[k - 1], z_send.at[k - 1], z_recv.at[k - 1], (n, place * 2 + core)
+        )
+
     for k in range(1, depth):
-        place = lax.rem(z_place + k, depth)
-        remote(
-            z_rows.at[place],
-            z_got.at[k - 1],
-            z_send.at[k - 1],
-            z_recv.at[k - 1],
-            (n, place * 2 + core),
-        ).start()
-    send_blocks(me, devices, wide, grads, grads_got, grads_send, grads_recv)
-    grads_got[me] = grads[me]
+        z_copy(k, lax.rem(z_place + k, depth)).start()
+    down_line.arrive()
+    down_sum[...] = down_line.total().astype(LOW)
+    wait_blocks(me, devices, wide, grads_got, grads_send, grads_recv)
+    xz_grads[...] = grads_got[...]
     total_rows = z_rows[z_place].astype(FULL)
     for k in range(1, depth):
-        remote(
-            z_rows.at[z_place], z_got.at[k - 1], z_send.at[k - 1], z_recv.at[k - 1], twin
-        ).wait_recv()
+        z_copy(k, z_place).wait_recv()
         total_rows += z_got[k - 1].astype(FULL)
-    rows_grad[...] = total_rows
-    wait_blocks(me, devices, wide, grads_got, grads_send, grads_recv)
-    xz_grads[...] = grads_got[...]
-    own_middle.wait()
-    for k in range(1, narrow):
-        middle_copy(k).wait_recv()
-    for z in range(depth):
-        middle_total = middle_got[0, z].astype(FULL)
-        for k in range(1, narrow):
-            middle_total += middle_got[k, z].astype(FULL)
-        middle_sums[z] = middle_total.astype(LOW)
-    own_feed.wait()
-    for k in range(1, depth):
-        feed_copy(k).wait_recv()
-    for i in range(3):
-        feed_total = feed_got[0, i].astype(FULL)
-        for k in range(1, depth):
-            feed_total += feed_got[k, i].astype(FULL)
-        feed_sums[i] = feed_total.astype(LOW)
-    for k in range(1, depth):
-        feed_copy(k).wait_send()
-    for k in range(1, narrow):
-        middle_copy(k).wait_send()
+    bcdt_grads[...] = total_rows[:, width:]
+    unit, scale = unit_rows(mixed_in[...])
+    normed_grad = total_rows[:, :width]
+    embed_grad = global_grad[...] + norm_back(normed_grad, gain[...], unit, scale)
+    end_pack[:, :width] = embed_grad.astype(LOW)
+    end_pack[:, width:] = gated_scale[...].astype(LOW)
+    gain_mix_grad = jnp.sum(normed_grad * unit, axis=0, keepdims=True)
+    wide_rows = [gain_mix_grad] + [gated_gain_grads[i : i + 1, :] for i in range(2)]
+    wide_rows += [gain_grads[i : i + 1, :] for i in range(2)]
+    wide_rows += [dwbc[i : i + 1, :] for i in range(CONV + 1)]
+    wide_rows += [dwx[i : i + 1, :] for i in range(CONV + 1)]
+    row = 0
+    for values in wide_rows:
+        for first in range(0, values.shape[1], 128):
+            sums[row : row + 1, :] = values[:, first : first + 128]
+            row += 1
+    lane = lax.broadcasted_iota(jnp.int32, (1, 128), 1)
+    sums[row : row + 1, :] = sum(
+        jnp.where(lane == i, dnumbers[i : i + 1, :], 0.0) for i in range(3)
+    )
+    mix_gather.finish()
+    down_line.finish()
+    middle_line.finish()
+    for back in backs:
+        back.finish()
     to_twin.wait_send()
     for k in range(1, narrow):
-        remote(
-            core_got.at[n], narrow_got.at[k - 1], narrow_send.at[k - 1], narrow_recv.at[k - 1], twin
-        ).wait_send()
+        narrow_copy(k, n).wait_send()
     for k in range(1, depth):
-        remote(
-            z_rows.at[z_place], z_got.at[k - 1], z_send.at[k - 1], z_recv.at[k - 1], twin
-        ).wait_send()
+        z_copy(k, z_place).wait_send()
 
 
 def in_smem():
@@ -1097,29 +1603,98 @@
     return pl.BlockSpec(memory_space=pltpu.VMEM)
 
 
-def mixer_forward(numbers, xz, bc, dt, marks, wx, bx, wbc, bbc):
-    count = xz.shape[0]
-    return pl.pallas_call(
-        mixer_forward_kernel,
+def mixer_front(scalars, start, table, w_xz, gain, conv_weight, conv_bias, turned, middle, collective_id):
+    narrow, wide = lax.axis_size(NARROW), lax.axis_size(WIDE)
+    devices = narrow * wide
+    count = start.shape[0]
+    patches = count // devices
+    dma = pltpu.SemaphoreType.DMA
+
+    def full(*shape):
+        return jax.ShapeDtypeStruct(shape, FULL)
+
+    def low(*shape):
+        return jax.ShapeDtypeStruct(shape, LOW)
+
+    depth = wide // 2
+    anywhere = pl.BlockSpec(memory_space=pl.ANY)
+    outs = pl.pallas_call(
+        partial(mixer_front_kernel, narrow, wide),
         out_shape=[
-            jax.ShapeDtypeStruct((count, HEAD_M), FULL),
-            jax.ShapeDtypeStruct((count, HEAD_M), FULL),
-            jax.ShapeDtypeStruct((count // QUERY, HEAD_M, STATE), FULL),
-        ],
-        in_specs=[in_smem()] + [in_vmem()] * 8,
-        out_specs=[in_vmem()] * 3,
+            low(count, D),
+            low(count, D),
+            low(count, 2 * HEAD_M),
+            low(count, 2 * STATE),
+            full(count, 1),
+            full(count, HEAD_M),
+            full(count, HEAD_M),
+            full(count // QUERY, HEAD_M, STATE),
+            full(patches, D),
+            low(devices, patches, HEAD_M),
+            full(count + 8, 8),
+            full(narrow, patches * PATCH, 1),
+            full(count, PATCH),
+        ]
+        + [low(depth, 2, *part.shape) for part in turned]
+        + [low(narrow, depth, 2, *middle.shape[1:])],
+        in_specs=[in_smem()] * 5 + [in_vmem()] * 6 + [anywhere] * 4,
+        out_specs=[in_vmem()] * 13 + [anywhere] * 4,
         scratch_shapes=[
+            pltpu.VMEM((count, D), FULL),
             pltpu.VMEM((count + 8, 2 * HEAD_M), FULL),
             pltpu.VMEM((count + 8, 2 * STATE), FULL),
             pltpu.VMEM((HEAD_M, STATE), FULL),
+            pltpu.VMEM((devices, patches, HEAD_M), LOW),
+            dma,
+            dma,
+            dma((4,)),
+            dma((3, depth, 2)),
+            dma((3, depth)),
+            dma((3,)),
+            dma((3,)),
+            dma((2, 8, depth)),
         ],
-        compiler_params=pltpu.CompilerParams(vmem_limit_bytes=32 << 20),
-        name="mixer_forward",
-    )(numbers, xz, bc, dt, marks, wx, bx, wbc, bbc)
+        compiler_params=pltpu.CompilerParams(
+            collective_id=collective_id, has_side_effects=True, vmem_limit_bytes=48 << 20
+        ),
+        name="mixer_front",
+    )(*scalars, start, table, w_xz, gain, conv_weight, conv_bias, *turned, middle)
+    gate_all, up_all, down_all, middle_all = outs[13:]
+    return (
+        outs[:13],
+        gate_all.reshape(wide, D, -1),
+        up_all.reshape(wide, D, -1),
+        down_all.reshape(-1, D),
+        middle_all.reshape(D, -1),
+    )
 
 
 def mixer_backward(
-    numbers, xz, bc, dt, marks, wx, bx, wbc, bbc, y, states, normed, w_xz, w_bcdt, du_blocks, feed_parts, middle_parts, collective_id
+    scalars,
+    xz,
+    bc,
+    dt,
+    marks,
+    conv_weight,
+    conv_bias,
+    y,
+    states,
+    normed,
+    w_xz,
+    start,
+    mixed_in,
+    global_grad,
+    gain,
+    gated_scale,
+    gain_grads,
+    gated_gain_grads,
+    du_blocks,
+    down_parts,
+    middle_parts,
+    gate_sum,
+    up_sum,
+    mix_grad,
+    collective_id,
 ):
     narrow, wide = lax.axis_size(NARROW), lax.axis_size(WIDE)
     devices = narrow * wide
@@ -1128,21 +1703,34 @@
     own_rows = width // devices
     dma = pltpu.SemaphoreType.DMA
     low = partial(pltpu.VMEM, dtype=LOW)
-    every = width + w_bcdt.shape[1]
+    every = width + 3 * STATE
+    back_shape = (gate_sum.shape[0] // narrow, gate_sum.shape[1] * narrow)
+    anywhere = pl.BlockSpec(memory_space=pl.ANY)
     return pl.pallas_call(
         partial(mixer_backward_kernel, narrow, wide),
         out_shape=[
-            jax.ShapeDtypeStruct((8, 2 * HEAD_M), FULL),
-            jax.ShapeDtypeStruct((8, 2 * STATE), FULL),
-            jax.ShapeDtypeStruct((8, 128), FULL),
-            jax.ShapeDtypeStruct((patches, every), FULL),
+            jax.ShapeDtypeStruct((patches, width + 128), LOW),
+            jax.ShapeDtypeStruct((SUM_ROWS + CONV + 2, 128), FULL),
+            jax.ShapeDtypeStruct((own_rows, 3 * STATE), FULL),
             jax.ShapeDtypeStruct((devices, own_rows, 2 * HEAD_M), LOW),
-            jax.ShapeDtypeStruct(feed_parts.shape[1:], LOW),
+            jax.ShapeDtypeStruct(down_parts.shape[1:], LOW),
             jax.ShapeDtypeStruct(middle_parts.shape[1:], LOW),
+            jax.ShapeDtypeStruct(back_shape, FULL),
+            jax.ShapeDtypeStruct(back_shape, FULL),
+            jax.ShapeDtypeStruct((narrow, wide // 2, 2) + mix_grad.shape, LOW),
         ],
-        in_specs=[in_smem()] + [in_vmem()] * 14 + [pl.BlockSpec(memory_space=pl.ANY)] * 2,
-        out_specs=[in_vmem()] * 7,
+        in_specs=[in_smem()] * 3
+        + [in_vmem()] * 10
+        + [anywhere]
+        + [in_vmem()] * 7
+        + [anywhere] * 5,
+        out_specs=[in_vmem()] * 8 + [anywhere],
         scratch_shapes=[
+            low((width, 3 * STATE)),
+            dma,
+            pltpu.VMEM((8, 2 * HEAD_M), FULL),
+            pltpu.VMEM((8, 2 * STATE), FULL),
+            pltpu.VMEM((8, 128), FULL),
             pltpu.VMEM((count + 8, 2 * HEAD_M), FULL),
             pltpu.VMEM((count + 8, 2 * STATE), FULL),
             pltpu.VMEM((count + 8, 2 * HEAD_M), FULL),
@@ -1158,8 +1746,10 @@
             low((wide // 2 - 1, patches, every)),
             low((devices, own_rows, 2 * HEAD_M)),
             low((devices, own_rows, 2 * HEAD_M)),
-            low(feed_parts.shape),
+            low(down_parts.shape),
             low(middle_parts.shape),
+            low(back_shape),
+            low(back_shape),
             dma,
             dma,
             dma,
@@ -1170,36 +1760,156 @@
             dma((wide // 2 - 1,)),
             dma,
             dma,
-            dma((wide // 2 - 1,)),
-            dma((wide // 2 - 1,)),
-            dma,
-            dma((narrow - 1,)),
-            dma((narrow - 1,)),
-            dma,
+            dma((wide,)),
+            dma((2 * narrow,)),
+            dma((2, narrow - 1)),
+            dma((2, narrow - 1)),
+            dma((2,)),
+            dma((7,)),
         ],
         compiler_params=pltpu.CompilerParams(
             collective_id=collective_id, has_side_effects=True, vmem_limit_bytes=56 << 20
         ),
         name="mixer_backward",
     )(
-        numbers,
+        *scalars,
         xz,
         bc,
         dt,
         marks,
-        wx,
-        bx,
-        wbc,
-        bbc,
+        conv_weight,
+        conv_bias,
         y,
         states,
         normed,
         w_xz,
-        w_bcdt,
+        start,
+        mixed_in,
+        global_grad,
+        gain,
+        gated_scale,
+        gain_grads,
+        gated_gain_grads,
         du_blocks,
-        feed_parts,
+        down_parts,
         middle_parts,
-    )
+        gate_sum,
+        up_sum,
+        mix_grad,
+    )
+
+
+def finish_kernel(
+    pack_all,
+    mix_all,
+    u,
+    keep,
+    middle,
+    xz_grads,
+    bcdt_grads,
+    gated_gain,
+    embedded,
+    start,
+    table_out,
+    patch_out,
+    in_out,
+    out_out,
+    local_out,
+    query_out,
+    key_out,
+    value_out,
+    attn_out,
+    embedded_own,
+    ids_all,
+    patch_all,
+    rows_of_four,
+    sems,
+):
+    me = lax.axis_index(NARROW) * lax.axis_size(WIDE) + lax.axis_index(WIDE)
+    own_rows = patch_out.shape[0]
+    group = 128 // own_rows
+    columns = pl.ds(pl.multiple_of(lax.div(me, group) * 128, 128), 128)
+    copies = [
+        pltpu.make_async_copy(embedded.at[:, columns], embedded_own, sems.at[0]),
+        pltpu.make_async_copy(start.at[:, pl.ds(3 * STATE, 128)], ids_all, sems.at[1]),
+        pltpu.make_async_copy(start.at[:, pl.ds(4 * STATE, D)], patch_all, sems.at[2]),
+    ]
+    for copy in copies:
+        copy.start()
+    for i, out in enumerate((query_out, key_out, value_out, attn_out)):
+        out[...] = middle[:, i * D : (i + 1) * D]
+    local_out[...] = middle[:, 4 * D :].T
+    for pair in range(0, HEADS_M, 2):
+        both = [xz_grads[pair + i].astype(FULL) for i in range(2)]
+        first = pair * HEAD_M
+        in_out[:, first : first + 128] = jnp.concatenate([v[:, HEAD_M:] for v in both], axis=1)
+        in_out[:, DI + first : DI + first + 128] = jnp.concatenate(
+            [v[:, :HEAD_M] for v in both], axis=1
+        )
+    in_out[:, 2 * DI : 2 * DI + 2 * STATE] = bcdt_grads[:, : 2 * STATE]
+    in_out[:, 2 * DI + 2 * STATE :] = bcdt_grads[:, 2 * STATE : 2 * STATE + HEADS_M]
+    scale = pack_all[:, D:].astype(FULL)[:, :HEAD_M]
+    gain = head_columns(gated_gain, me)[:, :HEAD_M]
+    gated = (u[...] * scale * gain).astype(LOW)
+    out_out[...] = tn(gated, mix_all[...])
+    copies[0].wait()
+    copies[1].wait()
+    grads = pack_all[:, :D]
+    rows_of_four[...] = tn(embedded_own[...], grads)
+    patch_out[...] = rows_of_four[pl.ds(pl.multiple_of(lax.rem(me, group) * own_rows, own_rows), own_rows), :]
+    own_words = table_out.shape[0]
+    count = pack_all.shape[0]
+    lane = lax.broadcasted_iota(jnp.int32, (count, PATCH * own_words), 1)
+    ids = jnp.zeros((count, PATCH * own_words), FULL)
+    kept = jnp.zeros((count, PATCH * own_words), FULL)
+    values = ids_all[...].astype(FULL)
+    for k in range(PATCH):
+        here = lax.div(lane, own_words) == k
+        ids = jnp.where(here, values[:, k : k + 1], ids)
+        kept = jnp.where(here, keep[:, k : k + 1], kept)
+    words = (me * own_words + lax.rem(lane, own_words)).astype(FULL)
+    sums = tn(jnp.where(ids == words, kept, 0.0).astype(LOW), grads)
+    high = sums.astype(LOW)
+    rest = (sums - high.astype(FULL)).astype(LOW)
+    copies[2].wait()
+    table = jnp.zeros(table_out.shape, FULL)
+    for k in range(PATCH):
+        rows = slice(k * own_words, (k + 1) * own_words)
+        weight = patch_all[k * EMB : (k + 1) * EMB, :]
+        table += nt(high[rows], weight) + nt(rest[rows], weight)
+    table_out[...] = table
+
+
+def finish(pack_all, mix_all, u, keep, middle, xz_grads, bcdt_grads, gated_gain, embedded, start):
+    count = pack_all.shape[0]
+    devices, own_rows = xz_grads.shape[:2]
+    anywhere = pl.BlockSpec(memory_space=pl.ANY)
+
+    def full(*shape):
+        return jax.ShapeDtypeStruct(shape, FULL)
+
+    return pl.pallas_call(
+        finish_kernel,
+        out_shape=[
+            full(VOCAB // devices, EMB),
+            full(own_rows, D),
+            full(own_rows, 2 * DI + 2 * STATE + HEADS_M),
+            full(DI // devices, D),
+            full(EMB, own_rows),
+        ]
+        + [full(own_rows, D)] * 4,
+        in_specs=[in_vmem()] * 8 + [anywhere] * 2,
+        out_specs=[in_vmem()] * 9,
+        scratch_shapes=[
+            pltpu.VMEM((count, 128), LOW),
+            pltpu.VMEM((count, 128), LOW),
+            pltpu.VMEM((D, D), LOW),
+            pltpu.VMEM((128, D), FULL),
+            pltpu.SemaphoreType.DMA((3,)),
+        ],
+        compiler_params=pltpu.CompilerParams(vmem_limit_bytes=40 << 20),
+        name="finish",
+    )(pack_all, mix_all, u, keep, middle, xz_grads, bcdt_grads, gated_gain, embedded, start)
 
 
 def patch_causal():
@@ -1415,13 +2125,18 @@
     gated_gain,
     pack,
     feed_parts,
+    gate_parts,
+    up_parts,
     global_out,
+    mix_out,
     scale_out,
     sums,
     gain_grads,
     gated_gain_grads,
     du_blocks,
     rows_out,
+    gate_out,
+    up_out,
     w_attn,
     w_q,
     w_k,
@@ -1436,20 +2151,28 @@
     parts_got,
     grads,
     grads_got,
+    gate_got,
+    up_got,
     sems,
     p_send,
     p_recv,
     t_send,
     t_recv,
+    gate_sems,
+    up_sems,
 ):
     n, wide_place = lax.axis_index(NARROW), lax.axis_index(WIDE)
     core = lax.rem(wide_place, 2)
     twin = (n, wide_place + 1 - 2 * core)
-    barrier = pltpu.get_barrier_semaphore()
-    pl.semaphore_signal(barrier, inc=1, device_id=twin, device_id_type=MESH)
-    for k in range(1, narrow):
-        peer = (lax.rem(n + k, narrow), wide_place)
-        pl.semaphore_signal(barrier, inc=1, device_id=peer, device_id_type=MESH)
+    depth = gate_parts.shape[0]
+    z_place = lax.div(wide_place, 2)
+    lines = [
+        LineSum(parts, landed, line_sems, z_place, depth, lambda there: (n, there * 2 + core))
+        for parts, landed, line_sems in (
+            (gate_parts, gate_got, gate_sems),
+            (up_parts, up_got, up_sems),
+        )
+    ]
 
     def twin_copy(i, columns):
         return remote(
@@ -1473,14 +2196,16 @@
     places = (w_attn, w_q, w_k, w_v, w_local, w_out0, w_out1)
     blocks = [3 * D, 0, D, 2 * D, 6 * D, 4 * D, 5 * D]
     waits = fetched(pack, places, blocks, sems)
-    pl.semaphore_wait(barrier, narrow)
+    greet_lines(narrow, depth)
+    for line in lines:
+        line.start()
     for k in range(1, narrow):
         part_copy(k).start()
     patches = global_out.shape[0]
     unit, scale = unit_rows(after[...])
     grad = feed_in_grad[...].astype(LOW).astype(FULL)
     gain_grads[1:2, :] = jnp.sum(grad * unit, axis=0, keepdims=True)
-    after_grad[...] = cotangent[...].astype(FULL) * keep[...] + norm_back(
+    after_grad[...] = cotangent[...].astype(FULL) * keep[0] + norm_back(
         grad, gains[1:2, :], unit, scale
     )
     attn_grad = after_grad[...].astype(LOW)
@@ -1506,6 +2231,7 @@
     for k in range(PATCH):
         global_out[:, k * EMB : (k + 1) * EMB] = pieces[pl.ds(k, patches, stride=PATCH), :]
     mix_grad = global_out[...].astype(LOW)
+    mix_out[...] = mix_grad
     waits[5]()
     waits[6]()
     inner = [nt(mix_grad, w_out0[...]), nt(mix_grad, w_out1[...])]
@@ -1540,7 +2266,7 @@
         for k in range(1, narrow):
             feed += parts_got[k, :, columns].astype(FULL)
         feed = feed.astype(LOW).astype(FULL)
-        rows_out[:, columns] = ((after[:, columns] + feed) * keep[...]).astype(LOW)
+        rows_out[:, columns] = ((after[:, columns] + feed) * keep[0]).astype(LOW)
 
     def add_twin(i, columns):
         twin_copy(i, columns).wait_recv()
@@ -1559,6 +2285,10 @@
     steps = 4 * D // WEIGHT_STEP
     add_twin(steps, pl.ds(4 * D, EMB))
     lax.fori_loop(0, steps, add_one, 0)
+    for line, out in zip(lines, (gate_out, up_out)):
+        line.arrive()
+        out[...] = line.total().astype(LOW)
+        line.finish()
     twin_copy(steps, pl.ds(4 * D, EMB)).wait_send()
     lax.fori_loop(0, steps, end_one, 0)
     for k in range(1, narrow):
@@ -1580,6 +2310,8 @@
     gated_gain,
     pack,
     feed_parts,
+    gate_parts,
+    up_parts,
     collective_id,
 ):
     narrow = feed_parts.shape[0]
@@ -1594,15 +2326,18 @@
         partial(bytes_backward_kernel, narrow),
         out_shape=[
             full((patches, D), FULL),
+            full((patches, D), LOW),
             full((patches, 128), FULL),
             full((HEADS_M // 2, D // HEADS_M, every), LOW),
             full((2, D), FULL),
             full((2, D), FULL),
             full((HEADS_M, patches, HEAD_M), LOW),
             full((rows, D), LOW),
+            full(gate_parts.shape[1:], LOW),
+            full(up_parts.shape[1:], LOW),
         ],
-        in_specs=[in_vmem()] * 12 + [pl.BlockSpec(memory_space=pl.ANY)] * 2,
-        out_specs=[in_vmem()] * 7,
+        in_specs=[in_vmem()] * 12 + [pl.BlockSpec(memory_space=pl.ANY)] * 4,
+        out_specs=[in_vmem()] * 10,
         scratch_shapes=[pltpu.VMEM((D, D), LOW)] * 4
         + [pltpu.VMEM((D, EMB), LOW)]
         + [pltpu.VMEM((D, D), LOW)] * 2
@@ -1614,14 +2349,18 @@
             pltpu.VMEM((narrow, rows, D), LOW),
             pltpu.VMEM((HEADS_M // 2, 2, D // HEADS_M, every), LOW),
             pltpu.VMEM((HEADS_M // 2, D // HEADS_M, every), LOW),
+            pltpu.VMEM(gate_parts.shape, LOW),
+            pltpu.VMEM(up_parts.shape, LOW),
             pltpu.SemaphoreType.DMA((8,)),
             pltpu.SemaphoreType.DMA((narrow - 1,)),
             pltpu.SemaphoreType.DMA((narrow - 1,)),
             pltpu.SemaphoreType.DMA((4 * D // WEIGHT_STEP + 1,)),
             pltpu.SemaphoreType.DMA((4 * D // WEIGHT_STEP + 1,)),
+            pltpu.SemaphoreType.DMA((2 * gate_parts.shape[0],)),
+            pltpu.SemaphoreType.DMA((2 * gate_parts.shape[0],)),
         ],
         compiler_params=pltpu.CompilerParams(
-            collective_id=collective_id, has_side_effects=True, vmem_limit_bytes=56 << 20
+            collective_id=collective_id, has_side_effects=True, vmem_limit_bytes=60 << 20
         ),
         name="bytes_backward",
     )(
@@ -1639,18 +2378,16 @@
         gated_gain,
         pack,
         feed_parts,
-    )
-
-
-def feed_kernel(
-    narrow,
-    x_in,
-    *refs,
-):
-    g_ins = refs[:narrow]
-    w_in, f_out, gx_out, grads, w, x, g, hid, gg, gu, sent, got = refs[narrow : narrow + 12]
-    twin_out, twin_got = refs[narrow + 12 : narrow + 14]
-    w_sem, g_sem, x_sem, x_send, x_recv, r_send, r_recv, t_send, t_recv = refs[narrow + 14 :]
+        gate_parts,
+        up_parts,
+    )
+
+
+def feed_kernel(narrow, x_in, g_own, g_others, keep, *refs):
+    gate_in, up_in, down_in, f_out, gx_out, gate_sum, up_sum, down_sum = refs[:8]
+    wg, wu, wd, x, xt, g, hid, gg, gu, sent, got = refs[8:19]
+    gate_twin, up_twin, down_twin, gate_got, up_got, down_got = refs[19:25]
+    w_sem, g_sem, x_sem, x_send, x_recv, r_send, r_recv, t_send, t_recv = refs[25:]
     n, wide_place = lax.axis_index(NARROW), lax.axis_index(WIDE)
     core = lax.rem(wide_place, 2)
     twin = (n, wide_place + 1 - 2 * core)
@@ -1659,10 +2396,24 @@
     for k in range(1, narrow):
         peer = (lax.rem(n + k, narrow), wide_place)
         pl.semaphore_signal(barrier, inc=1, device_id=peer, device_id_type=MESH)
+    places, width, share = gate_in.shape
+    rows = x_in.shape[0]
+    hidden = places * share
+    depth = places // 2
+    chunk = 2 * share
     own_x = pltpu.make_async_copy(x_in, x.at[0], x_sem)
     own_x.start()
-    g_copies = [pltpu.make_async_copy(g_ins[k], g.at[k], g_sem.at[k]) for k in range(narrow)]
-    w_copies = [pltpu.make_async_copy(w_in.at[:, i], w.at[i], w_sem.at[i]) for i in range(3)]
+    g_copies = [
+        pltpu.make_async_copy(g_own, g.at[0], g_sem.at[0]),
+        pltpu.make_async_copy(g_others, g.at[pl.ds(1, narrow - 1)], g_sem.at[1]),
+    ]
+    w_copies = [pltpu.make_async_copy(down_in, wd, w_sem.at[2 * places])]
+    for place in range(places):
+        units = slice(place * share, (place + 1) * share)
+        w_copies.append(pltpu.make_async_copy(gate_in.at[place], wg.at[:, units], w_sem.at[place]))
+        w_copies.append(
+            pltpu.make_async_copy(up_in.at[place], wu.at[:, units], w_sem.at[places + place])
+        )
     g_copies[0].start()
     for copy in w_copies:
         copy.start()
@@ -1671,24 +2422,12 @@
     pl.semaphore_wait(barrier, narrow)
 
     def x_copy(k):
-        return pltpu.make_async_remote_copy(
-            src_ref=x_in,
-            dst_ref=x.at[k],
-            send_sem=x_send.at[k - 1],
-            recv_sem=x_recv.at[k - 1],
-            device_id=(lax.rem(n + narrow - k, narrow), wide_place),
-            device_id_type=MESH,
-        )
+        peer = (lax.rem(n + narrow - k, narrow), wide_place)
+        return remote(x_in, x.at[k], x_send.at[k - 1], x_recv.at[k - 1], peer)
 
     def r_copy(k):
-        return pltpu.make_async_remote_copy(
-            src_ref=sent.at[k - 1],
-            dst_ref=got.at[k - 1],
-            send_sem=r_send.at[k - 1],
-            recv_sem=r_recv.at[k - 1],
-            device_id=(lax.rem(n + k, narrow), wide_place),
-            device_id_type=MESH,
-        )
+        peer = (lax.rem(n + k, narrow), wide_place)
+        return remote(sent.at[k - 1], got.at[k - 1], r_send.at[k - 1], r_recv.at[k - 1], peer)
 
     for k in range(1, narrow):
         x_copy(k).start()
@@ -1697,28 +2436,21 @@
         copy.wait()
     for copy in g_copies:
         copy.wait()
-    rows, width = x_in.shape
-    places, share = w.shape[1], w.shape[2]
-    hidden = places * share
-    chunk = 2 * share
-
-    def weights(i, start):
-        return w[i, pl.ds(start, 2)].reshape(chunk, width)
-
-    def columns(i, first):
-        return w[i, :, :, first : first + chunk].reshape(hidden, chunk)
 
     def block(k, carry):
         @pl.when(k > 0)
         def _():
             x_copy(k).wait_recv()
 
-        xk, gk = x[k], g[k]
-        for place in range(0, places, 2):
-            units = slice(place * share, place * share + chunk)
-            gate = nt(xk, weights(0, place))
-            up = nt(xk, weights(1, place))
-            dhid = nt(gk, weights(2, place))
+        xk = x[k]
+        gk = (g[k].astype(FULL) * keep[k]).astype(LOW)
+        g[k] = gk
+        xt[k] = xk.T
+        for first in range(0, hidden, chunk):
+            units = slice(first, first + chunk)
+            gate = nn(xk, wg[:, units])
+            up = nn(xk, wu[:, units])
+            dhid = nt(gk, wd[units, :])
             s = jax.nn.sigmoid(gate)
             act = gate * s
             hid[k, :, units] = (act * up).astype(LOW)
@@ -1726,116 +2458,134 @@
             gu[k, :, units] = (dhid * act).astype(LOW)
         ggk, guk, hidk = gg[k], gu[k], hid[k]
         for first in range(0, width, chunk):
-            gx = nn(ggk, columns(0, first)) + nn(guk, columns(1, first))
+            columns = slice(first, first + chunk)
+            gx = nt(ggk, wg[columns, :]) + nt(guk, wu[columns, :])
 
             @pl.when(k == 0)
             def _():
-                gx_out[:, first : first + chunk] = gx
+                gx_out[:, columns] = gx
 
             @pl.when(k > 0)
             def _():
-                sent[k - 1, :, first : first + chunk] = gx.astype(LOW)
+                sent[k - 1, :, columns] = gx.astype(LOW)
 
         @pl.when(k > 0)
         def _():
             r_copy(k).start()
 
         for first in range(0, width, chunk):
-            f_out[k, :, first : first + chunk] = nn(hidk, columns(2, first)).astype(LOW)
+            columns = slice(first, first + chunk)
+            f_out[k, :, columns] = nn(hidk, wd[:, columns]).astype(LOW)
         return carry
 
     lax.fori_loop(0, narrow, block, 0)
 
-    depth = places // 2
-
-    def weight_grads(place, i, first, columns):
-        left, right = ((gg, x), (gu, x), (hid, g))[i]
-        units = pl.ds(pl.multiple_of(place * share, share), share)
-        lhs = left[:, :, units].reshape(narrow * rows, share)
-        rhs = right[:, :, first : first + columns].reshape(narrow * rows, columns)
-        return tn(lhs, rhs)
-
-    def t_copy(j):
-        return remote(twin_out.at[j], twin_got.at[j], t_send.at[j], t_recv.at[j], twin)
+    def units_of(j, of_core):
+        start = (2 * j + of_core) * share
+        return pl.ds(pl.multiple_of(start, share), share)
+
+    def columns_grads(left, j, of_core):
+        total = jnp.zeros((width, chunk), FULL)
+        for k in range(narrow):
+            pair = [left[k, :, units_of(2 * j + i, of_core)] for i in range(2)]
+            total += nn(xt[k], jnp.concatenate(pair, axis=1))
+        return total[:, :share], total[:, share:]
+
+    def rows_grads(j, of_core):
+        lhs = hid[:, :, units_of(j, of_core)].reshape(narrow * rows, share)
+        return tn(lhs, g[...].reshape(narrow * rows, width))
+
+    outs = (gate_twin, up_twin, down_twin)
+    ins = (gate_got, up_got, down_got)
+
+    def t_copy(i, j):
+        return remote(outs[i].at[j], ins[i].at[j], t_send.at[i, j], t_recv.at[i, j], twin)
 
     def for_twin(j, carry):
-        for i in range(3):
-            for first in range(0, width, 2 * chunk):
-                twin_out[j, i, :, first : first + 2 * chunk] = weight_grads(
-                    2 * j + 1 - core, i, first, 2 * chunk
-                ).astype(LOW)
-        t_copy(j).start()
+        for i, left in enumerate((gg, gu)):
+            for half, part in enumerate(columns_grads(left, j, 1 - core)):
+                outs[i][2 * j + half] = part.astype(LOW)
+                t_copy(i, 2 * j + half).start()
+        for half in range(2):
+            outs[2][2 * j + half] = rows_grads(2 * j + half, 1 - core).astype(LOW)
+            t_copy(2, 2 * j + half).start()
         return carry
 
     def for_own(j, carry):
-        t_copy(j).wait_recv()
-        for i in range(3):
-            for first in range(0, width, 2 * chunk):
-                columns = slice(first, first + 2 * chunk)
-                part = weight_grads(2 * j + core, i, first, 2 * chunk)
-                grads[j, i, :, columns] = (
-                    part + twin_got[j, i, :, columns].astype(FULL)
-                ).astype(LOW)
+        for i, (left, total) in enumerate(((gg, gate_sum), (gu, up_sum))):
+            for half, part in enumerate(columns_grads(left, j, core)):
+                t_copy(i, 2 * j + half).wait_recv()
+                total[2 * j + half] = (part + ins[i][2 * j + half].astype(FULL)).astype(LOW)
+        for half in range(2):
+            part = rows_grads(2 * j + half, core)
+            t_copy(2, 2 * j + half).wait_recv()
+            down_sum[2 * j + half] = (part + ins[2][2 * j + half].astype(FULL)).astype(LOW)
         return carry
 
-    lax.fori_loop(0, depth, for_twin, 0)
-    lax.fori_loop(0, depth, for_own, 0)
+    lax.fori_loop(0, depth // 2, for_twin, 0)
+    lax.fori_loop(0, depth // 2, for_own, 0)
     for k in range(1, narrow):
         r_copy(k).wait_recv()
         gx_out[...] += got[k - 1].astype(FULL)
     for k in range(1, narrow):
         x_copy(k).wait_send()
         r_copy(k).wait_send()
-    for j in range(depth):
-        t_copy(j).wait_send()
-
-
-def feed_forward_back(x_own, g_blocks, feed_all, collective_id):
-    narrow = len(g_blocks)
+    for i in range(3):
+        for j in range(depth):
+            t_copy(i, j).wait_send()
+
+
+def feed_forward_back(x_own, g_own, g_others, keep, gate_all, up_all, down_all, collective_id):
+    narrow = keep.shape[0]
     rows, width = x_own.shape
-    places, _, share, _ = feed_all.shape
+    places, _, share = gate_all.shape
+    hidden, depth = places * share, places // 2
     dma = pltpu.SemaphoreType.DMA
     anywhere = pl.BlockSpec(memory_space=pl.ANY)
 
-    def rows_scratch(count, columns):
-        return pltpu.VMEM((count, rows, columns), LOW)
-
-    hidden = places * share
+    def low(*shape):
+        return pltpu.VMEM(shape, LOW)
+
+    sums = [(depth, width, share), (depth, width, share), (depth, share, width)]
     return pl.pallas_call(
         partial(feed_kernel, narrow),
         out_shape=[
             jax.ShapeDtypeStruct((narrow, rows, width), LOW),
             jax.ShapeDtypeStruct((rows, width), FULL),
-            jax.ShapeDtypeStruct((places // 2,) + feed_all.shape[1:], LOW),
-        ],
-        in_specs=[anywhere] * (narrow + 2),
-        out_specs=[in_vmem()] * 3,
+        ]
+        + [jax.ShapeDtypeStruct(shape, LOW) for shape in sums],
+        in_specs=[anywhere] * 3 + [in_vmem()] + [anywhere] * 3,
+        out_specs=[in_vmem()] * 5,
         scratch_shapes=[
-            pltpu.VMEM((3, places, share, width), LOW),
-            rows_scratch(narrow, width),
-            rows_scratch(narrow, width),
-            rows_scratch(narrow, hidden),
-            rows_scratch(narrow, hidden),
-            rows_scratch(narrow, hidden),
-            rows_scratch(narrow - 1, width),
-            rows_scratch(narrow - 1, width),
-            pltpu.VMEM((places // 2,) + feed_all.shape[1:], LOW),
-            pltpu.VMEM((places // 2,) + feed_all.shape[1:], LOW),
-            dma((3,)),
-            dma((narrow,)),
+            low(width, hidden),
+            low(width, hidden),
+            low(hidden, width),
+            low(narrow, rows, width),
+            low(narrow, width, rows),
+            low(narrow, rows, width),
+            low(narrow, rows, hidden),
+            low(narrow, rows, hidden),
+            low(narrow, rows, hidden),
+            low(narrow - 1, rows, width),
+            low(narrow - 1, rows, width),
+        ]
+        + [low(*shape) for shape in sums + sums]
+        + [
+            dma((2 * places + 1,)),
+            dma((2,)),
             dma,
             dma((narrow - 1,)),
             dma((narrow - 1,)),
             dma((narrow - 1,)),
             dma((narrow - 1,)),
-            dma((places // 2,)),
-            dma((places // 2,)),
+            dma((3, depth)),
+            dma((3, depth)),
         ],
         compiler_params=pltpu.CompilerParams(
-            collective_id=collective_id, has_side_effects=True, vmem_limit_bytes=58 << 20
+            collective_id=collective_id, has_side_effects=True, vmem_limit_bytes=44 << 20
         ),
         name="feed",
-    )(x_own, *g_blocks, feed_all)
+    )(x_own, g_own, g_others, keep, gate_all, up_all, down_all)
 
 
 def per_device_heads(
@@ -1875,31 +2625,13 @@
     hidden_width = gate_weight.shape[1]
     share = hidden_width // narrow
 
-    segment, _, keep_all = patch_layout(doc_patches, pad_bytes, 0, everything)
-    keep_all = keep_all.reshape(everything, PATCH)
-    place = jnp.arange(everything)
-    mark_columns = [segment.astype(FULL)]
-    for lag in range(1, CONV):
-        earlier = jnp.concatenate([jnp.full((lag,), -1, jnp.int32), segment[:-lag]])
-        mark_columns.append((earlier == segment).astype(FULL))
-    by_block = segment.reshape(-1, QUERY)
-    before = jnp.concatenate([jnp.full((1,), -1, jnp.int32), by_block[:-1, -1]])
-    mark_columns.append((by_block == before[:, None]).astype(FULL).reshape(-1))
-    mark_columns.append((by_block == by_block[:, -1:]).astype(FULL).reshape(-1))
-    mark_columns.append(
-        jnp.broadcast_to((by_block[:, -1:] == before[:, None]).astype(FULL), by_block.shape).reshape(-1)
-    )
-    mark_columns.append(jnp.zeros((everything,), FULL))
-    marks = jnp.pad(jnp.stack(mark_columns, axis=1), ((0, 8), (0, 0)))
-    keep_rows = lax.dynamic_slice_in_dim(keep_all, device * patches, patches).reshape(-1)
-
     ids_low = byte_ids.astype(LOW).reshape(patches, PATCH)
     bcdt_width = 2 * STATE + HEADS_M
     start_pack = jnp.concatenate(
         [
-            patch_weight,
             jnp.pad(in_weight[:, 2 * DI :], ((0, 0), (0, 96))),
             jnp.pad(ids_low, ((0, 0), (0, 120))),
+            patch_weight,
         ],
         axis=1,
     )
@@ -1910,8 +2642,6 @@
         ],
         axis=2,
     ).transpose(1, 0, 2)
-    xz_weight = exchange(xz_blocks, BOTH).reshape(D, 2 * HEAD_M)
-    start_all, table_all = gather_all([start_pack, byte_table], 0)
     middle_pack = jnp.concatenate(
         [
             query_weight,
@@ -1924,51 +2654,31 @@
         ],
         axis=1,
     )
-    middle_all = lax.all_gather(middle_pack, BOTH, axis=0, tiled=True)
-    feed_blocks = jnp.stack(
-        [
-            gate_weight.T.reshape(narrow, share, -1),
-            up_weight.T.reshape(narrow, share, -1),
-            down_weight.reshape(narrow, share, -1),
-        ],
-        axis=1,
-    )
-    feed_turned = exchange(feed_blocks, NARROW).transpose(1, 2, 0, 3).reshape(3, share, D)
-    feed_all = lax.all_gather(feed_turned, WIDE)
-
-    patch_all = start_all[:, :D]
-    bcdt_weight = start_all[:, D : D + bcdt_width]
-    ids_all = start_all[:, D + 384 : D + 384 + PATCH].astype(jnp.int32)
-
-    vocabulary = jnp.arange(VOCAB, dtype=jnp.int32)
-    onehot = (ids_all[:, :, None] == vocabulary).astype(LOW) * keep_all[:, :, None].astype(LOW)
-    embedded = (
-        jnp.dot(onehot.reshape(everything * PATCH, VOCAB), table_all, preferred_element_type=FULL)
-        .astype(LOW)
-        .reshape(everything, D)
-    )
-    mixed_all = jnp.dot(embedded, patch_all, preferred_element_type=FULL)
-    normed_all = root_norm(mixed_all, gain_mix).astype(LOW)
-    xz = jnp.dot(normed_all, xz_weight, preferred_element_type=FULL).astype(LOW)
-    bcdt = jnp.dot(normed_all, bcdt_weight, preferred_element_type=FULL).astype(LOW)
-    bc = bcdt[:, : 2 * STATE]
-    dt = lax.dynamic_slice_in_dim(bcdt[:, 2 * STATE :], device, 1, axis=1).astype(FULL)
-    mixed_in = lax.dynamic_slice_in_dim(mixed_all, device * patches, patches)
-
-    conv_x = lax.dynamic_slice_in_dim(conv_weight, device * HEAD_M, HEAD_M, axis=1)
-    bias_x = lax.dynamic_slice_in_dim(conv_bias, device * HEAD_M, HEAD_M)[None]
-    conv_x = jnp.pad(conv_x, ((0, 0), (0, HEAD_M)))
-    bias_x = jnp.pad(bias_x, ((0, 0), (0, HEAD_M)))
-    conv_bc = conv_weight[:, DI:]
-    bias_bc = conv_bias[None, DI:]
-
-    def own(values):
-        return lax.dynamic_index_in_dim(values, device, 0, False)
-
-    numbers = jnp.stack([own(step_bias), jnp.exp(own(log_rate)), own(skip_gain)])
-    mixer_args = (numbers, xz, bc, dt, marks, conv_x, bias_x, conv_bc, bias_bc)
-    u, y, states = mixer_forward(*mixer_args)
-    u_blocks = exchange(u.astype(LOW).reshape(devices, patches, HEAD_M), BOTH)
+    start_all, table_all, xz_weight, *turned, middle_line, others = start_weights(
+        start_pack,
+        byte_table,
+        xz_blocks,
+        gate_weight,
+        up_weight,
+        down_weight,
+        middle_pack,
+        cotangent,
+        0,
+    )
+    numbers = (step_bias, log_rate, skip_gain)
+    conv = (conv_weight, conv_bias[None])
+    front, gate_all, up_all, down_all, middle_all = mixer_front(
+        (doc_patches, pad_bytes) + numbers,
+        start_all,
+        table_all,
+        xz_weight,
+        gain_mix[None],
+        *conv,
+        turned,
+        middle_line,
+        5,
+    )
+    embedded, normed_all, xz, bc, dt, u, y, states, mixed_in, u_blocks, marks, keep_rows, keep_all = front
     half = HEAD_M // 2
     gated_gain_split = gated_gain.reshape(devices, 2, half).transpose(1, 0, 2).reshape(2, D)
 
@@ -1983,27 +2693,25 @@
         after_attn,
         normed_feed,
     ) = bytes_forward(u_blocks, mixed_in, byte_gains, gated_gain_split, middle_all)
-    feed_grad = (cotangent.astype(FULL) * keep_rows[:, None]).astype(LOW)
-
-    def passed_narrow(values, by):
-        pairs = [(i, (i + by) % narrow) for i in range(narrow)]
-        return lax.ppermute(values, NARROW, pairs)
-
-    g_blocks = [feed_grad] + [passed_narrow(feed_grad, narrow - k) for k in range(1, narrow)]
-    feed_parts, feed_in_grad, feed_grads = feed_forward_back(normed_feed, g_blocks, feed_all, 2)
+    feed_parts, feed_in_grad, gate_parts, up_parts, down_parts = feed_forward_back(
+        normed_feed, cotangent, others, keep_rows, gate_all, up_all, down_all, 2
+    )
 
     (
         global_grad,
+        mix_grad,
         gated_scale,
         middle_parts,
         byte_gain_grads,
         gated_gain_grads,
         du_blocks,
         out_rows,
+        gate_sum,
+        up_sum,
     ) = bytes_backward(
         feed_in_grad,
         cotangent,
-        keep_rows[:, None],
+        keep_rows,
         after_attn,
         stream,
         normed_attn,
@@ -2015,98 +2723,83 @@
         gated_gain_split,
         middle_all,
         feed_parts,
+        gate_parts,
+        up_parts,
         4,
     )
     middle_parts = middle_parts.reshape(narrow, wide // 2, own_rows, -1)
-    grad_gated_gain = gated_gain_grads.reshape(2, devices, half).transpose(1, 0, 2).reshape(DI)
-    grad_gain_attn, grad_feed_gain = byte_gain_grads[0], byte_gain_grads[1]
-
-    mix_grad = global_grad.astype(LOW)
-    bcdt_padded = start_all[:, D : D + 3 * STATE]
-    dwx, dwbc, dnumbers, rows_grad, xz_grads, feed_sums, middle_sums = mixer_backward(
-        *mixer_args,
+
+    (
+        end_pack,
+        sums_pack,
+        bcdt_grads,
+        xz_grads,
+        down_sum,
+        middle_sums,
+        grad_gate,
+        grad_up,
+        mix_grad_all,
+    ) = mixer_backward(
+        numbers,
+        xz,
+        bc,
+        dt,
+        marks,
+        *conv,
         y,
         states,
         normed_all,
         xz_weight,
-        bcdt_padded,
+        start_all,
+        mixed_in,
+        global_grad,
+        gain_mix[None],
+        gated_scale,
+        byte_gain_grads,
+        gated_gain_grads,
         du_blocks,
-        feed_grads,
+        down_parts,
         middle_parts,
+        gate_sum,
+        up_sum,
+        mix_grad,
         3,
     )
-    normed_mix_grad, bcdt_grads = rows_grad[:, :D], rows_grad[:, D:]
-    feed_sums = feed_sums.reshape(3, share, narrow, D // narrow).transpose(2, 0, 1, 3)
-    grad_xz = xz_grads.astype(FULL).transpose(1, 0, 2)
-    _, mix_norm_back = jax.vjp(root_norm, mixed_in, gain_mix)
-    mixed_norm_grad, grad_gain_mix = mix_norm_back(normed_mix_grad)
-    embed_grad = (global_grad + mixed_norm_grad).astype(LOW)
-
-    end_pack = jnp.concatenate(
-        [
-            embed_grad,
-            mix_grad,
-            gated_scale.astype(LOW),
-        ],
-        axis=1,
-    )
-    sums_pack = jnp.concatenate(
-        [
-            grad_gain_mix,
-            grad_gated_gain,
-            grad_gain_attn,
-            grad_feed_gain,
-            dwbc[: CONV + 1].reshape(-1),
-            dwx[: CONV + 1, :HEAD_M].reshape(-1),
-            dnumbers[:3, 0],
-        ]
-    )
-    sums_width = -(-sums_pack.shape[0] // 1024) * 1024
-    sums_pack = jnp.pad(sums_pack, (0, sums_width - sums_pack.shape[0])).reshape(-1, 128)
-    end_all, sums_all, middle_sums, feed_sums = gather_all(
-        [end_pack, sums_pack], 1, middle_sums, feed_sums
-    )
-    feed_sums = feed_sums.transpose(1, 0, 2, 3).astype(FULL).reshape(3, hidden_width, D // narrow)
-    grad_gate, grad_up, grad_down = feed_sums[0].T, feed_sums[1].T, feed_sums[2]
-    sums_all = sums_all.reshape(devices, sums_width)
-    embed_grad_all = end_all[:, :D]
-    mix_grad_all = end_all[:, D : 2 * D]
-    scale_all = end_all[:, 2 * D : 2 * D + 1].astype(FULL)
-    gain_own = lax.dynamic_slice_in_dim(gated_gain, device * HEAD_M, HEAD_M)
-    grad_out = tn((u * scale_all * gain_own).astype(LOW), mix_grad_all)
-    grad_in = jnp.concatenate(
-        [
-            grad_xz[:, :, HEAD_M:].reshape(own_rows, DI),
-            grad_xz[:, :, :HEAD_M].reshape(own_rows, DI),
-            bcdt_grads[:, :bcdt_width],
-        ],
-        axis=1,
-    )
-    embedded_own = lax.dynamic_slice_in_dim(embedded, device * own_rows, own_rows, axis=1)
-    grad_patch = tn(embedded_own, embed_grad_all)
-    own_words = byte_table.shape[0]
-    words = device * own_words + jnp.arange(own_words, dtype=jnp.int32)
-    chosen = (ids_all[:, :, None] == words).astype(LOW) * keep_all[:, :, None].astype(LOW)
-    word_sums = tn(chosen.reshape(everything, PATCH * own_words), embed_grad_all)
-    grad_table = jnp.einsum(
-        "kvd,ked->ve",
-        word_sums.reshape(PATCH, own_words, D),
-        patch_all.astype(FULL).reshape(PATCH, EMB, D),
-        precision=highest,
-    )
-
-    owned = 3 * D + DI + (CONV + 1) * 2 * STATE
-    small = jnp.sum(sums_all[:, :owned], axis=0)
+    mix_grad_all = mix_grad_all.reshape(everything, D)
+
+    end_all, sums_all, middle_sums, grad_down = end_gather(
+        end_pack, sums_pack, middle_sums, down_sum, 1
+    )
+    (
+        grad_table,
+        grad_patch,
+        grad_in,
+        grad_out,
+        grad_local,
+        grad_query,
+        grad_key,
+        grad_value,
+        grad_attn,
+    ) = finish(
+        end_all,
+        mix_grad_all,
+        u,
+        keep_all,
+        middle_sums,
+        xz_grads,
+        bcdt_grads,
+        gated_gain[None],
+        embedded,
+        start_all,
+    )
+    small = jnp.sum(sums_all[:, :SUM_ROWS], axis=0).reshape(-1)
     gain_grads = jnp.split(small[: 3 * D + DI], [D, D + DI, 2 * D + DI])
-    conv_own = sums_all[:, owned : owned + (CONV + 1) * HEAD_M].reshape(devices, CONV + 1, HEAD_M)
+    gain_grads[1] = gain_grads[1].reshape(2, devices, half).transpose(1, 0, 2).reshape(DI)
+    conv_own = sums_all[:, SUM_ROWS : SUM_ROWS + CONV + 1, :HEAD_M].transpose(1, 0, 2)
     conv_grads = jnp.concatenate(
-        [
-            conv_own.transpose(1, 0, 2).reshape(CONV + 1, DI),
-            small[3 * D + DI :].reshape(CONV + 1, 2 * STATE),
-        ],
-        axis=1,
-    )
-    number_grads = sums_all[:, owned + (CONV + 1) * HEAD_M : owned + (CONV + 1) * HEAD_M + 3].T
+        [conv_own.reshape(CONV + 1, DI), small[3 * D + DI :].reshape(CONV + 1, 2 * STATE)], axis=1
+    )
+    number_grads = sums_all[:, SUM_ROWS + CONV + 1, :3].T
     return (
         out_rows,
         grad_table,
@@ -2120,12 +2813,12 @@
         number_grads[2],
         gain_grads[1],
         grad_out,
-        middle_sums[:, 4 * D :].T,
+        grad_local,
         gain_grads[2],
-        middle_sums[:, :D],
-        middle_sums[:, D : 2 * D],
-        middle_sums[:, 2 * D : 3 * D],
-        middle_sums[:, 3 * D : 4 * D],
+        grad_query,
+        grad_key,
+        grad_value,
+        grad_attn,
         gain_grads[3],
         grad_gate,
         grad_up,

time: 508 us -> 461 us (0.907)
  Pallas kernels: 340 us -> 408 us
  matrix products: 23.8 us -> 0 us
  local copies, waits for them, and re-layouts: 59.2 us -> 38.6 us
  waiting for transfers between devices: 17.9 us -> 0 us
  blocking collectives: 15.7 us -> 0 us
  starting transfers between devices: 15.4 us -> 0 us
  between operations: 16.2 us -> 1.75 us
  other arithmetic: 11.5 us -> 3.86 us
    pallas_call x3 -> x4, Pallas kernels: 125 us -> 178 us  [the longest x1 72.5 us: mixer_front(): pl.pallas_call(partial(mixer_front_kernel, narrow, wide), out_shape=[low(...]
    dot_general x8 -> x0, matrix products: 23.8 us -> none  [the longest x3 7.69 us: tn(): lax.dot_general(a, b, (((0,), (0,)), ((), ())), precision=precision, pref...]
    pallas_call x1, Pallas kernels: 37.9 us -> 56.7 us  [bytes_backward(): pl.pallas_call(partial(bytes_backward_kernel, narrow), out_shape=[full((p...]
    all_gather x2 -> x0, waiting for transfers between devices: 17.8 us -> none  [the longest x1 17.8 us: per_device_heads(): feed_all = lax.all_gather(feed_turned, WIDE)]
    all_to_all x1 -> x0, blocking collectives: 15.7 us -> none  [exchange(): return lax.all_to_all(blocks, axis, split_axis=0, concat_axis=0, tiled=True)]
    unnamed x130 -> x127, local copies, waits for them, and re-layouts: 18.6 us -> 31.1 us
    all_to_all x2 -> x0, starting transfers between devices: 11.8 us -> none  [exchange(): return lax.all_to_all(blocks, axis, split_axis=0, concat_axis=0, tiled=True)]
    slice x19 -> x1, local copies, waits for them, and re-layouts: 10.8 us -> 0.02 us  [per_device_heads(): number_grads = sums_all[:, SUM_ROWS + CONV + 1, :3].T]
  transfers between devices with their start and end apart: 7 -> 0, of which waited for: 2 -> 0; matrix products, arithmetic and copies ran while one was open for 10% -> 0% of each run, Pallas kernels for 15% -> 0%
where the time goes in v4:
time: 461 us; the launch traced here: 452 us
  Pallas kernels  408 us (89%)
  local copies, waits for them, and re-layouts  38.6 us (8%)
    pallas_call x1, Pallas kernels, mixer_backward(): pl.pallas_call(partial(mixer_backward_kernel, narrow, wide), out_shape=[j...  109 us
    pallas_call x1, Pallas kernels, mixer_front(): pl.pallas_call(partial(mixer_front_kernel, narrow, wide), out_shape=[low(...  72.5 us
    pallas_call x1, Pallas kernels, start_weights(): pl.pallas_call(partial(start_kernel, narrow, wide), out_shape=[low(narrow...  61 us
    pallas_call x1, Pallas kernels, bytes_backward(): pl.pallas_call(partial(bytes_backward_kernel, narrow), out_shape=[full((p...  56.7 us
    pallas_call x1, Pallas kernels, feed_forward_back(): pl.pallas_call(partial(feed_kernel, narrow), out_shape=[jax.ShapeDtypeStr...  49.6 us
    pallas_call x1, Pallas kernels, end_gather(): pl.pallas_call(partial(end_kernel, narrow, depth), out_shape=[jax.ShapeDt...  38.8 us
    unnamed x127, local copies, waits for them, and re-layouts  31.1 us
    pallas_call x1, Pallas kernels, bytes_forward(): pl.pallas_call(bytes_forward_kernel, out_shape=[full((2, patches, D), FUL...  14.1 us

profile of v4, /device:TPU:9, one launch (start us, length us, event | category | flops | bytes accessed | tf_op | source)
XLA Modules:
  0.0 451.9 jit_solution(15210736519268760732)
XLA Ops:
  0.7 0.7 convert_element_type.7
  1.5 0.7 pad_maximum_fusion.gains
  2.3 0.7 broadcast_in_dim.11.conv_bias
  3.0 0.7 slice.53
  3.7 0.8 reshape.119
  4.7 1.5 fusion.4.pack
  6.1 1.0 fusion.5
  7.9 0.9 maximum_bitcast_fusion.xz_blocks
  8.9 0.7 copy-done.47
  9.7 61.0 %start_weights.1 = (bf16[4,4,2,32,1536]{4,3,2,1,0:T(8,128)(2,1)}, bf16[4,4,2,8,128]{4,3,2,1,0:T(8,128)(2,1)}, bf16[32,32,128]{2,1,0:T(8,128)(2,1)}, bf16[1024,12...) custom-call(bf16[32,1536]{1,0:T(8,128)(2,1)} %fusion.4.pack, ...), custom_call_target="tpu_custom_call" | custom-call | tf_op jit(solution)/shard_map/start_weights/pallas_call | solution.py:796
  70.8 0.9 copy-done.9
  71.8 0.9 copy-done.27
  72.7 0.9 copy-done.28
  73.7 0.9 copy-done.29
  74.6 0.8 copy-done.37
  75.5 72.5 %mixer_front.1 = (bf16[1024,1024]{1,0:T(8,128)(2,1)}, bf16[1024,1024]{1,0:T(8,128)(2,1)}, bf16[1024,128]{1,0:T(8,128)(2,1)S(1)}, bf16[1024,256]{1,0:T(8,128)(2,1...) custom-call(s32[9]{0:T(128)S(1)} %copy-done.45, ...), custom_call_target="tpu_custom_call" | custom-call | tf_op jit(solution)/shard_map/mixer_front/pallas_call | solution.py:1621
  148.0 0.8 copy-done.16
  148.8 0.8 copy-done.18
  149.6 0.8 copy-done.20
  150.4 0.7 copy-done.23
  151.1 14.1 %bytes_forward.1 = (f32[2,32,1024]{2,1,0:T(8,128)S(1)}, bf16[256,128]{1,0:T(8,128)(2,1)S(1)}, f32[256,1024]{1,0:T(8,128)S(1)}, bf16[256,1024]{1,0:T(8,128)(2,1)S...) custom-call(bf16[32,32,64]{2,1,0:T(8,128)(2,1)S(1)} %get-tuple-eleme, ...), custom_call_target="tpu_custom_call" | custom-call | tf_op jit(solution)/shard_map/bytes_forward/pallas_call | solution.py:2089
  165.2 1.1 copy-done.7
  166.4 1.0 copy-done.11
  167.4 1.0 copy-done.12
  168.4 0.8 copy-done.21
  169.1 0.8 copy-done.22
  169.9 0.7 copy-done.25
  171.3 49.6 %feed.1 = (bf16[4,256,1024]{2,1,0:T(8,128)(2,1)S(1)}, f32[256,1024]{1,0:T(8,128)S(1)}, bf16[4,1024,128]{2,1,0:T(8,128)(2,1)S(1)}, bf16[4,1024,128]{2,1,0:T(8,128)(2,1)S(1)}, bf16[4,128,1024]{2,1,0:T(8,128)(2,1)S(1)}) custom-call(bf16[256,1024]{1,0:T(8,128)(2,1)S(1)} %get-tuple-element.102.x_in, bf16[256,1024]{1,0:T(8,128)(2,1)S(1)} %copy-done.1, ...), custom_call_target="tpu_custom_call" | custom-call | tf_op jit(solution)/shard_map/feed/pallas_call | solution.py:2550
  220.9 1.4 copy-done.4
  222.3 1.0 copy-done.10
  223.4 1.0 copy-done.13
  224.4 1.0 copy-done.14
  225.4 1.0 copy-done.15
  226.3 56.7 %bytes_backward.1 = (f32[32,1024]{1,0:T(8,128)}, bf16[32,1024]{1,0:T(8,128)(2,1)}, f32[32,128]{1,0:T(8,128)}, bf16[16,32,4224]{2,1,0:T(8,128)(2,1)}, f32[2,1024]...) custom-call(f32[256,1024]{1,0:T(8,128)} %copy-done.13, ...), custom_call_target="tpu_custom_call" | custom-call | tf_op jit(solution)/shard_map/bytes_backward/pallas_call | solution.py:2325
  283.1 109.0 %mixer_backward.1 = (bf16[32,1152]{1,0:T(8,128)(2,1)}, f32[56,128]{1,0:T(8,128)}, f32[32,384]{1,0:T(8,128)}, bf16[32,32,128]{2,1,0:T(8,128)(2,1)}, bf16[128,1024...) custom-call(f32[32]{0:T(128)} %step_biases.3, ...), custom_call_target="tpu_custom_call" | custom-call | tf_op jit(solution)/shard_map/mixer_backward/pallas_call | solution.py:1709
  392.1 1.2 copy-done.8
  393.3 0.9 copy-done.30
  394.2 0.9 copy-done.35
  395.1 0.7 copy-done.40
  395.9 38.8 %end_gather.1 = (bf16[4,4,2,32,1152]{4,3,2,1,0:T(8,128)(2,1)S(1)}, f32[4,4,2,56,128]{4,3,2,1,0:T(8,128)S(1)}, f32[32,4224]{1,0:T(8,128)S(1)}, f32[512,256]{1,0:T(8,128)S(1)}) custom-call(bf16[32,1152]{1,0:T(8,128)(2,1)S(1)} %copy-done.35, f32[56,128]{1,0:T(8,128)S(1)} %copy-done.40, bf16[4,32,4224]{2,1,0:T(8,128)(2,1)S(1)} %copy-done.8, ...), custom_call_target="tpu_custom_call" | custom-call | tf_op jit(solution)/shard_map/end_gather/pallas_call | solution.py:919
  434.8 1.6 copy-done.3
  436.3 0.9 copy-done.26
  437.3 0.8 copy-done.38
  438.1 6.0 %finish.1 = (f32[8,128]{1,0:T(8,128)}, f32[32,1024]{1,0:T(8,128)}, f32[32,4384]{1,0:T(8,128)}, f32[64,1024]{1,0:T(8,128)}, f32[128,32]{1,0:T(8,128)S(1)}, /*inde...) custom-call(bf16[1024,1152]{1,0:T(8,128)(2,1)S(1)} %bitcast.41, ...), custom_call_target="tpu_custom_call" | custom-call | tf_op jit(solution)/shard_map/finish/pallas_call | solution.py:1891
  448.3 0.8 copy.75
  449.1 0.8 copy.76
  449.9 0.8 copy.77
  450.7 0.8 copy.78
  (119 shorter events, 5.9 us)
Async XLA Ops:
  0.7 8.2 %copy-start.51 = (bf16[64,1024]{1,0:T(8,128)(2,1)S(1)}, bf16[64,1024]{1,0:T(8,128)(2,1)}, u32[]{:S(2)}) copy-start(bf16[64,1024]{1,0:T(8,128)(2,1)} %param.38) | copy-start | bytes 393220
  0.7 8.2 %copy-start.55 = (bf16[32,1024]{1,0:T(8,128)(2,1)S(1)}, bf16[32,1024]{1,0:T(8,128)(2,1)}, u32[]{:S(2)}) copy-start(bf16[32,1024]{1,0:T(8,128)(2,1)} %param.44) | copy-start | bytes 196612
  0.7 8.1 %copy-start.54 = (bf16[32,1024]{1,0:T(8,128)(2,1)S(1)}, bf16[32,1024]{1,0:T(8,128)(2,1)}, u32[]{:S(2)}) copy-start(bf16[32,1024]{1,0:T(8,128)(2,1)} %param.43) | copy-start | bytes 196612
  0.7 8.1 %copy-start.53 = (bf16[32,1024]{1,0:T(8,128)(2,1)S(1)}, bf16[32,1024]{1,0:T(8,128)(2,1)}, u32[]{:S(2)}) copy-start(bf16[32,1024]{1,0:T(8,128)(2,1)} %param.42) | copy-start | bytes 196612
  0.7 8.1 %copy-start.52 = (bf16[32,1024]{1,0:T(8,128)(2,1)S(1)}, bf16[32,1024]{1,0:T(8,128)(2,1)}, u32[]{:S(2)}) copy-start(bf16[32,1024]{1,0:T(8,128)(2,1)} %param.41) | copy-start | bytes 196612
  2.3 148.8 %copy-start.34 = (f32[2,1024]{1,0:T(2,128)}, f32[2,1024]{1,0:T(2,128)S(1)}, u32[]{:S(2)}) copy-start(f32[2,1024]{1,0:T(2,128)S(1)} %pad_maximum_fusion.gains) | copy-start | bytes 24580
  3.0 67.7 %copy-start.32 = (f32[1,2304]{1,0:T(1,128)}, f32[1,2304]{1,0:T(1,128)S(1)}, u32[]{:S(2)}) copy-start(f32[1,2304]{1,0:T(1,128)S(1)} %broadcast_in_dim.11.conv_bias) | copy-start | bytes 27652
  4.5 4.4 copy-start.56
  4.6 146.5 %copy-start.33 = (f32[2,1024]{1,0:T(2,128)}, f32[2,1024]{1,0:T(2,128)S(1)}, u32[]{:S(2)}) copy-start(f32[2,1024]{1,0:T(2,128)S(1)} %reshape.120.gated_gain) | copy-start | bytes 24580
  7.7 63.0 %copy-start.31 = (f32[4,2304]{1,0:T(4,128)S(1)}, f32[4,2304]{1,0:T(4,128)}, u32[]{:S(2)}) copy-start(f32[4,2304]{1,0:T(4,128)} %conv_weight.3) | copy-start | bytes 110596
  7.7 63.0 %copy-start.41 = (f32[1024]{0:T(1024)S(1)}, f32[1024]{0:T(1024)}, u32[]{:S(2)}) copy-start(f32[1024]{0:T(1024)} %param.30) | copy-start | bytes 12292
  7.8 63.0 %copy-start.42 = (f32[32]{0:T(128)S(1)}, f32[32]{0:T(128)}, u32[]{:S(2)}) copy-start(f32[32]{0:T(128)} %step_biases.3) | copy-start | bytes 388
  7.8 63.0 %copy-start.43 = (f32[32]{0:T(128)S(1)}, f32[32]{0:T(128)}, u32[]{:S(2)}) copy-start(f32[32]{0:T(128)} %log_rates.3) | copy-start | bytes 388
  7.8 63.0 %copy-start.44 = (f32[32]{0:T(128)S(1)}, f32[32]{0:T(128)}, u32[]{:S(2)}) copy-start(f32[32]{0:T(128)} %skip_gains.3) | copy-start | bytes 388
  7.8 63.0 %copy-start.45 = (s32[9]{0:T(128)S(1)}, s32[9]{0:T(128)}, u32[]{:S(2)}) copy-start(s32[9]{0:T(128)} %doc_patches.1) | copy-start | bytes 112
  7.8 63.0 %copy-start.46 = (s32[9]{0:T(128)S(1)}, s32[9]{0:T(128)}, u32[]{:S(2)}) copy-start(s32[9]{0:T(128)} %pad_bytes.1) | copy-start | bytes 112
  70.8 1.0 copy-start.9
  71.8 0.9 copy-start.27
  72.7 0.9 copy-start.28
  73.7 0.9 copy-start.29
  74.6 0.8 copy-start.37
  149.6 0.8 copy-start.20
  151.1 14.1 %copy-start.17 = (f32[32,1024]{1,0:T(8,128)}, f32[32,1024]{1,0:T(8,128)S(1)}, u32[]{:S(2)}) copy-start(f32[32,1024]{1,0:T(8,128)S(1)} %get-tuple-element.100.mixed_in) | copy-start | bytes 393220
  151.1 14.1 %copy-start.19 = (f32[1024,1]{1,0:T(8,128)}, f32[1024,1]{1,0:T(8,128)S(1)}, u32[]{:S(2)}) copy-start(f32[1024,1]{1,0:T(8,128)S(1)} %get-tuple-element.122.dt) | copy-start | bytes 12292
  151.1 14.2 %copy-start.24 = (f32[8,64,128]{2,1,0:T(8,128)}, f32[8,64,128]{2,1,0:T(8,128)S(1)}, u32[]{:S(2)}) copy-start(f32[8,64,128]{2,1,0:T(8,128)S(1)} %get-tuple-element.125.states) | copy-start | bytes 786436
  151.1 20.2 %copy-start.5 = (f32[4,256,1]{2,1,0:T(8,128)}, f32[4,256,1]{2,1,0:T(8,128)S(1)}, u32[]{:S(2)}) copy-start(f32[4,256,1]{2,1,0:T(8,128)S(1)} %get-tuple-element.104.keep) | copy-start | bytes 12292
  151.1 20.2 %copy-start.1 = (bf16[256,1024]{1,0:T(8,128)(2,1)S(1)}, bf16[256,1024]{1,0:T(8,128)(2,1)}, u32[]{:S(2)}) copy-start(bf16[256,1024]{1,0:T(8,128)(2,1)} %cotangent.3) | copy-start | bytes 1572868
  151.1 20.2 %copy-start.6 = (bf16[3,256,1024]{2,1,0:T(8,128)(2,1)S(1)}, bf16[3,256,1024]{2,1,0:T(8,128)(2,1)}, u32[]{:S(2)}) copy-start(bf16[3,256,1024]{2,1,0:T(8,128)(2,1)} %get-tuple-element.103.g_others) | copy-start | bytes 4718596
  165.2 1.1 copy-start.7
  166.4 1.0 copy-start.11
  167.4 1.0 copy-start.12
  220.9 1.4 copy-start.4
  222.3 1.0 copy-start.10
  223.4 1.0 copy-start.13
  224.4 1.0 copy-start.14
  225.4 1.0 copy-start.15
  283.0 151.7 %copy-start = (bf16[4,4,2,32,1536]{4,3,2,1,0:T(8,128)(2,1)S(1)}, bf16[4,4,2,32,1536]{4,3,2,1,0:T(8,128)(2,1)}, u32[]{:S(2)}) copy-start(bf16[4,4,2,32,1536]{4,3,2,1,0:T(8,128)(2,1)} %get-tuple-element.92) | copy-start | bytes 9437188
  283.0 151.7 %copy-start.2 = (bf16[1024,1024]{1,0:T(8,128)(2,1)S(1)}, bf16[1024,1024]{1,0:T(8,128)(2,1)}, u32[]{:S(2)}) copy-start(bf16[1024,1024]{1,0:T(8,128)(2,1)} %get-tuple-element.148.embedded) | copy-start | bytes 6291460
  283.0 151.7 %copy-start.39 = (f32[2048]{0:T(1024)S(1)}, f32[2048]{0:T(1024)}, u32[]{:S(2)}) copy-start(f32[2048]{0:T(1024)} %param.37) | copy-start | bytes 24580
  392.0 1.2 copy-start.8
  393.3 0.9 copy-start.30
  394.2 0.9 copy-start.35
  434.7 1.6 copy-start.3
  436.3 0.9 copy-start.26
  437.3 0.8 copy-start.38
  444.1 4.2 copy-start.48
  444.1 5.0 %copy-start.50 = (f32[256,512]{1,0:T(8,128)S(1)}, f32[256,512]{1,0:T(8,128)}, u32[]{:S(2)}) copy-start(f32[256,512]{1,0:T(8,128)} %get-tuple-element.277) | copy-start | bytes 1572868
  444.8 5.1 %copy-start.49 = (f32[256,512]{1,0:T(8,128)S(1)}, f32[256,512]{1,0:T(8,128)}, u32[]{:S(2)}) copy-start(f32[256,512]{1,0:T(8,128)} %get-tuple-element.278) | copy-start | bytes 1572868
  (9 other events, 6.7 us)
